TPU v7x, 32 devices: a whole 2x2x4 slice. The times are simulated.
32 devices in a mesh: fsdp: 16 (over z, x, core), tp: 2 (over y).
Axes of the slice: x: 2, y: 2, z: 4, core: 2. Of those that a mesh axis runs over, the one named last changes fastest.
Arguments:
- layer_in: bfloat16 [32768, 1536], P(('fsdp', 'tp')), may hold values from -6 to 6
- seg_ids: int32 [32768], P('fsdp'), may hold values from 0 to 127, as said below
- gain_one: float32 [1536], replicated, may hold values from 0.5 to 1.5
- x_weight: bfloat16 [1536, 3072], P('fsdp', 'tp'), may hold values from -0.15625 to 0.15625
- z_weight: bfloat16 [1536, 3072], P('fsdp', 'tp'), may hold values from -0.15625 to 0.15625
- dt_weight: bfloat16 [1536, 48], P('fsdp', 'tp'), may hold values from -0.15625 to 0.15625
- bc_weight: bfloat16 [1536, 32], P('fsdp'), may hold values from -0.078125 to 0.078125
- conv_weight: float32 [4, 3072], P(None, 'tp'), may hold values from -3 to 3
- conv_bias: float32 [3072], P('tp'), may hold values from -0.5 to 0.5
- dt_bias: float32 [48], P('tp'), may hold values from -4 to -1
- a_log: float32 [48], P('tp'), may hold values from -4.5 to 0.5
- d_skip: float32 [48], P('tp'), may hold values from 0.5 to 1.5
- out_weight: bfloat16 [1536, 3072], P('fsdp', 'tp'), may hold values from -0.109375 to 0.109375
- gain_two: float32 [1536], replicated, may hold values from 0.5 to 1.5
- gate_weight: bfloat16 [1536, 4096], P('fsdp', 'tp'), may hold values from -0.15625 to 0.15625
- up_weight: bfloat16 [1536, 4096], P('fsdp', 'tp'), may hold values from -0.15625 to 0.15625
- down_weight: bfloat16 [1536, 4096], P('fsdp', 'tp'), may hold values from -0.09375 to 0.09375
- cotangent: bfloat16 [32768, 1536], P(('fsdp', 'tp')), may hold values from -6 to 6
Outputs:
- layer_out: bfloat16 [32768, 1536], P(('fsdp', 'tp'))
- input_grad: float32 [32768, 1536], P(('fsdp', 'tp'))
- gain_one_grad: float32 [1536], replicated
- x_weight_grad: float32 [1536, 3072], P('fsdp', 'tp')
- z_weight_grad: float32 [1536, 3072], P('fsdp', 'tp')
- dt_weight_grad: float32 [1536, 48], P('fsdp', 'tp')
- bc_weight_grad: float32 [1536, 32], P('fsdp')
- conv_weight_grad: float32 [4, 3072], P(None, 'tp')
- conv_bias_grad: float32 [3072], P('tp')
- dt_bias_grad: float32 [48], P('tp')
- a_log_grad: float32 [48], P('tp')
- d_skip_grad: float32 [48], P('tp')
- out_weight_grad: float32 [1536, 3072], P('fsdp', 'tp')
- gain_two_grad: float32 [1536], replicated
- gate_weight_grad: float32 [1536, 4096], P('fsdp', 'tp')
- up_weight_grad: float32 [1536, 4096], P('fsdp', 'tp')
- down_weight_grad: float32 [1536, 4096], P('fsdp', 'tp')
Inputs may be any that keep to these rules, and one draw needn't show every extreme that they name: `seg_ids`: within each sequence of 2048 tokens the ids never fall; every document has between 409 and 1365 tokens unless a sequence's end cuts it; ids of different sequences differ.
All inputs are finite; a program needn't handle non-finite values.
Results may differ from a plain program's by a relative error of at most 0.0099.
Values may be sent and summed in bfloat16 or wider, within the bound.
A program may use at most 384 MiB of HBM per device.

v0:
```python
import jax
import jax.numpy as jnp
from jax import lax
from jax.sharding import PartitionSpec as P

HEADDIM = 64
BLOCK_LEN = 256


highest = lax.Precision.HIGHEST
epsilon = 1e-05


def for_sending(x):
    return jax.tree.map(lambda a: a.astype(jnp.bfloat16) if a.dtype == jnp.float32 else a, x)


def conv_restart(x_in, seg_rows, conv_weight, conv_bias):
    summed = conv_bias[None, :] + conv_weight[0][None, :] * x_in
    for offset in range(1, conv_weight.shape[0]):
        shifted = jnp.pad(x_in, ((offset, 0), (0, 0)))[:-offset]
        earlier = jnp.pad(seg_rows, (offset, 0), constant_values=-1)[:-offset]
        same_seg = (earlier == seg_rows).astype(x_in.dtype)
        summed = summed + conv_weight[offset][None, :] * shifted * same_seg[:, None]
    return summed


def block_step(carry_in, pieces, a_rate):
    carried, prev_seg = carry_in
    values, steps_dt, b_rows, c_rows, seg_block = pieces
    length = seg_block.shape[0]
    running = jnp.cumsum(steps_dt * a_rate[None, :], axis=0)
    places = jnp.arange(length)
    same_doc = (seg_block[:, None] == seg_block[None, :]) & (places[:, None] >= places[None, :])
    log_gaps = running.T[:, :, None] - running.T[:, None, :]
    decays = jnp.where(same_doc[None], jnp.exp(jnp.where(same_doc[None], log_gaps, 0.0)), 0.0)
    scores = jnp.dot(c_rows, b_rows.T, precision=highest)
    scaled = steps_dt[:, :, None] * values
    within = jnp.einsum("hts,shp->thp", decays * scores[None], scaled, precision=highest)
    carry_on = (seg_block == prev_seg).astype(values.dtype)
    from_state = jnp.einsum("tn,hpn->thp", c_rows, carried, precision=highest)
    within = within + from_state * (jnp.exp(running) * carry_on[:, None])[:, :, None]
    last_seg = seg_block[length - 1]
    tail_weight = (seg_block == last_seg).astype(values.dtype)[:, None] * jnp.exp(
        running[length - 1][None, :] - running
    )
    fresh = jnp.einsum("sh,shp,sn->hpn", tail_weight, scaled, b_rows, precision=highest)
    keep_state = jnp.where(last_seg == prev_seg, 1.0, 0.0) * jnp.exp(running[length - 1])
    return ((keep_state[:, None, None] * carried + fresh, last_seg), within)


def mixer(x_in, z_in, bc_rows, dt_raw, conv_weight, conv_bias, dt_bias, a_log, d_skip, seg_rows):
    values = jax.nn.silu(conv_restart(x_in, seg_rows, conv_weight, conv_bias))
    steps_dt = jax.nn.softplus(dt_raw + dt_bias[None, :])
    a_rate = -jnp.exp(a_log)
    tokens, channels = values.shape
    heads = channels // HEADDIM
    state_n = bc_rows.shape[1] // 2
    blocks = tokens // BLOCK_LEN
    per_block = (
        values.reshape(blocks, BLOCK_LEN, heads, HEADDIM),
        steps_dt.reshape(blocks, BLOCK_LEN, heads),
        bc_rows[:, :state_n].reshape(blocks, BLOCK_LEN, state_n),
        bc_rows[:, state_n:].reshape(blocks, BLOCK_LEN, state_n),
        seg_rows.reshape(blocks, BLOCK_LEN),
    )

    def advance(carry_in, pieces):
        return block_step(carry_in, pieces, a_rate)

    start = (jnp.zeros((heads, HEADDIM, state_n), values.dtype), jnp.array(-1, jnp.int32))
    final_state, scanned = lax.scan(jax.checkpoint(advance), start, per_block)
    scanned = scanned.reshape(tokens, channels)
    skipped = jnp.repeat(d_skip, HEADDIM)[None, :] * values
    return (scanned + skipped) * jax.nn.silu(z_in)


def bf_dot(left_arg, right_arg):
    return jnp.dot(left_arg, right_arg, preferred_element_type=jnp.float32)


def dot_rows(left_arg, right_arg):
    return lax.dot_general(
        left_arg, right_arg, (((1,), (1,)), ((), ())), preferred_element_type=jnp.float32
    )


def dot_cols(left_arg, right_arg):
    return lax.dot_general(
        left_arg, right_arg, (((0,), (0,)), ((), ())), preferred_element_type=jnp.float32
    )


def whole_rows(rows):
    return lax.all_gather(rows, "tp", axis=0, tiled=True)


def share_rows(terms):
    return lax.psum_scatter(terms, "tp", scatter_dimension=0, tiled=True)


def collect(weights):
    return jax.tree.map(
        lambda part, own: part.astype(own.dtype),
        lax.all_gather(for_sending(weights), "fsdp", axis=0, tiled=True),
        weights,
    )


def norm_forward(rows, gain_row):
    scale_row = lax.rsqrt(jnp.mean(rows * rows, axis=-1, keepdims=True) + epsilon)
    unit_rows = rows * scale_row
    return (unit_rows, scale_row, (unit_rows * gain_row).astype(jnp.bfloat16))


def norm_backward(grad_rows, unit_rows, scale_row, gain_row):
    gain_part = jnp.sum(grad_rows * unit_rows, axis=0)
    unit_grad = grad_rows * gain_row
    back_rows = scale_row * (
        unit_grad - unit_rows * jnp.mean(unit_grad * unit_rows, axis=-1, keepdims=True)
    )
    return (back_rows, gain_part)


def local(
    layer_in,
    seg_ids,
    gain_one,
    x_weight,
    z_weight,
    dt_weight,
    bc_weight,
    conv_weight,
    conv_bias,
    dt_bias,
    a_log,
    d_skip,
    out_weight,
    gain_two,
    gate_weight,
    up_weight,
    down_weight,
    cotangent,
):
    rows_in = layer_in.astype(jnp.float32)
    unit_one, scale_one, normed = norm_forward(rows_in, gain_one)
    normed_all = whole_rows(normed)
    mamba_full = collect((x_weight, z_weight, dt_weight, bc_weight, out_weight))
    full_x, full_z, full_dt, full_bc, full_out = mamba_full
    x_in = bf_dot(normed_all, full_x)
    z_in = bf_dot(normed_all, full_z)
    dt_raw = bf_dot(normed_all, full_dt)
    bc_rows = bf_dot(normed_all, full_bc)

    def core(x_arg, z_arg, bc_arg, dt_arg, conv_w_arg, conv_b_arg, dt_b_arg, a_arg, skip_arg):
        return mixer(
            x_arg, z_arg, bc_arg, dt_arg, conv_w_arg, conv_b_arg, dt_b_arg, a_arg, skip_arg, seg_ids
        )

    gated, core_back = jax.vjp(
        core, x_in, z_in, bc_rows, dt_raw, conv_weight, conv_bias, dt_bias, a_log, d_skip
    )
    gated_low = gated.astype(jnp.bfloat16)
    mixed = share_rows(dot_rows(gated_low, full_out))
    hidden = rows_in + mixed
    unit_two, scale_two, normed_two = norm_forward(hidden, gain_two)
    normed_two_all = whole_rows(normed_two)
    mlp_full = collect((gate_weight, up_weight, down_weight))
    full_gate, full_up, full_down = mlp_full
    gate = bf_dot(normed_two_all, full_gate)
    up_rows = bf_dot(normed_two_all, full_up)
    sigmoid_gate = jax.nn.sigmoid(gate)
    silu_gate = gate * sigmoid_gate
    act = (silu_gate * up_rows).astype(jnp.bfloat16)
    fed = share_rows(dot_rows(act, full_down))
    layer_out = (hidden + fed).astype(jnp.bfloat16)
    back_gate, back_up, back_down = collect((gate_weight, up_weight, down_weight))
    cot_all = whole_rows(cotangent)
    act_grad = bf_dot(cot_all, back_down)
    down_grad = dot_cols(cot_all, act)
    gate_grad = (act_grad * up_rows * sigmoid_gate * (1.0 + gate * (1.0 - sigmoid_gate))).astype(
        jnp.bfloat16
    )
    up_grad = (act_grad * silu_gate).astype(jnp.bfloat16)
    gate_w_grad = dot_cols(normed_two_all, gate_grad)
    up_w_grad = dot_cols(normed_two_all, up_grad)
    normed_two_grad = share_rows(dot_rows(gate_grad, back_gate) + dot_rows(up_grad, back_up))
    norm_two_back, gain_two_part = norm_backward(normed_two_grad, unit_two, scale_two, gain_two)
    hidden_grad = cotangent.astype(jnp.float32) + norm_two_back
    back_x, back_z, back_dt, back_bc, back_out = collect(
        (x_weight, z_weight, dt_weight, bc_weight, out_weight)
    )
    mixed_grad = whole_rows(hidden_grad.astype(jnp.bfloat16))
    gated_grad = bf_dot(mixed_grad, back_out)
    out_w_grad = dot_cols(mixed_grad, gated_low)
    (
        x_in_grad,
        z_in_grad,
        bc_part,
        dt_raw_grad,
        conv_w_grad,
        conv_b_grad,
        dt_b_grad,
        a_log_part,
        skip_grad,
    ) = core_back(gated_grad)
    bc_grad = lax.psum(bc_part, "tp")
    x_in_low = x_in_grad.astype(jnp.bfloat16)
    z_in_low = z_in_grad.astype(jnp.bfloat16)
    dt_raw_low = dt_raw_grad.astype(jnp.bfloat16)
    bc_low = bc_grad.astype(jnp.bfloat16)
    x_w_grad = dot_cols(normed_all, x_in_low)
    z_w_grad = dot_cols(normed_all, z_in_low)
    dt_w_grad = dot_cols(normed_all, dt_raw_low)
    bc_w_grad = dot_cols(normed_all, bc_low)
    normed_terms = (
        dot_rows(x_in_low, back_x)
        + dot_rows(z_in_low, back_z)
        + dot_rows(dt_raw_low, back_dt)
        + 0.5 * dot_rows(bc_low, back_bc)
    )
    normed_grad = share_rows(normed_terms)
    norm_one_back, gain_one_part = norm_backward(normed_grad, unit_one, scale_one, gain_one)
    input_grad = hidden_grad + norm_one_back
    (
        x_w_share,
        z_w_share,
        dt_w_share,
        bc_w_share,
        out_w_share,
        gate_w_share,
        up_w_share,
        down_w_share,
    ) = (
        lax.psum_scatter(x_w_grad, "fsdp", scatter_dimension=0, tiled=True),
        lax.psum_scatter(z_w_grad, "fsdp", scatter_dimension=0, tiled=True),
        lax.psum_scatter(dt_w_grad, "fsdp", scatter_dimension=0, tiled=True),
        lax.psum_scatter(bc_w_grad, "fsdp", scatter_dimension=0, tiled=True),
        lax.psum_scatter(out_w_grad, "fsdp", scatter_dimension=0, tiled=True),
        lax.psum_scatter(gate_w_grad, "fsdp", scatter_dimension=0, tiled=True),
        lax.psum_scatter(up_w_grad, "fsdp", scatter_dimension=0, tiled=True),
        lax.psum_scatter(down_grad, "fsdp", scatter_dimension=0, tiled=True),
    )
    conv_w_total, conv_b_total, dt_b_total, a_log_total, skip_total = lax.psum(
        (conv_w_grad, conv_b_grad, dt_b_grad, a_log_part, skip_grad), "fsdp"
    )
    gain_one_total, gain_two_total = lax.psum((gain_one_part, gain_two_part), ("fsdp", "tp"))
    return (
        layer_out,
        input_grad,
        gain_one_total,
        x_w_share,
        z_w_share,
        dt_w_share,
        bc_w_share,
        conv_w_total,
        conv_b_total,
        dt_b_total,
        a_log_total,
        skip_total,
        out_w_share,
        gain_two_total,
        gate_w_share,
        up_w_share,
        down_w_share,
    )


def solution(mesh):
    in_specs = (
        P(("fsdp", "tp"), None),
        P("fsdp"),
        P(),
        P("fsdp", "tp"),
        P("fsdp", "tp"),
        P("fsdp", "tp"),
        P("fsdp", None),
        P(None, "tp"),
        P("tp"),
        P("tp"),
        P("tp"),
        P("tp"),
        P("fsdp", "tp"),
        P(),
        P("fsdp", "tp"),
        P("fsdp", "tp"),
        P("fsdp", "tp"),
        P(("fsdp", "tp"), None),
    )
    out_specs = (
        P(("fsdp", "tp"), None),
        P(("fsdp", "tp"), None),
        P(),
        P("fsdp", "tp"),
        P("fsdp", "tp"),
        P("fsdp", "tp"),
        P("fsdp", None),
        P(None, "tp"),
        P("tp"),
        P("tp"),
        P("tp"),
        P("tp"),
        P("fsdp", "tp"),
        P(),
        P("fsdp", "tp"),
        P("fsdp", "tp"),
        P("fsdp", "tp"),
    )
    return jax.shard_map(local, mesh=mesh, in_specs=in_specs, out_specs=out_specs, check_vma=False)
```

profile of v0, /device:TPU:0, one launch (start us, length us, event | category | flops | bytes accessed | tf_op | source)
XLA Modules:
  0.0 3267.6 jit_solution(7452648825811919902)
XLA Ops:
  17.8 23.4 all-gather.1
  60.1 38.0 %all-gather.13.cloned.1.call-done = bf16[2048,1536]{1,0:T(8,128)(2,1)} async-done(((bf16[1024,1536]{1,0:T(8,128)(2,1)}), bf16[2048,1536]{1,0:T(8,128)(2,1)}) %all-gather.13.cloned.1.call-update) | async-done | bytes 6291472 | tf_op jit(solution)/shard_map/all_gather | solution.py:95
  106.9 46.8 %all-gather.15.cloned.1.call-done = bf16[1536,1536]{1,0:T(8,128)(2,1)} async-done(((bf16[96,1536]{1,0:T(8,128)(2,1)}), bf16[1536,1536]{1,0:T(8,128)(2,1)}) %all-gather.15.cloned.1.call-update) | async-done | bytes 4718608 | tf_op jit(solution)/shard_map/all_gather | solution.py:105
  225.4 195.4 %while.46 = (s32[]{:T(128)}, f32[24,64,16]{1,2,0:T(8,128)S(1)}, s32[]{:T(128)}, f32[8,256,24,64]{1,3,2,0:T(8,128)}, f32[8,24,64,16]{2,3,1,0:T(8,128)}, /*index=5...) while((s32[]{:T(128)}, f32[24,64,16]{1,2,0:T(8,128)S(1)}, ...), condition=%wide.region_4.5_spmd.clone, body=%wide.region_1.4_spmd.clone.sunk | while | flops 1380637824 | bytes 9689099 | solution.py:72
  438.6 21.2 reshape.481
  459.8 27.4 multiply_convert_fusion.3
  503.9 142.4 %reduce-scatter.19.cloned.1.call-done = f32[1024,1536]{1,0:T(8,128)} async-done(((f32[2048,1536]{1,0:T(8,128)}), f32[1024,1536]{1,0:T(8,128)}) %reduce-scatter.19.cloned.1.call-update) | async-done | bytes 6291472 | tf_op jit(solution)/shard_map/reduce_scatter | solution.py:99
  657.0 53.3 %all-gather.23.cloned.1.call-done = bf16[1536,2048]{1,0:T(8,128)(2,1)} async-done(((bf16[96,2048]{1,0:T(8,128)(2,1)}), bf16[1536,2048]{1,0:T(8,128)(2,1)}) %all-gather.23.cloned.1.call-update) | async-done | bytes 6291472 | tf_op jit(solution)/shard_map/all_gather | solution.py:105
  710.3 81.1 %all-gather.21.cloned.1.call-done = bf16[2048,1536]{1,0:T(8,128)(2,1)} async-done(((bf16[1024,1536]{1,0:T(8,128)(2,1)}), bf16[2048,1536]{1,0:T(8,128)(2,1)}) %all-gather.21.cloned.1.call-update) | async-done | bytes 6291472 | tf_op jit(solution)/shard_map/all_gather | solution.py:95
  791.4 19.7 fusion.143
  811.0 44.5 %all-gather.25.cloned.1.call-done = bf16[1536,2048]{1,0:T(8,128)(2,1)} async-done(((bf16[96,2048]{1,0:T(8,128)(2,1)}), bf16[1536,2048]{1,0:T(8,128)(2,1)}) %all-gather.25.cloned.1.call-update) | async-done | bytes 6291472 | tf_op jit(solution)/shard_map/all_gather | solution.py:105
  855.5 19.4 fusion.144
  875.0 61.1 %all-gather.29.cloned.1.call-done = bf16[2048,1536]{1,0:T(8,128)(2,1)} async-done(((bf16[1024,1536]{1,0:T(8,128)(2,1)}), bf16[2048,1536]{1,0:T(8,128)(2,1)}) %all-gather.29.cloned.1.call-update) | async-done | bytes 6291472 | tf_op jit(solution)/shard_map/all_gather | solution.py:95
  936.1 64.0 %all-gather.27.cloned.1.call-done = bf16[1536,2048]{1,0:T(8,128)(2,1)} async-done(((bf16[96,2048]{1,0:T(8,128)(2,1)}), bf16[1536,2048]{1,0:T(8,128)(2,1)}) %all-gather.27.cloned.1.call-update) | async-done | bytes 6291472 | tf_op jit(solution)/shard_map/all_gather | solution.py:105
  1000.1 31.1 multiply_convert_fusion
  1031.2 19.7 fusion.146
  1050.9 21.8 convolution_add_fusion.3
  1072.8 143.2 %reduce-scatter.23.cloned.1.call-done = f32[1024,1536]{1,0:T(8,128)} async-done(((f32[2048,1536]{1,0:T(8,128)}), f32[1024,1536]{1,0:T(8,128)}) %reduce-scatter.23.cloned.1.call-update) | async-done | bytes 6291472 | tf_op jit(solution)/shard_map/reduce_scatter | solution.py:99
  1227.9 80.5 %all-gather.31.cloned.1.call-done = bf16[2048,1536]{1,0:T(8,128)(2,1)} async-done(((bf16[1024,1536]{1,0:T(8,128)(2,1)}), bf16[2048,1536]{1,0:T(8,128)(2,1)}) %all-gather.31.cloned.1.call-update) | async-done | bytes 6291472 | tf_op jit(solution)/shard_map/all_gather | solution.py:95
  1308.4 32.2 multiply_reduce_fusion.3
  1386.4 585.2 %while.47 = (s32[]{:T(128)}, f32[24]{0:T(128)}, f32[24,64,16]{1,2,0:T(8,128)}, f32[8,256,24,64]{1,3,2,0:T(8,128)}, f32[8,256,24]{1,0,2:T(8,128)}, /*index=5*/f32...) while((s32[]{:T(128)}, f32[24]{0:T(128)}, ...), condition=%wide.region_23.24_spmd.clone, body=%wide.region_10.23_spmd.clone.sunk | while | flops 2861126656 | bytes 33109948 | solution.py:72
  1989.5 21.2 reshape.483
  2010.8 37.8 %multiply_reduce_fusion.7 = (f32[1536]{0:T(1024)}, f32[1536]{0:T(1024)}, f32[1536]{0:T(1024)}, f32[1536]{0:T(1024)}, f32[1536]{0:T(1024)}, /*index=5*/f32[2048,1536]{1,0:T(8,128)}) fusion(f32[2048,1536]{1,0:T(8,128)} %copy-done.5, f32[2048]{0:T(1024)S(1)} %copy-done.33, f32[2048]{0:T(1024)S(1)} %copy-done.31, f32[2048]{0:T(1024)S(1)} %copy-done.29, ...), kind=kLoop, calls=%fused_computation.172 | loop fusion | flops 72344064 | bytes 62976000 | tf_op jit(solution)/shard_map/transpose(jvp())/reduce_sum | solution.py:24
  2299.5 60.8 %all-reduce.18 = (f32[4,1536]{1,0:T(4,128)}, f32[1536]{0:T(1024)}, f32[24]{0:T(128)}, f32[24]{0:T(128)}, f32[24]{0:T(128)}) all-reduce(f32[4,1536]{1,0:T(4,128)S(1)} %pad_add_fusion.1, f32[1536]{0:T(1024)S(1)} %copy-done.63, f32[24]{0:T(128)S(1)} %copy-done.75, ...), channel_id=1, replica_groups=mesh['fsdp'=16,'tp'=2] {'fsdp'}, use_global_device_ids=true, to_apply=%region_37.38 | all-reduce | flops 7752 | bytes 62016 | tf_op jit(solution)/shard_map/psum | solution.py:244
  2367.2 37.5 %all-reduce.17 = (f32[1536]{0:T(1024)}, f32[1536]{0:T(1024)}) all-reduce(f32[1536]{0:T(1024)S(1)} %get-tuple-element.880, f32[1536]{0:T(1024)S(1)} %copy-done.65), channel_id=1, replica_groups=mesh['fsdp'=16,'tp'=2] {'fsdp','tp'}, use_global_device_ids=true, to_apply=%region_28.29 | all-reduce | flops 3072 | bytes 24576 | tf_op jit(solution)/shard_map/psum | solution.py:247
  2404.7 92.4 %reduce-scatter.21.cloned.1.call-done = f32[1024,1536]{1,0:T(8,128)} async-done(((f32[2048,1536]{1,0:T(8,128)}), f32[1024,1536]{1,0:T(8,128)}) %reduce-scatter.21.cloned.1.call-update) | async-done | bytes 6291472 | tf_op jit(solution)/shard_map/reduce_scatter | solution.py:99
  2512.5 123.7 %reduce-scatter.33.cloned.1.call-done = f32[96,2048]{1,0:T(8,128)} async-done(((f32[1536,2048]{1,0:T(8,128)}), f32[96,2048]{1,0:T(8,128)}) %reduce-scatter.33.cloned.1.call-update) | async-done | bytes 786448 | tf_op jit(solution)/shard_map/reduce_scatter | solution.py:240
  2636.2 138.3 %reduce-scatter.35.cloned.1.call-done = f32[96,2048]{1,0:T(8,128)} async-done(((f32[1536,2048]{1,0:T(8,128)}), f32[96,2048]{1,0:T(8,128)}) %reduce-scatter.35.cloned.1.call-update) | async-done | bytes 786448 | tf_op jit(solution)/shard_map/reduce_scatter | solution.py:241
  2774.5 138.5 %reduce-scatter.41.cloned.1.call-done = f32[96,2048]{1,0:T(8,128)} async-done(((f32[1536,2048]{1,0:T(8,128)}), f32[96,2048]{1,0:T(8,128)}) %reduce-scatter.41.cloned.1.call-update) | async-done | bytes 786448
  2913.0 115.1 %reduce-scatter.27.cloned.1.call-done = f32[96,1536]{1,0:T(8,128)} async-done(((f32[1536,1536]{1,0:T(8,128)}), f32[96,1536]{1,0:T(8,128)}) %reduce-scatter.27.cloned.1.call-update) | async-done | bytes 589840 | tf_op jit(solution)/shard_map/reduce_scatter | solution.py:235
  3028.1 116.3 %reduce-scatter.31.cloned.1.call-done = f32[96,1536]{1,0:T(8,128)} async-done(((f32[1536,1536]{1,0:T(8,128)}), f32[96,1536]{1,0:T(8,128)}) %reduce-scatter.31.cloned.1.call-update) | async-done | bytes 589840 | tf_op jit(solution)/shard_map/reduce_scatter | solution.py:239
  3144.4 115.8 %reduce-scatter.29.cloned.1.call-done = f32[96,1536]{1,0:T(8,128)} async-done(((f32[1536,1536]{1,0:T(8,128)}), f32[96,1536]{1,0:T(8,128)}) %reduce-scatter.29.cloned.1.call-update) | async-done | bytes 589840 | tf_op jit(solution)/shard_map/reduce_scatter | solution.py:236
  (1094 shorter events, 1260.0 us)
Async XLA Ops:
  7.2 90.9 %all-gather.13.cloned.1.call-start = ((), (), s32[]{:S(2)}) async-start(), calls=%async_computation.12 | async-start | bytes 9437184 | tf_op jit(solution)/shard_map/all_gather | solution.py:95
  14.8 138.8 %all-gather.15.cloned.1.call-start = ((), (), s32[]{:S(2)}) async-start(), calls=%async_computation.13 | async-start | bytes 5013504 | tf_op jit(solution)/shard_map/all_gather | solution.py:105
  15.6 444.2 %all-gather.17.cloned.1.call-start = ((), (), s32[]{:S(2)}) async-start(), calls=%async_computation.14 | async-start | bytes 5013504 | tf_op jit(solution)/shard_map/all_gather | solution.py:105
  16.3 470.9 %all-gather.19.cloned.1.call-start = ((), (), s32[]{:S(2)}) async-start(), calls=%async_computation.15 | async-start | bytes 5013504 | tf_op jit(solution)/shard_map/all_gather | solution.py:105
  16.9 629.3 %reduce-scatter.19.cloned.1.call-start = ((), (), s32[]{:S(2)}) async-start(), calls=%async_computation.16 | async-start | bytes 18874368 | tf_op jit(solution)/shard_map/reduce_scatter | solution.py:99
  17.0 150.0 %copy-start.28 = (f32[2048]{0:T(1024)}, f32[2048]{0:T(1024)S(1)}, u32[]{:S(2)}) copy-start(f32[2048]{0:T(1024)S(1)} %get-tuple-element.997) | copy-start | bytes 24580
  17.0 150.0 %copy-start.30 = (f32[2048]{0:T(1024)}, f32[2048]{0:T(1024)S(1)}, u32[]{:S(2)}) copy-start(f32[2048]{0:T(1024)S(1)} %get-tuple-element.998) | copy-start | bytes 24580
  17.0 150.0 %copy-start.32 = (f32[2048]{0:T(1024)}, f32[2048]{0:T(1024)S(1)}, u32[]{:S(2)}) copy-start(f32[2048]{0:T(1024)S(1)} %get-tuple-element.999) | copy-start | bytes 24580
  17.7 149.3 %copy-start.42 = (f32[1536]{0:T(1024)}, f32[1536]{0:T(1024)S(1)}, u32[]{:S(2)}) copy-start(f32[1536]{0:T(1024)S(1)} %get-tuple-element.883) | copy-start | bytes 18436
  17.7 149.3 %copy-start.44 = (f32[1536]{0:T(1024)}, f32[1536]{0:T(1024)S(1)}, u32[]{:S(2)}) copy-start(f32[1536]{0:T(1024)S(1)} %get-tuple-element.884) | copy-start | bytes 18436
  60.1 399.8 %copy-start.60 = (f32[1536]{0:T(1024)}, f32[1536]{0:T(1024)S(1)}, u32[]{:S(2)}) copy-start(f32[1536]{0:T(1024)S(1)} %mul.786) | copy-start | bytes 18436
  503.2 207.0 %all-gather.23.cloned.1.call-start = ((), (), s32[]{:S(2)}) async-start(), calls=%async_computation.18 | async-start | bytes 6684672 | tf_op jit(solution)/shard_map/all_gather | solution.py:105
  503.8 287.6 %all-gather.21.cloned.1.call-start = ((), (), s32[]{:S(2)}) async-start(), calls=%async_computation.17 | async-start | bytes 9437184 | tf_op jit(solution)/shard_map/all_gather | solution.py:95
  654.9 200.7 %all-gather.25.cloned.1.call-start = ((), (), s32[]{:S(2)}) async-start(), calls=%async_computation.19 | async-start | bytes 6684672 | tf_op jit(solution)/shard_map/all_gather | solution.py:105
  655.6 280.5 %all-gather.29.cloned.1.call-start = ((), (), s32[]{:S(2)}) async-start(), calls=%async_computation.22 | async-start | bytes 9437184 | tf_op jit(solution)/shard_map/all_gather | solution.py:95
  656.3 343.8 %all-gather.27.cloned.1.call-start = ((), (), s32[]{:S(2)}) async-start(), calls=%async_computation.20 | async-start | bytes 6684672 | tf_op jit(solution)/shard_map/all_gather | solution.py:105
  656.9 559.0 %reduce-scatter.23.cloned.1.call-start = ((), (), s32[]{:S(2)}) async-start(), calls=%async_computation.23 | async-start | bytes 18874368 | tf_op jit(solution)/shard_map/reduce_scatter | solution.py:99
  1072.7 150.0 %copy-start.6 = (bf16[1024,1536]{1,0:T(8,128)(2,1)S(1)}, bf16[1024,1536]{1,0:T(8,128)(2,1)}, u32[]{:S(2)}) copy-start(bf16[1024,1536]{1,0:T(8,128)(2,1)} %param.39) | copy-start | bytes 9437188
  1072.8 235.7 %all-gather.31.cloned.1.call-start = ((), (), s32[]{:S(2)}) async-start(), calls=%async_computation.24 | async-start | bytes 9437184 | tf_op jit(solution)/shard_map/all_gather | solution.py:95
  1227.9 1132.4 %reduce-scatter.37.cloned.1.call-start = ((), (), s32[]{:S(2)}) async-start(), calls=%async_computation.31 | async-start | bytes 835584
  2086.2 275.6 %reduce-scatter.39.cloned.1.call-start = ((), (), s32[]{:S(2)}) async-start(), calls=%async_computation.32 | async-start | bytes 835584
  2092.5 270.7 %reduce-scatter.25.cloned.1.call-start = ((), (), s32[]{:S(2)}) async-start(), calls=%async_computation.25 | async-start | bytes 18874368 | tf_op jit(solution)/shard_map/reduce_scatter | solution.py:99
  2160.8 336.3 %reduce-scatter.21.cloned.1.call-start = ((), (), s32[]{:S(2)}) async-start(), calls=%async_computation.21 | async-start | bytes 18874368 | tf_op jit(solution)/shard_map/reduce_scatter | solution.py:99
  2180.5 455.7 %reduce-scatter.33.cloned.1.call-start = ((), (), s32[]{:S(2)}) async-start(), calls=%async_computation.29 | async-start | bytes 13369344 | tf_op jit(solution)/shard_map/reduce_scatter | solution.py:240
  2199.7 574.7 %reduce-scatter.35.cloned.1.call-start = ((), (), s32[]{:S(2)}) async-start(), calls=%async_computation.30 | async-start | bytes 13369344 | tf_op jit(solution)/shard_map/reduce_scatter | solution.py:241
  2218.9 694.1 %reduce-scatter.41.cloned.1.call-start = ((), (), s32[]{:S(2)}) async-start(), calls=%async_computation.33 | async-start | bytes 13369344
  2251.2 776.8 %reduce-scatter.27.cloned.1.call-start = ((), (), s32[]{:S(2)}) async-start(), calls=%async_computation.26 | async-start | bytes 10027008 | tf_op jit(solution)/shard_map/reduce_scatter | solution.py:235
  2267.1 877.3 %reduce-scatter.31.cloned.1.call-start = ((), (), s32[]{:S(2)}) async-start(), calls=%async_computation.28 | async-start | bytes 10027008 | tf_op jit(solution)/shard_map/reduce_scatter | solution.py:239
  2282.8 977.5 %reduce-scatter.29.cloned.1.call-start = ((), (), s32[]{:S(2)}) async-start(), calls=%async_computation.27 | async-start | bytes 10027008 | tf_op jit(solution)/shard_map/reduce_scatter | solution.py:236
  2298.6 198.5 %copy-start.36 = (f32[1536]{0:T(1024)S(1)}, f32[1536]{0:T(1024)}, u32[]{:S(2)}) copy-start(f32[1536]{0:T(1024)} %param.35) | copy-start | bytes 18436
  2298.6 198.4 %copy-start.41 = (f32[1024]{0:T(1024)S(1)}, f32[1024]{0:T(1024)}, u32[]{:S(2)}) copy-start(f32[1024]{0:T(1024)} %copy-done.39) | copy-start | bytes 12292
  2298.6 198.4 %copy-start.55 = (f32[1024]{0:T(1024)S(1)}, f32[1024]{0:T(1024)}, u32[]{:S(2)}) copy-start(f32[1024]{0:T(1024)} %copy-done.54) | copy-start | bytes 12292
  (192 other events, 3277.9 us)
Sparse Core Ops, SparseCore 0:
  15.0 83.0 all-gather.12
  100.4 53.2 all-gather.14
  155.9 51.7 all-gather.16
  209.9 51.7 all-gather.18
  503.4 142.8 reduce-scatter.18
  648.4 61.8 all-gather.22
  712.4 78.9 all-gather.20
  793.7 61.8 all-gather.24
  857.1 78.9 all-gather.28
  938.2 61.8 all-gather.26
  1072.9 143.0 reduce-scatter.22
  1228.0 80.3 all-gather.30
  2086.3 57.4 reduce-scatter.36
  2147.7 55.6 reduce-scatter.38
  2205.5 143.4 reduce-scatter.24
  2351.1 145.8 reduce-scatter.20
  2501.5 134.6 reduce-scatter.32
  2640.7 133.7 reduce-scatter.34
  2779.1 133.8 reduce-scatter.40
  2917.5 110.4 reduce-scatter.26
  3033.3 111.0 reduce-scatter.30
  3149.1 111.1 reduce-scatter.28
where the time goes:
time: 3290 us; the launch traced here: 3270 us
  waiting for transfers between devices  1600 us (49%)
  matrix products  769 us (23%)
  local copies, waits for them, and re-layouts  386 us (12%)
  other arithmetic  322 us (10%)
  blocking collectives  150 us (5%)
    reduce_scatter x4, waiting for transfers between devices, share_rows(): return lax.psum_scatter(terms, 'tp', scatter_dimension=0, tiled=True)  378 us
    all_gather x4, waiting for transfers between devices, whole_rows(): return lax.all_gather(rows, 'tp', axis=0, tiled=True)  261 us
    dot_general x24, matrix products, block_step(): jnp.einsum('hts,shp->thp', decays * scores[None], scaled, precision=highest)  212 us
    all_gather x6, waiting for transfers between devices, collect(): lax.all_gather(for_sending(weights), 'fsdp', axis=0, tiled=True)  209 us
    dot_general x8, matrix products, bf_dot(): return jnp.dot(left_arg, right_arg, preferred_element_type=jnp.float32)  150 us
    unnamed x25, waiting for transfers between devices  143 us
    reduce_scatter x1, waiting for transfers between devices, local(): lax.psum_scatter(up_w_grad, 'fsdp', scatter_dimension=0, tiled=True)  138 us
    dot_general x8, matrix products, dot_rows(): lax.dot_general(left_arg, right_arg, (((1,), (1,)), ((), ())), preferred_...  133 us
  transfers between devices with their start and end apart: 22, of which 17 were waited for; matrix products, arithmetic and copies ran while one was open for 19% of the time, Pallas kernels for 0%

commit v1 on v0

v1 whole, which is shorter than its diff:
```python
import jax
import jax.numpy as jnp
from jax import lax
from jax.experimental import pallas as pl
from jax.experimental.pallas import tpu as pltpu
from jax.sharding import PartitionSpec as P

HEADDIM = 64
HEADS = 24
STATES = 16
Q = 128
HALO = 16
EXTRA = 128
RUN, DT, DEC, TAIL, SEG, CONT, LAST, LOGDT = 0, 24, 48, 72, 96, 100, 101, 104
COLB, COLC = HEADS, HEADS + STATES

f32 = jnp.float32
bf16 = jnp.bfloat16
highest = lax.Precision.HIGHEST
epsilon = 1e-05
NEG = -1e30


def dot(a, b, precision=None):
    return jnp.dot(a, b, preferred_element_type=f32, precision=precision)


def dot_t(a, b):
    return lax.dot_general(a, b, (((1,), (1,)), ((), ())), preferred_element_type=f32)


def split(v):
    high = v.astype(bf16)
    return high, (v - high.astype(f32)).astype(bf16)


def wide_left(v):
    high, low = split(v)
    return jnp.concatenate([high, low, high], axis=1)


def stack_right(v):
    high, low = split(v)
    return jnp.concatenate([high, high, low], axis=0)


def sigmoid(v):
    return 0.5 * jnp.tanh(0.5 * v) + 0.5


def lanes_of(rows=Q):
    return lax.broadcasted_iota(jnp.int32, (rows, 128), 1)


def pair_cols(col, first, j, left):
    a = col[:, first + 2 * j : first + 2 * j + 1]
    b = col[:, first + 2 * j + 1 : first + 2 * j + 2]
    return jnp.where(left, a, b)


def triangle(strict=False, transposed=False):
    i = lax.broadcasted_iota(jnp.int32, (Q, Q), 1 if transposed else 0)
    k = lax.broadcasted_iota(jnp.int32, (Q, Q), 0 if transposed else 1)
    return (i > k) if strict else (i >= k)


def conv_rows(x_ref, xp_ref, halo_ref, cw_ref, col, q, lanes):
    x = x_ref[:, lanes]
    prev = jnp.where(q == 0, halo_ref[:, lanes], xp_ref[:, lanes])
    cat = jnp.concatenate([prev, x], axis=0)
    acc = cw_ref[4:5, lanes] + cw_ref[0:1, lanes] * x
    shifted = []
    for k in (1, 2, 3):
        back = pltpu.roll(cat, k, 0)[HALO:, :] * col[:, SEG + k : SEG + k + 1]
        shifted.append(back)
        acc = acc + cw_ref[k : k + 1, lanes] * back
    return x, shifted, acc


def conv_state_kernel(
    x_ref, xp_ref, halo_ref, cw_ref, e_ref, hp_ref, mark_ref, u_ref, end_ref, col_ref, row_ref, et_ref
):
    q = pl.program_id(0)

    @pl.when(q == 0)
    def _():
        end_ref[...] = jnp.zeros_like(end_ref)

    e, marks = e_ref[...], mark_ref[...]
    lane = lanes_of()
    head = lane < HEADS
    raw = e + hp_ref[0:1, :]
    dt = jnp.where(head, jnp.maximum(raw, 0.0) + jnp.log1p(jnp.exp(-jnp.abs(raw))), 0.0)
    run = dot(jnp.where(triangle(), 1.0, 0.0), dt * hp_ref[1:2, :], highest)
    dec = jnp.where(head, jnp.exp(run) * marks[:, CONT : CONT + 1], 0.0)
    tail = jnp.where(head, jnp.exp(run[Q - 1 : Q, :] - run) * marks[:, LAST : LAST + 1], 0.0)
    log_dt = jnp.where(head, jnp.log(dt), 0.0)
    col = (
        run
        + pltpu.roll(dt, DT, 1)
        + pltpu.roll(dec, DEC, 1)
        + pltpu.roll(tail, TAIL, 1)
        + marks
        + pltpu.roll(log_dt, LOGDT, 1)
    )
    col_ref[...] = col
    row_ref[...] = col.T
    et = e.T
    et_ref[...] = et
    bt = et[COLB:COLC, :].astype(bf16)
    left = lane < HEADDIM
    for j in range(x_ref.shape[1] // 128):
        lanes = slice(128 * j, 128 * j + 128)
        _, _, acc = conv_rows(x_ref, xp_ref, halo_ref, cw_ref, col, q, lanes)
        u = acc * sigmoid(acc)
        u_ref[:, lanes] = u
        scaled = (u * (pair_cols(col, DT, j, left) * pair_cols(col, TAIL, j, left))).astype(bf16)
        keep = pair_cols(col[Q - 1 : Q, :], DEC, j, left[:1])
        end_ref[:, lanes] = keep * end_ref[:, lanes] + dot(bt, scaled)


def scan_kernel(
    u_ref, z_ref, col_ref, row_ref, e_ref, et_ref, s0_ref, cw_ref, gated_ref, y_ref, st_ref, S
):
    @pl.when(pl.program_id(0) == 0)
    def _():
        S[...] = s0_ref[...]

    col, row = col_ref[...], row_ref[...]
    left = lanes_of() < HEADDIM
    c = e_ref[:, COLC : COLC + STATES]
    bt = et_ref[COLB:COLC, :]
    scores = dot(c, bt, highest)
    neg = jnp.where((col[:, SEG : SEG + 1] == row[SEG : SEG + 1, :]) & triangle(), 0.0, NEG)
    c, bt = wide_left(c), bt.astype(bf16)
    for j in range(u_ref.shape[1] // 128):
        lanes = slice(128 * j, 128 * j + 128)
        uf = u_ref[:, lanes]
        u = uf.astype(bf16)
        state = S[:, lanes]
        st_ref[:, lanes] = state
        parts = []
        for h in (2 * j, 2 * j + 1):
            gap = col[:, h : h + 1] - (row[h : h + 1, :] - row[LOGDT + h : LOGDT + h + 1, :])
            parts.append((jnp.exp(gap + neg) * scores).astype(bf16))
        zero = jnp.zeros_like(u)
        both = jnp.concatenate([jnp.where(left, u, zero), jnp.where(left, zero, u)], axis=0)
        y = dot(jnp.concatenate(parts, axis=1), both)
        y = y + dot(c, stack_right(state)) * pair_cols(col, DEC, j, left) + cw_ref[5:6, lanes] * uf
        z = z_ref[:, lanes]
        y_ref[:, lanes] = y
        gated_ref[:, lanes] = (y * (z * sigmoid(z))).astype(bf16)
        scaled = (uf * (pair_cols(col, DT, j, left) * pair_cols(col, TAIL, j, left))).astype(bf16)
        keep = pair_cols(col[Q - 1 : Q, :], DEC, j, left[:1])
        S[:, lanes] = keep * state + dot(bt, scaled)


def gate_back_kernel(gg_ref, z_ref, y_ref, col_ref, et_ref, dy_ref, dz_ref, ds_ref):
    @pl.when(pl.program_id(0) == 0)
    def _():
        ds_ref[...] = jnp.zeros_like(ds_ref)

    col = col_ref[...]
    left = lanes_of() < HEADDIM
    ct = et_ref[COLC : COLC + STATES, :].astype(bf16)
    for j in range(z_ref.shape[1] // 128):
        lanes = slice(128 * j, 128 * j + 128)
        z = z_ref[:, lanes]
        gg = gg_ref[:, lanes]
        sig = sigmoid(z)
        dy = gg * (z * sig)
        dy_ref[:, lanes] = dy
        dz_ref[:, lanes] = (gg * y_ref[:, lanes] * (sig * (1.0 + z * (1.0 - sig)))).astype(bf16)
        scaled = (dy * pair_cols(col, DEC, j, left)).astype(bf16)
        keep = pair_cols(col[Q - 1 : Q, :], DEC, j, left[:1])
        ds_ref[:, lanes] = keep * ds_ref[:, lanes] + dot(ct, scaled)


def scan_back_kernel(
    u_ref, dy_ref, x_ref, xp_ref, halo_ref, cw_ref, col_ref, row_ref, e_ref, et_ref, st_ref, de_ref, hp_ref,
    lw_ref, sm_ref, pick_ref, head_ref,
    dx_ref, de_out_ref, cg_ref, edge_ref, hg_ref,
    D, WA, CONST, TAILS, DECS, DS, ST, SUMS, DG,
):
    step = pl.program_id(0)
    q = pl.num_programs(0) - 1 - step

    @pl.when(step == 0)
    def _():
        D[...] = de_ref[...]
        cg_ref[...] = jnp.zeros_like(cg_ref)
        edge_ref[...] = jnp.zeros_like(edge_ref)
        hg_ref[...] = jnp.zeros_like(hg_ref)
        WA[...] = jnp.zeros_like(WA)
        CONST[...] = jnp.zeros_like(CONST)
        DS[...] = jnp.zeros_like(DS)
        ST[...] = jnp.zeros_like(ST)

    col, row = col_ref[...], row_ref[...]
    lane = lanes_of()
    left = lane < HEADDIM
    e = e_ref[...]
    b, ct = e[:, COLB:COLC], et_ref[COLC : COLC + STATES, :]
    scores = dot(b, ct, highest)
    neg = jnp.where((col[:, SEG : SEG + 1] == row[SEG : SEG + 1, :]) & triangle(transposed=True), 0.0, NEG)
    b, ct, c = wide_left(b), ct.astype(bf16), wide_left(e[:, COLC : COLC + STATES])
    DG[...] = jnp.zeros_like(DG)
    SUMS[...] = jnp.zeros_like(SUMS)
    for j in range(u_ref.shape[1] // 128):
        lanes = slice(128 * j, 128 * j + 128)
        u = u_ref[:, lanes]
        dyf = dy_ref[:, lanes]
        dy = dyf.astype(bf16)
        dt = pair_cols(col, DT, j, left)
        dec = pair_cols(col, DEC, j, left)
        tail = pair_cols(col, TAIL, j, left)
        keep = pair_cols(col[Q - 1 : Q, :], DEC, j, left[:1])
        state, grad_state = st_ref[:, lanes], D[:, lanes]
        DS[COLB:COLC, lanes] = grad_state
        ST[COLC : COLC + STATES, lanes] = state
        xs = u * dt
        zero = jnp.zeros_like(dy)
        both = jnp.concatenate([jnp.where(left, dy, zero), jnp.where(left, zero, dy)], axis=0)
        d_mat = dot_t(xs.astype(bf16), both)
        mats, pairs, d_scores = [], [], None
        for i, h in enumerate((2 * j, 2 * j + 1)):
            decay = jnp.exp((row[h : h + 1, :] - col[:, h : h + 1]) + neg)
            mat = decay * scores
            dm = d_mat[:, Q * i : Q * i + Q]
            d_scores = decay * dm if d_scores is None else d_scores + decay * dm
            mats.append(mat.astype(bf16))
            pairs.append((mat * dm).astype(bf16))
        DG[...] += d_scores
        dxs = dot(jnp.concatenate(mats, axis=1), both)
        spans = dot(jnp.concatenate(pairs, axis=1), lw_ref[...]) * sm_ref[...]
        sums = jnp.sum(spans, axis=0, keepdims=True)
        WA[2 * j : 2 * j + 1, :] = sums[:, :Q]
        WA[2 * j + 1 : 2 * j + 2, :] = sums[:, Q:]
        from_tail = tail * dot(b, stack_right(grad_state))
        dxs = dxs + from_tail
        ydec = dyf * dec
        found = [u * dxs, ydec * dot(c, stack_right(state)), xs * from_tail]
        SUMS[...] += dot(jnp.concatenate([v.astype(bf16) for v in found], axis=1), pick_ref[j])
        TAILS[:, lanes] = (xs * tail).astype(bf16)
        low_dec = ydec.astype(bf16)
        DECS[:, lanes] = low_dec
        CONST[0:1, lanes] = keep * jnp.sum(state * grad_state, axis=0, keepdims=True)
        D[:, lanes] = keep * grad_state + dot(ct, low_dec)

        x, shifted, acc = conv_rows(x_ref, xp_ref, halo_ref, cw_ref, col, q, lanes)
        sig = sigmoid(acc)
        dconv = (dxs * dt + cw_ref[5:6, lanes] * dyf) * (sig * (1.0 + acc * (1.0 - sig)))
        dx = cw_ref[0:1, lanes] * dconv
        cg_ref[0:1, lanes] += jnp.sum(dconv * x, axis=0, keepdims=True)
        for k in (1, 2, 3):
            masked = dconv * col[:, SEG + k : SEG + k + 1]
            after = edge_ref[8 * (k - 1) : 8 * k, lanes]
            cat = jnp.concatenate([masked, after], axis=0)
            dx = dx + cw_ref[k : k + 1, lanes] * pltpu.roll(cat, Q + 8 - k, 0)[:Q, :]
            edge_ref[8 * (k - 1) : 8 * k, lanes] = masked[:8, :]
            cg_ref[k : k + 1, lanes] += jnp.sum(dconv * shifted[k - 1], axis=0, keepdims=True)
        cg_ref[4:5, lanes] += jnp.sum(dconv, axis=0, keepdims=True)
        cg_ref[5:6, lanes] += jnp.sum(dyf * u, axis=0, keepdims=True)
        dx_ref[:, lanes] = dx.astype(bf16)

    head = lane < HEADS
    found = SUMS[...]
    suffix = jnp.where(triangle(transposed=True), 1.0, 0.0)
    prefix = jnp.where(triangle(strict=True), 1.0, 0.0)
    d_step = (
        WA[...].T
        + dot(suffix, pltpu.roll(found, 128 - HEADS, 1), highest)
        + dot(prefix, pltpu.roll(found, 128 - 2 * HEADS, 1), highest)
        + dot(CONST[...], head_ref[...], highest)[0:1, :]
    )
    d_dt = d_step * hp_ref[1:2, :] + found
    d_raw = jnp.where(head, d_dt * sigmoid(e + hp_ref[0:1, :]), 0.0)
    step_dt = jnp.where(head, pltpu.roll(col, 128 - DT, 1), 0.0)
    hg_ref[0:1, :] += jnp.sum(d_raw, axis=0, keepdims=True)
    hg_ref[1:2, :] += jnp.sum(jnp.where(head, d_step, 0.0) * step_dt, axis=0, keepdims=True) * hp_ref[1:2, :]
    total = DG[...]
    b_part = jnp.where((lane >= COLB) & (lane < COLC), e, 0.0)
    c_part = jnp.where((lane >= COLC) & (lane < COLC + STATES), e, 0.0)
    de_out_ref[...] = (
        d_raw
        + dot_t(TAILS[...], DS[...].astype(bf16))
        + dot_t(DECS[...], ST[...].astype(bf16))
        + dot(total, pltpu.roll(c_part, 128 - STATES, 1), highest)
        + dot(total.T, pltpu.roll(b_part, STATES, 1), highest)
    )


def norm_kernel(*refs):
    *row_refs, gain_ref, hidden_ref, out_ref, turned_ref = refs
    rows = row_refs[0][...]
    for r in row_refs[1:]:
        rows = rows + r[...]
    hidden_ref[...] = rows
    scale = lax.rsqrt(jnp.mean(rows * rows, axis=-1, keepdims=True) + epsilon)
    normed = rows * scale * gain_ref[...]
    out_ref[...] = normed.astype(bf16)
    turned_ref[...] = normed.T.astype(bf16)


def norm_back_kernel(grad_ref, rows_ref, gain_ref, *refs):
    *base_refs, high_ref, low_ref, part_ref, turned_ref = refs

    @pl.when(pl.program_id(0) == 0)
    def _():
        part_ref[...] = jnp.zeros_like(part_ref)

    rows, grad = rows_ref[...], grad_ref[...]
    scale = lax.rsqrt(jnp.mean(rows * rows, axis=-1, keepdims=True) + epsilon)
    unit = rows * scale
    part_ref[0:1, :] += jnp.sum(grad * unit, axis=0, keepdims=True)
    unit_grad = grad * gain_ref[...]
    total = scale * (unit_grad - unit * jnp.mean(unit_grad * unit, axis=-1, keepdims=True))
    for r in base_refs:
        total = total + r[...].astype(f32)
    high = total.astype(bf16)
    high_ref[...] = high
    low_ref[...] = (total - high.astype(f32)).astype(bf16)
    turned_ref[...] = total.T.astype(bf16)


def flip(i, mask):
    bit = 1
    while bit <= mask:
        if mask & bit:
            i = i + bit * (1 - 2 * ((i // bit) % 2))
        bit *= 2
    return i


class Load:
    def __init__(self, *movers):
        self.reads, self.updates, self.news, self.copies = {}, {}, {}, []
        self.movers = movers
        for mover in movers:
            reads, updates, news, copies = mover.moves()
            self.reads.update(reads)
            self.updates.update(updates)
            self.news.update(news)
            self.copies += copies

    def arrive(self, got):
        for mover in self.movers:
            mover.take(got)


IDS = {}


def run(body, grid, in_specs, out_specs, out_shape, scratch, args, name, estimate=None, load=None, vmem=56):
    params = dict(dimension_semantics=("arbitrary",) * len(grid), vmem_limit_bytes=vmem * 1024 * 1024)
    if load is None:
        return pl.pallas_call(
            body, name=name, grid=grid, in_specs=in_specs, out_specs=out_specs, out_shape=out_shape,
            scratch_shapes=scratch, compiler_params=pltpu.CompilerParams(**params), cost_estimate=estimate,
        )(*args)
    cid = IDS.setdefault(name, len(IDS) + 1)
    reads, updates, news = list(load.reads), list(load.updates), list(load.news)
    n_in, n_out, n_scratch, n_copies = len(args), len(out_shape), len(scratch), len(load.copies)
    routes = []
    for c in load.copies:
        if c[4] is not None and c[4] not in routes:
            routes.append(c[4])

    def kernel(*refs):
        ins, rest = refs[:n_in], refs[n_in:]
        held = dict(zip(reads, rest))
        rest = rest[len(reads) + len(updates) :]
        outs, rest = rest[:n_out], rest[n_out:]
        held.update(zip(updates + news, rest))
        rest = rest[len(updates) + len(news) :]
        mine, (send, recv) = rest[:n_scratch], rest[n_scratch:]

        def device(route):
            return {route[0]: flip(lax.axis_index(route[0]), route[1])}

        def make(i, c):
            src, dst = held[c[0]].at[c[1]], held[c[2]].at[c[3]]
            if c[4] is None:
                return pltpu.make_async_copy(src, dst, recv.at[i])
            return pltpu.make_async_remote_copy(
                src_ref=src, dst_ref=dst, send_sem=send.at[i], recv_sem=recv.at[i],
                device_id=device(c[4]), device_id_type=pl.DeviceIdType.MESH,
            )

        first, last = pl.program_id(0) == 0, pl.program_id(0) == grid[0] - 1
        for axis in range(1, len(grid)):
            first = first & (pl.program_id(axis) == 0)
            last = last & (pl.program_id(axis) == grid[axis] - 1)

        @pl.when(first)
        def _():
            barrier = pltpu.get_barrier_semaphore()
            for route in routes:
                pl.semaphore_signal(
                    barrier, inc=1, device_id=device(route), device_id_type=pl.DeviceIdType.MESH
                )
            pl.semaphore_wait(barrier, len(routes))
            for i, c in enumerate(load.copies):
                make(i, c).start()

        if body is not None:
            body(*ins, *outs, *mine)

        @pl.when(last)
        def _():
            for i, c in enumerate(load.copies):
                make(i, c).wait()

    hbm = pl.BlockSpec(memory_space=pltpu.HBM)
    result = pl.pallas_call(
        kernel,
        name=name,
        grid=grid,
        in_specs=list(in_specs) + [hbm] * (len(reads) + len(updates)),
        out_specs=list(out_specs) + [hbm] * (len(updates) + len(news)),
        out_shape=list(out_shape)
        + [jax.ShapeDtypeStruct(load.updates[k].shape, load.updates[k].dtype) for k in updates]
        + [load.news[k] for k in news],
        scratch_shapes=list(scratch) + [pltpu.SemaphoreType.DMA((n_copies,)), pltpu.SemaphoreType.DMA((n_copies,))],
        input_output_aliases={n_in + len(reads) + i: n_out + i for i in range(len(updates))},
        compiler_params=pltpu.CompilerParams(collective_id=cid, has_side_effects=True, **params),
        cost_estimate=estimate,
    )(*args, *[load.reads[k] for k in reads], *[load.updates[k] for k in updates])
    load.arrive(dict(zip(updates + news, result[n_out:])))
    return result[:n_out]


def matmul(jobs, dtype, tile, name, load=None, nt=False, turned=False):
    n_jobs, n_pairs = len(jobs), len(jobs[0])
    rows = jobs[0][0][0].shape[0]
    columns = jobs[0][0][1].shape[0 if nt else 1]
    tiles = columns // tile

    def at(job):
        def place(j, t):
            return jnp.where(j == job, t, jnp.where(j < job, 0, tiles - 1))

        return place

    args, in_specs = [], []
    for job, pairs in enumerate(jobs):
        for left, right in pairs:
            args += [left, right]
            k = left.shape[1]
            in_specs.append(pl.BlockSpec((rows, k), lambda j, t: (0, 0), pipeline_mode=pl.Buffered(1)))
            if nt:
                in_specs.append(pl.BlockSpec((tile, k), lambda j, t, p=at(job): (p(j, t), 0)))
            else:
                in_specs.append(pl.BlockSpec((k, tile), lambda j, t, p=at(job): (0, p(j, t))))
    out_specs = [pl.BlockSpec((rows, tile), lambda j, t, p=at(job): (0, p(j, t))) for job in range(n_jobs)]
    out_shape = [jax.ShapeDtypeStruct((rows, columns), dtype)] * n_jobs
    if turned:
        out_specs += [pl.BlockSpec((tile, rows), lambda j, t, p=at(job): (p(j, t), 0)) for job in range(n_jobs)]
        out_shape += [jax.ShapeDtypeStruct((columns, rows), dtype)] * n_jobs

    def body(*refs):
        ins, outs = refs[: 2 * n_jobs * n_pairs], refs[2 * n_jobs * n_pairs :]
        for job in range(n_jobs):

            @pl.when(pl.program_id(0) == job)
            def _(job=job):
                total = None
                for p in range(n_pairs):
                    left, right = ins[2 * (job * n_pairs + p)], ins[2 * (job * n_pairs + p) + 1]
                    term = (dot_t if nt else dot)(left[...], right[...])
                    total = term if total is None else total + term
                outs[job][...] = total.astype(dtype)
                if turned:
                    outs[n_jobs + job][...] = total.T.astype(dtype)

    depth = sum(p[0].shape[1] for p in jobs[0])
    return run(
        body, (n_jobs, tiles), in_specs, out_specs, out_shape, [], args, name,
        pl.CostEstimate(
            flops=2 * n_jobs * rows * columns * depth, bytes_accessed=4 * n_jobs * rows * columns, transcendentals=0
        ),
        load,
    )


def feed_forward(normed, cot, gate_w, up_w, down_w):
    tokens, width = normed.shape
    cols, tile, step = gate_w[0].shape[1], 512, 256
    tiles = cols // tile

    def at(job):
        def place(j, t):
            return jnp.where(j == job, t, jnp.where(j < job, 0, tiles - 1))

        return place

    whole = pl.BlockSpec((tokens, width), lambda j, t: (0, 0), pipeline_mode=pl.Buffered(1))
    args, in_specs, out_specs = [normed, cot], [whole, whole], []
    for b in (0, 1):
        args += [gate_w[b], up_w[b], down_w[b]]
        in_specs += [pl.BlockSpec((width, tile), lambda j, t, p=at(b): (0, p(j, t)))] * 3
        out_specs += [pl.BlockSpec((tokens, tile), lambda j, t, p=at(b): (0, p(j, t)))] * 3

    def body(n_ref, c_ref, *refs):
        for b in (0, 1):
            wg, wu, wd = refs[3 * b : 3 * b + 3]
            act, gg, ug = refs[6 + 3 * b : 9 + 3 * b]

            @pl.when(pl.program_id(0) == b)
            def _(wg=wg, wu=wu, wd=wd, act=act, gg=gg, ug=ug):
                for i in range(tokens // step):
                    rows = slice(step * i, step * i + step)
                    gate, up, back = dot(n_ref[rows, :], wg[...]), dot(n_ref[rows, :], wu[...]), dot(c_ref[rows, :], wd[...])
                    sig = sigmoid(gate)
                    silu = gate * sig
                    act[rows, :] = (silu * up).astype(bf16)
                    gg[rows, :] = (back * up * sig * (1.0 + gate * (1.0 - sig))).astype(bf16)
                    ug[rows, :] = (back * silu).astype(bf16)

    out = run(
        body, (2, tiles), in_specs, out_specs, [jax.ShapeDtypeStruct((tokens, cols), bf16)] * 6, [], args,
        "feed_forward", pl.CostEstimate(flops=12 * tokens * cols * width, bytes_accessed=12 * tokens * cols, transcendentals=0),
    )
    return [out[0], out[3]], [out[1], out[4]], [out[2], out[5]]


def carry_only(load, name):
    run(None, (1,), [], [], [], [], [], name, None, load)


ALL = (slice(None),)


def low_sum(a, b):
    return (a.astype(f32) + b.astype(f32)).astype(bf16)


class Gather:
    def __init__(self, key, shard, n):
        rows, cols = shard.shape
        self.n, self.key, self.phase = n, key, 0
        self.shard = shard.reshape(2, rows // 2, cols)
        self.cols = cols

    def moves(self):
        k, n = self.key, self.n
        q = n // 4
        s, a, b = k + "s", k + "0", k + "1"
        if self.phase == 0:
            whole = jax.ShapeDtypeStruct((2, n) + self.shard.shape[1:], bf16)
            copies = [
                (s, (i,), a, (i, m), ("fsdp", m << 2) if m else None) for m in range(q) for i in (0, 1)
            ]
            return {s: self.shard}, {}, {a: whole, b: whole}, copies
        near, far, both = slice(0, q), slice(q, 2 * q), slice(0, 2 * q)
        if self.phase == 1:
            copies = [(a, (0, near), b, (0, near), ("tp", 1)), (a, (1, near), a, (1, far), ("fsdp", 2))]
        elif self.phase == 2:
            copies = [
                (a, (0, near), a, (0, far), ("fsdp", 2)),
                (b, (0, near), b, (0, far), ("fsdp", 2)),
                (a, (1, both), b, (1, both), ("tp", 1)),
            ]
        else:
            copies = [(h, (i, both), h, (i, slice(2 * q, 4 * q)), ("fsdp", 1)) for h in (a, b) for i in (0, 1)]
        return {}, {a: self.halves[0], b: self.halves[1]}, {}, copies

    def take(self, got):
        self.halves = [got[self.key + "0"], got[self.key + "1"]]
        self.phase += 1
        if self.phase == 4:
            self.full = [h.reshape(-1, self.cols) for h in self.halves]


class Scatter:
    def __init__(self, key, grads, n, piece=0, pieces=1):
        self.n, self.key, self.phase = n, f"{key}{piece}_", 0
        cols = grads[0].shape[1]
        self.cols = cols // pieces
        self.rows = grads[0].shape[0] // n
        self.now = [g.reshape(2, n, self.rows // 2, cols) for g in grads]
        self.range = slice(piece * self.cols, (piece + 1) * self.cols)

    def moves(self):
        n, v = self.n, self.now
        q = n // 4
        part = (self.rows // 2, self.cols)
        far, rest = slice(q, 2 * q), slice(2 * q, 4 * q)

        def name(i):
            return f"{self.key}{i}"

        def new(*dims):
            return jax.ShapeDtypeStruct(dims + part, bf16)

        if self.phase == 0:
            news = [new(2, 2 * q), new(2, 2 * q)]
            copies = [
                (b, (i, rest, slice(None), self.range), b, (i,), ("fsdp", 1)) for b in (0, 1) for i in (0, 1)
            ]
        elif self.phase == 1:
            news = [new(q), new(q), new(2 * q)]
            copies = [
                (0, (0, far), 0, ALL, ("fsdp", 2)),
                (1, (0, far), 1, ALL, ("fsdp", 2)),
                (1, (1,), 2, ALL, ("tp", 1)),
            ]
        elif self.phase == 2:
            news = [new(q), new(q)]
            copies = [(1, ALL, 0, ALL, ("tp", 1)), (2, (far,), 1, ALL, ("fsdp", 2))]
        else:
            news = [new(2) for _ in range(1, q)]
            copies = [(i, (m,), m - 1, (i,), ("fsdp", m << 2)) for m in range(1, q) for i in (0, 1)]
        reads = {name(f"v{i}"): a for i, a in enumerate(v) if any(c[0] == i for c in copies)}
        self.names = [name(f"r{i}") for i in range(len(news))]
        copies = [(name(f"v{c[0]}"), c[1], self.names[c[2]], c[3], c[4]) for c in copies]
        return reads, {}, dict(zip(self.names, news)), copies

    def take(self, got):
        r, v = [got[k] for k in self.names], self.now
        q = self.n // 4
        if self.phase == 0:
            self.now = [low_sum(p[:, : 2 * q, :, self.range], a) for p, a in zip(v, r)]
        elif self.phase == 1:
            self.now = [low_sum(v[0][0, :q], r[0]), low_sum(v[1][0, :q], r[1]), low_sum(v[0][1], r[2])]
        elif self.phase == 2:
            self.now = [low_sum(v[0], r[0]), low_sum(v[2][:q], r[1])]
        else:
            total = jnp.stack([v[0][0], v[1][0]]).astype(f32)
            for p in r:
                total = total + p.astype(f32)
            self.out = total.reshape(self.rows, self.cols)
        self.phase += 1


def specs(blocks, ch, reverse):
    def at(q):
        return blocks - 1 - q if reverse else q

    def whole(rows, cols):
        return pl.BlockSpec((rows, cols), lambda q: (0, 0))

    return dict(
        main=pl.BlockSpec((Q, ch), lambda q: (at(q), 0)),
        prev=pl.BlockSpec((HALO, ch), lambda q: (jnp.maximum(at(q) * (Q // HALO) - 1, 0), 0)),
        tile=pl.BlockSpec((Q, 128), lambda q: (at(q), 0)),
        state=pl.BlockSpec((STATES, ch), lambda q: (at(q), 0)),
        halo=whole(HALO, ch), row8=whole(8, ch), row24=whole(24, ch), row16=whole(STATES, ch), small=whole(8, 128),
    )


def shape(dims, dtype):
    return jax.ShapeDtypeStruct(dims, dtype)


def cost(flops, moved):
    return pl.CostEstimate(flops=int(flops), bytes_accessed=int(moved), transcendentals=0)


def conv_state(x, halo, cw, e, hp, marks, tag="", load=None):
    tokens, ch = x.shape
    s = specs(tokens // Q, ch, False)
    return run(
        conv_state_kernel,
        (tokens // Q,),
        [s["main"], s["prev"], s["halo"], s["row8"], s["tile"], s["small"], s["tile"]],
        [s["main"], s["row16"], s["tile"], s["tile"], s["tile"]],
        [shape((tokens, ch), f32), shape((STATES, ch), f32)] + [shape((tokens, 128), f32)] * 3,
        [],
        [x, x, halo, cw, e, hp, marks],
        "conv_state" + tag,
        cost(tokens * ch * 5000, 4 * tokens * ch),
        load,
    )


def scan_forward(u, z, col, row, e, et, s0, cw, tag="", load=None):
    tokens, ch = u.shape
    s = specs(tokens // Q, ch, False)
    return run(
        scan_kernel,
        (tokens // Q,),
        [s["main"], s["main"], s["tile"], s["tile"], s["tile"], s["tile"], s["row16"], s["row8"]],
        [s["main"], s["main"], s["state"]],
        [shape((tokens, ch), bf16), shape((tokens, ch), f32), shape((tokens // Q * STATES, ch), f32)],
        [pltpu.VMEM((STATES, ch), f32)],
        [u, z, col, row, e, et, s0, cw],
        "scan_forward" + tag,
        cost(tokens * ch * 10000, 8 * tokens * ch),
        load,
    )


def gate_backward(gg, z, y, col, et, tag="", load=None):
    tokens, ch = z.shape
    s = specs(tokens // Q, ch, True)
    return run(
        gate_back_kernel,
        (tokens // Q,),
        [s["main"], s["main"], s["main"], s["tile"], s["tile"]],
        [s["main"], s["main"], s["row16"]],
        [shape((tokens, ch), f32), shape((tokens, ch), bf16), shape((STATES, ch), f32)],
        [],
        [gg, z, y, col, et],
        "gate_backward" + tag,
        cost(tokens * ch * 5000, 10 * tokens * ch),
        load,
    )


def scan_backward(u, dy, x, halo, cw, col, row, e, et, st, de, hp, tag="", load=None):
    tokens, ch = u.shape
    s = specs(tokens // Q, ch, True)
    place = jnp.arange(2 * Q)
    lower = ((place[:, None] >= place[None, :]) & (place[:, None] // Q == place[None, :] // Q)).astype(bf16)
    strict = (jnp.arange(Q)[:, None] < (place % Q)[None, :]).astype(f32)
    pairs = ch // 128
    lane = jnp.arange(3 * 128)
    target = (lane // 128) * HEADS + 2 * jnp.arange(pairs)[:, None] + ((lane % 128) // HEADDIM)[None, :]
    pick = (target[:, :, None] == jnp.arange(128)[None, None, :]).astype(bf16)
    by_head = (jnp.arange(ch)[:, None] // HEADDIM == jnp.arange(128)[None, :]).astype(f32)
    return run(
        scan_back_kernel,
        (tokens // Q,),
        [
            s["main"], s["main"], s["main"], s["prev"], s["halo"], s["row8"], s["tile"], s["tile"], s["tile"],
            s["tile"], s["state"], s["row16"], s["small"],
            pl.BlockSpec((2 * Q, 2 * Q), lambda q: (0, 0)), pl.BlockSpec((Q, 2 * Q), lambda q: (0, 0)),
            pl.BlockSpec((pairs, 3 * 128, 128), lambda q: (0, 0, 0)), pl.BlockSpec((ch, 128), lambda q: (0, 0)),
        ],
        [s["main"], s["tile"], s["row8"], s["row24"], s["small"]],
        [
            shape((tokens, ch), bf16), shape((tokens, 128), f32), shape((8, ch), f32), shape((24, ch), f32),
            shape((8, 128), f32),
        ],
        [
            pltpu.VMEM((STATES, ch), f32), pltpu.VMEM((128, Q), f32), pltpu.VMEM((8, ch), f32),
            pltpu.VMEM((Q, ch), bf16), pltpu.VMEM((Q, ch), bf16), pltpu.VMEM((128, ch), f32),
            pltpu.VMEM((128, ch), f32), pltpu.VMEM((Q, 128), f32), pltpu.VMEM((Q, Q), f32),
        ],
        [u, dy, x, x, halo, cw, col, row, e, et, st, de, hp, lower, strict, pick, by_head],
        "scan_backward" + tag,
        cost(tokens * ch * 25000, 12 * tokens * ch),
        load,
    )


def norm_specs(width):
    main = pl.BlockSpec((Q, width), lambda q: (q, 0))
    return main, pl.BlockSpec((width, Q), lambda q: (0, q)), pl.BlockSpec((1, width), lambda q: (0, 0))


def norm_forward(rows, gain_row, name, load=None):
    tokens, width = rows[0].shape
    main, turned, one = norm_specs(width)
    return run(
        norm_kernel,
        (tokens // Q,),
        [main] * len(rows) + [one],
        [main, main, turned],
        [shape((tokens, width), f32), shape((tokens, width), bf16), shape((width, tokens), bf16)],
        [],
        [*rows, gain_row],
        name,
        cost(tokens * width * 20, 12 * tokens * width),
        load,
    )


def norm_back(grad, rows, gain_row, bases, name, load=None):
    tokens, width = rows.shape
    main, turned, one = norm_specs(width)
    high, low, part, high_t = run(
        norm_back_kernel,
        (tokens // Q,),
        [main, main, one] + [main] * len(bases),
        [main, main, pl.BlockSpec((8, width), lambda q: (0, 0)), turned],
        [
            shape((tokens, width), bf16), shape((tokens, width), bf16), shape((8, width), f32),
            shape((width, tokens), bf16),
        ],
        [],
        [grad, rows, gain_row, *bases],
        name,
        cost(tokens * width * 20, 16 * tokens * width),
        load,
    )
    return high, low, high_t, part[0]


def token_marks(seg, seg_before):
    tokens = seg.shape[0]
    by_block = seg.reshape(tokens // Q, Q)
    before = jnp.concatenate([seg_before[2:3], by_block[:-1, Q - 1]])
    padded = jnp.concatenate([seg_before, seg])
    found = [seg.astype(f32)] + [(padded[3 - k : 3 - k + tokens] == seg).astype(f32) for k in (1, 2, 3)]
    found.append((by_block == before[:, None]).astype(f32).reshape(-1))
    found.append((by_block == by_block[:, Q - 1 :]).astype(f32).reshape(-1))
    lane = jnp.arange(128)[None, :]
    out = jnp.zeros((tokens, 128), f32)
    for i, v in enumerate(found):
        out = jnp.where(lane == SEG + i, v[:, None], out)
    return out


def swap(x, axis, n, mask):
    return lax.ppermute(x, axis, [(i, i ^ mask) for i in range(n)])


def sum_all(x, n):
    bit = 1
    while bit < n:
        x = x + swap(x, "fsdp", n, bit)
        bit *= 2
    return x


def bf_dot(a, b):
    return jnp.dot(a, b, preferred_element_type=f32)


def make_local(n):
    def local(
        layer_in, seg_ids, gain_one, x_weight, z_weight, dt_weight, bc_weight, conv_weight, conv_bias,
        dt_bias, a_log, d_skip, out_weight, gain_two, gate_weight, up_weight, down_weight, cotangent,
    ):
        tokens, width = layer_in.shape
        rows, ch = x_weight.shape
        heads = dt_weight.shape[1]
        states = bc_weight.shape[1] // 2
        me, half = lax.axis_index("fsdp"), lax.axis_index("tp")

        epack = jnp.concatenate([dt_weight, bc_weight, jnp.zeros((rows, EXTRA - heads - 2 * states), bf16)], axis=1)
        X, E = Gather("x", x_weight, n), Gather("e", epack, n)
        Z, O = Gather("z", z_weight, n), Gather("o", out_weight, n)
        G, U, D = Gather("g", gate_weight, n), Gather("u", up_weight, n), Gather("d", down_weight, n)

        rate = -jnp.exp(a_log)
        pad = jnp.zeros((128 - heads,), f32)
        by_head = jnp.stack([jnp.concatenate([dt_bias, pad]), jnp.concatenate([rate, pad])])
        small = jnp.concatenate(
            [
                conv_weight,
                conv_bias[None, :],
                jnp.repeat(d_skip, HEADDIM)[None, :],
                jnp.pad(by_head, ((0, 0), (0, ch - 128))),
            ],
            axis=0,
        )
        smalls = [small, swap(small, "tp", 2, 1)]
        head_rows = [jnp.pad(v[6:8, :128], ((0, 6), (0, 0))) for v in smalls]
        before_rows = lax.ppermute(layer_in[tokens - HALO :], "tp", [(0, 1)])
        seg = lax.dynamic_slice(seg_ids, (half * tokens,), (tokens,))
        seg_before = jnp.where(half == 0, -1, seg_ids[tokens - 3 : tokens])

        part = rows // 2
        place = jnp.arange(2 * n)
        q = n // 4
        p = place % n
        part_at = (me ^ (p // (2 * q) + 2 * ((p // q) % 2) + 4 * (p % q))) * 2 + place // n
        seek = (place // 2) ^ me
        place_of = (place % 2) * n + (seek % 2) * 2 * q + ((seek // 2) % 2) * q + seek // 4
        col_at = (part_at[:, None] * part + jnp.arange(part)[None, :]).reshape(-1)
        turn = (jnp.arange(width)[:, None] == col_at[None, :]).astype(bf16)

        def to_local(v):
            return jnp.take(v.reshape(2 * n, part), part_at, axis=0).reshape(-1)

        def to_global(v):
            return jnp.take(v.reshape(2 * n, part), place_of, axis=0).reshape(-1)

        gain_one, gain_two = to_local(gain_one)[None, :], to_local(gain_two)[None, :]
        (rows_in,) = matmul([[(layer_in, turn)]], f32, 512, "turn_rows", Load(X, E))
        rows_in, normed, normed_t = norm_forward([rows_in], gain_one, "norm_one", Load(X, E, Z))
        cot_low, cot_t = matmul([[(cotangent, turn)]], bf16, 512, "turn_cotangent", Load(X, E, O), turned=True)
        carry_only(Load(X, E, Z), "carry_one")
        halo_rows = bf_dot(before_rows, turn)
        halo_scale = lax.rsqrt(jnp.mean(halo_rows * halo_rows, axis=-1, keepdims=True) + epsilon)
        normed_before = (halo_rows * halo_scale * gain_one).astype(bf16)
        marks = token_marks(seg, seg_before)

        xs = matmul([[(normed, w)] for w in X.full], f32, 512, "project_x", Load(Z, O, G))
        saved = []
        for b in (0, 1):
            v = dict(x=xs[b], cw=smalls[b], hp=head_rows[b])
            v["e"] = bf_dot(normed, E.full[b])
            v["halo"] = bf_dot(normed_before, X.full[b])
            load = Load(Z, O, U) if b == 0 else Load(G, O, D)
            v["u"], v["end"], v["col"], v["row"], v["et"] = conv_state(
                v["x"], v["halo"], v["cw"], v["e"], v["hp"], marks, tag=str(b), load=load
            )
            saved.append(v)
        starts = lax.ppermute(jnp.stack([v["end"] for v in saved]), "tp", [(0, 1)])[::-1]
        zs = matmul([[(normed, w)] for w in Z.full], f32, 512, "project_z", Load(G))
        for b in (0, 1):
            v = saved[b]
            v["z"] = zs[b]
            v["gated"], v["y"], v["states"] = scan_forward(
                v["u"], v["z"], v["col"], v["row"], v["e"], v["et"], starts[b], v["cw"],
                tag=str(b), load=Load(G, U, D) if b == 0 else Load(U),
            )
        (mixed,) = matmul(
            [[(v["gated"], w) for v, w in zip(saved, O.full)]], f32, 512, "project_out", Load(U, D), nt=True
        )
        hidden, normed_two, two_t = norm_forward([rows_in, mixed], gain_two, "norm_two", Load(D))

        acts, gate_grads, up_grads = feed_forward(normed_two, cot_low, G.full, U.full, D.full)
        def halves(key, grads):
            return [Scatter(key, grads, n, i, 2) for i in (0, 1)]

        da, db = halves("d", matmul([[(cot_t, a)] for a in acts], bf16, 512, "down_grad"))
        ga, gb = halves("g", matmul([[(two_t, a)] for a in gate_grads], bf16, 512, "gate_grad", Load(da, db)))
        ua, ub = halves("u", matmul([[(two_t, a)] for a in up_grads], bf16, 512, "up_grad", Load(da, ga, gb)))
        (fed,) = matmul([list(zip(acts, D.full))], f32, 512, "project_down", Load(db, da, ua, ub), nt=True)
        layer_out = matmul([[((hidden + fed).astype(bf16), turn)]], bf16, 512, "turn_out", nt=True)[0]
        (grad_two,) = matmul(
            [list(zip(gate_grads, G.full)) + list(zip(up_grads, U.full))], f32, 256, "two_back",
            Load(ga, gb, db, da), nt=True,
        )
        mixed_grad, mixed_low, mixed_t, gain_two_part = norm_back(
            grad_two, hidden, gain_two, [cot_low], "norm_two_back", Load(ga, db)
        )

        so = Scatter("o", matmul([[(mixed_t, v["gated"])] for v in saved], bf16, 512, "out_grad", Load(ua, ga)), n)
        gg = matmul([[(mixed_grad, w)] for w in O.full], f32, 512, "gated_back", Load(gb, so))
        for b in (0, 1):
            v = saved[b]
            v["dy"], v["dz"], v["ds"] = gate_backward(
                gg[b], v["z"], v["y"], v["col"], v["et"], tag=str(b), load=Load(ua, gb) if b == 0 else None
            )
        ends = lax.ppermute(jnp.stack([v["ds"] for v in saved]), "tp", [(1, 0)])[::-1]
        sz = Scatter("z", matmul([[(normed_t, v["dz"])] for v in saved], bf16, 512, "z_grad", Load(ub, ua)), n)
        for b in (0, 1):
            v = saved[b]
            v["dx"], v["de"], v["cg"], v["edge"], v["hg"] = scan_backward(
                v["u"], v["dy"], v["x"], v["halo"], v["cw"], v["col"], v["row"], v["e"], v["et"], v["states"],
                ends[b], v["hp"], tag=str(b), load=Load(sz, so, ub) if b else Load(so, ub, sz),
            )
        edges = lax.ppermute(jnp.stack([v["edge"] for v in saved]), "tp", [(1, 0)])[::-1]
        shared = 0.5 * (saved[0]["de"] + saved[1]["de"])
        own_lane = jnp.arange(EXTRA)[None, :] < heads
        for b in (0, 1):
            v = saved[b]
            cw, edge = v["cw"], edges[b].reshape(3, 8, ch)
            fix = [jnp.zeros((HALO - 3, ch), f32)]
            for j in (3, 2, 1):
                fix.append(sum(cw[k : k + 1] * edge[k - 1, k - j : k - j + 1] for k in range(j, 4)))
            last = v["dx"][tokens - HALO :].astype(f32) + jnp.concatenate(fix, axis=0)
            v["dx"] = lax.dynamic_update_slice(v["dx"], last.astype(bf16), (tokens - HALO, 0))
            v["de"] = jnp.where(own_lane, v["de"], shared).astype(bf16)
        xa, xb = halves("x", matmul([[(normed_t, v["dx"])] for v in saved], bf16, 512, "x_grad", Load(sz, so)))
        se = Scatter("e", matmul([[(normed_t, v["de"])] for v in saved], bf16, 128, "e_grad"), n)
        pairs = [(v["dx"], w) for v, w in zip(saved, X.full)] + [(v["de"], w) for v, w in zip(saved, E.full)]
        (grad_x,) = matmul([pairs], f32, 512, "x_back", Load(xa, xb, se, sz), nt=True)
        (grad_z,) = matmul([[(v["dz"], w) for v, w in zip(saved, Z.full)]], f32, 512, "z_back", Load(xa, xb, se), nt=True)
        high, low, _, gain_one_part = norm_back(
            grad_x + grad_z, rows_in, gain_one, [mixed_grad, mixed_low], "norm_one_back", Load(xa, xb, se)
        )
        (input_grad,) = matmul([[(high, turn), (low, turn)]], f32, 512, "turn_back", Load(xa, xb, se), nt=True)

        def small_row(v):
            cg, hg = v["cg"], v["hg"]
            skip = jnp.sum(cg[5].reshape(heads, HEADDIM), axis=1)
            return jnp.concatenate([cg[:5].reshape(-1), hg[0, :heads], hg[1, :heads], skip])

        gains = jnp.concatenate([to_global(gain_one_part), to_global(gain_two_part)])
        own = jnp.concatenate([small_row(saved[0]), gains])
        other = jnp.concatenate([small_row(saved[1]), gains])
        total = sum_all(own + swap(other, "tp", 2, 1), n)
        base = 5 * ch
        dt_b_total, a_total, skip_total = (total[base + heads * i : base + heads * (i + 1)] for i in range(3))
        base += 3 * heads
        return (
            layer_out,
            input_grad,
            total[base : base + width],
            jnp.concatenate([xa.out, xb.out], axis=1),
            sz.out,
            se.out[:, :heads],
            2.0 * se.out[:, heads : heads + 2 * states],
            total[: 4 * ch].reshape(4, ch),
            total[4 * ch : 5 * ch],
            dt_b_total,
            a_total,
            skip_total,
            so.out,
            total[base + width :],
            jnp.concatenate([ga.out, gb.out], axis=1),
            jnp.concatenate([ua.out, ub.out], axis=1),
            jnp.concatenate([da.out, db.out], axis=1),
        )

    return local


def solution(mesh):
    rows = P(("fsdp", "tp"), None)
    weight = P("fsdp", "tp")
    in_specs = (
        rows, P("fsdp"), P(), weight, weight, weight, P("fsdp", None), P(None, "tp"), P("tp"), P("tp"), P("tp"),
        P("tp"), weight, P(), weight, weight, weight, rows,
    )
    out_specs = (
        rows, rows, P(), weight, weight, weight, P("fsdp", None), P(None, "tp"), P("tp"), P("tp"), P("tp"), P("tp"),
        weight, P(), weight, weight, weight,
    )
    return jax.shard_map(
        make_local(mesh.shape["fsdp"]), mesh=mesh, in_specs=in_specs, out_specs=out_specs, check_vma=False
    )
```

time: 3290 us -> 1290 us (0.39)
  waiting for transfers between devices: 1600 us -> 7.75 us
  Pallas kernels: 0 us -> 1030 us
  matrix products: 769 us -> 13.7 us
  local copies, waits for them, and re-layouts: 386 us -> 38.7 us
  other arithmetic: 322 us -> 168 us
  blocking collectives: 150 us -> 0 us
    pallas_call x0 -> x33, Pallas kernels: none -> 1030 us  [the longest x28 929 us: run(): pl.pallas_call(kernel, name=name, grid=grid, in_specs=list(in_specs) + [h...]
    reduce_scatter x9 -> x0, waiting for transfers between devices: 987 us -> none  [the longest x4 378 us: share_rows(): return lax.psum_scatter(terms, 'tp', scatter_dimension=0, tiled=True)]
    dot_general x134 -> x5, matrix products: 760 us -> 13.7 us  [bf_dot(): return jnp.dot(a, b, preferred_element_type=f32)]
    all_gather x10 -> x0, waiting for transfers between devices: 469 us -> none  [the longest x4 261 us: whole_rows(): return lax.all_gather(rows, 'tp', axis=0, tiled=True)]
    unnamed x25 -> x0, waiting for transfers between devices: 143 us -> none
    reshape x21 -> x7, local copies, waits for them, and re-layouts: 129 us -> 4.52 us  [the longest x2 2.21 us: small_row(): cg[:5].reshape(-1)]
    psum x3 -> x0, blocking collectives: 109 us -> none  [the longest x1 60.8 us: local(): lax.psum((conv_w_grad, conv_b_grad, dt_b_grad, a_log_part, skip_grad), 'f...]
    convert_element_type x21 -> x67, other arithmetic: 50.3 us -> 135 us  [the longest x58 119 us: low_sum(): return (a.astype(f32) + b.astype(f32)).astype(bf16)]
  transfers between devices with their start and end apart: 22 -> 10, of which waited for: 17 -> 5; matrix products, arithmetic and copies ran while one was open for 19% -> 5% of each run, Pallas kernels for 0% -> 22%
where the time goes in v1:
time: 1290 us; the launch traced here: 1280 us
  Pallas kernels  1030 us (80%)
  other arithmetic  168 us (13%)
  local copies, waits for them, and re-layouts  38.7 us (3%)
  starting transfers between devices  15.2 us (1%)
  matrix products  13.7 us (1%)
    pallas_call x28, Pallas kernels, run(): pl.pallas_call(kernel, name=name, grid=grid, in_specs=list(in_specs) + [h...  929 us
    convert_element_type x58, other arithmetic, low_sum(): return (a.astype(f32) + b.astype(f32)).astype(bf16)  119 us
    pallas_call x5, Pallas kernels, run(): pl.pallas_call(body, name=name, grid=grid, in_specs=in_specs, out_specs=o...  102 us
  transfers between devices with their start and end apart: 10, of which 5 were waited for; matrix products, arithmetic and copies ran while one was open for 5% of the time, Pallas kernels for 22%

profile of v1, /device:TPU:0, one launch (start us, length us, event | category | flops | bytes accessed | tf_op | source)
XLA Modules:
  0.0 1276.6 jit_solution(5276546811890200068)
XLA Ops:
  28.7 35.9 %turn_rows.1 = (f32[1024,1536]{1,0:T(8,128)}, bf16[2,16,48,1536]{3,2,1,0:T(8,128)(2,1)}, bf16[2,16,48,1536]{3,2,1,0:T(8,128)(2,1)}, bf16[2,16,48,128]{3,2,1,0:T(8,128)(2,1)}, bf16[2,16,48,128]{3,2,1,0:T(8,128)(2,1)}) custom-call(bf16[1024,1536]{1,0:T(8,128)(2,1)} %refs_0_.2, bf16[1536,1536]{1,0:T(8,128)(2,1)} %fusion.1.refs_1_.refs_3_, ...), custom_call_target="tpu_custom_call" | custom-call | flops 4831838208 | bytes 6291456 | tf_op jit(solution)/shard_map/turn_rows/pallas_call | solution.py:415
  64.6 26.9 %norm_one.1 = (f32[1024,1536]{1,0:T(8,128)}, bf16[1024,1536]{1,0:T(8,128)(2,1)}, bf16[1536,1024]{1,0:T(8,128)(2,1)}, bf16[2,16,48,1536]{3,2,1,0:T(8,128)(2,1)}, ...) custom-call(f32[1024,1536]{1,0:T(8,128)} %get-tuple-element.264.refs, ...), custom_call_target="tpu_custom_call", output_to_operand_aliasing={{3}: (3, {}), {4}: (4, {}), {5}: (5, {}), {6}: (6, {})} | custom-call | flops 31457280 | bytes 18874368 | tf_op jit(solution)/shard_map/norm_one/pallas_call | solution.py:415
  91.5 35.6 %turn_cotangent.1 = (bf16[1024,1536]{1,0:T(8,128)(2,1)}, bf16[1536,1024]{1,0:T(8,128)(2,1)}, bf16[2,16,48,1536]{3,2,1,0:T(8,128)(2,1)}, bf16[2,16,48,1536]{3,2,1...) custom-call(bf16[1024,1536]{1,0:T(8,128)(2,1)} %refs_0_.3, ...), custom_call_target="tpu_custom_call", output_to_operand_aliasing={{2}: (3, {}), {3}: (4, {}), {4}: (5, {}), {5}: (6, {})} | custom-call | flops 4831838208 | bytes 6291456 | tf_op jit(solution)/shard_map/turn_cotangent/pallas_call | solution.py:415
  127.1 15.5 %carry_one.1 = (bf16[2,16,48,1536]{3,2,1,0:T(8,128)(2,1)}, bf16[2,16,48,1536]{3,2,1,0:T(8,128)(2,1)}, bf16[2,16,48,128]{3,2,1,0:T(8,128)(2,1)}, bf16[2,16,48,128...) custom-call(bf16[2,16,48,1536]{3,2,1,0:T(8,128)(2,1)} %get-tuple-ele, ...), custom_call_target="tpu_custom_call", output_to_operand_aliasing={{0}: (0, {}), {1}: (1, {}), {2}: (2, {}), {3}: (3, {}), {4}... | custom-call | tf_op jit(solution)/shard_map/carry_one/pallas_call | solution.py:415
  148.1 47.9 %project_x.1 = (f32[1024,1536]{1,0:T(8,128)}, f32[1024,1536]{1,0:T(8,128)}, bf16[2,16,48,1536]{3,2,1,0:T(8,128)(2,1)}, bf16[2,16,48,1536]{3,2,1,0:T(8,128)(2,1)}...) custom-call(bf16[1024,1536]{1,0:T(8,128)(2,1)} %get-tuple-element.27, ...), custom_call_target="tpu_custom_call", output_to_operand_aliasing={{2}: (5, {}), {3}: (6, {}), {4}: (7, {}), {5}: (8, {})} | custom-call | flops 9663676416 | bytes 12582912 | tf_op jit(solution)/shard_map/project_x/pallas_call | solution.py:415
  209.8 33.1 %conv_state0.1 = (f32[1024,1536]{1,0:T(8,128)}, f32[16,1536]{1,0:T(8,128)}, f32[1024,128]{1,0:T(8,128)}, f32[1024,128]{1,0:T(8,128)}, f32[1024,128]{1,0:T(8,128)...) custom-call(f32[1024,1536]{1,0:T(8,128)} %get-tuple-element.287.refs, ...), custom_call_target="tpu_custom_call", output_to_operand_aliasing={{5}: (8, {}), {6}: (9, {}), {7}: (10, {}), {8}: (11, {})} | custom-call | flops 7864320000 | bytes 6291456 | tf_op jit(solution)/shard_map/conv_state0/pallas_call | solution.py:415
  243.0 37.7 %conv_state1.1 = (f32[1024,1536]{1,0:T(8,128)}, f32[16,1536]{1,0:T(8,128)}, f32[1024,128]{1,0:T(8,128)}, f32[1024,128]{1,0:T(8,128)}, f32[1024,128]{1,0:T(8,128)...) custom-call(f32[1024,1536]{1,0:T(8,128)} %get-tuple-element.296.refs, ...), custom_call_target="tpu_custom_call", output_to_operand_aliasing={{5}: (8, {}), {6}: (9, {}), {7}: (10, {}), {8}: (11, {})} | custom-call | flops 7864320000 | bytes 6291456 | tf_op jit(solution)/shard_map/conv_state1/pallas_call | solution.py:415
  285.0 40.2 %project_z.1 = (f32[1024,1536]{1,0:T(8,128)}, f32[1024,1536]{1,0:T(8,128)}, bf16[2,16,48,2048]{3,2,1,0:T(8,128)(2,1)}, bf16[2,16,48,2048]{3,2,1,0:T(8,128)(2,1)}) custom-call(bf16[1024,1536]{1,0:T(8,128)(2,1)} %get-tuple-element.270.refs_0_.refs_2_, bf16[1536,1536]{1,0:T(8,128)(2,1)} %bitcast.356, ...), custom_call_target="tpu_custom_call", output_to_operand_aliasing={{2}: (4, {}), {3}: (5, {})} | custom-call | flops 9663676416 | bytes 12582912 | tf_op jit(solution)/shard_map/project_z/pallas_call | solution.py:415
  325.9 40.3 %scan_forward0.1 = (bf16[1024,1536]{1,0:T(8,128)(2,1)}, f32[1024,1536]{1,0:T(8,128)}, f32[128,1536]{1,0:T(8,128)}, bf16[2,16,48,2048]{3,2,1,0:T(8,128)(2,1)}, bf...) custom-call(f32[1024,1536]{1,0:T(8,128)} %get-tuple-element.293.refs, ...), custom_call_target="tpu_custom_call", output_to_operand_aliasing={{3}: (8, {}), {4}: (9, {}), {5}: (10, {}), {6}: (11, {}), {... | custom-call | flops 15728640000 | bytes 12582912 | tf_op jit(solution)/shard_map/scan_forward0/pallas_call | solution.py:415
  366.2 39.4 %scan_forward1.1 = (bf16[1024,1536]{1,0:T(8,128)(2,1)}, f32[1024,1536]{1,0:T(8,128)}, f32[128,1536]{1,0:T(8,128)}, bf16[2,16,48,2048]{3,2,1,0:T(8,128)(2,1)}, bf16[2,16,48,2048]{3,2,1,0:T(8,128)(2,1)}) custom-call(f32[1024,1536]{1,0:T(8,128)} %get-tuple-element.318.refs_0_, ...), custom_call_target="tpu_custom_call", output_to_operand_aliasing={{3}: (8, {}), {4}: (9, {})} | custom-call | flops 15728640000 | bytes 12582912 | tf_op jit(solution)/shard_map/scan_forward1/pallas_call | solution.py:415
  405.6 41.0 %project_out.1 = (f32[1024,1536]{1,0:T(8,128)}, bf16[2,16,48,2048]{3,2,1,0:T(8,128)(2,1)}, bf16[2,16,48,2048]{3,2,1,0:T(8,128)(2,1)}, bf16[2,16,48,2048]{3,2,1,0:T(8,128)(2,1)}, bf16[2,16,48,2048]{3,2,1,0:T(8,128)(2,1)}) custom-call(bf16[1024,1536]{1,0:T(8,128)(2,1)} %get-tuple-element.316.re, ...), custom_call_target="tpu_custom_call", output_to_operand_aliasing={{1}: (4, {}), {2}: (5, {}), {3}: (6, {}), {4}: (7, {})} | custom-call | flops 9663676416 | bytes 6291456 | tf_op jit(solution)/shard_map/project_out/pallas_call | solution.py:415
  446.6 13.1 %norm_two.1 = (f32[1024,1536]{1,0:T(8,128)}, bf16[1024,1536]{1,0:T(8,128)(2,1)}, bf16[1536,1024]{1,0:T(8,128)(2,1)}, bf16[2,16,48,2048]{3,2,1,0:T(8,128)(2,1)}, bf16[2,16,48,2048]{3,2,1,0:T(8,128)(2,1)}) custom-call(f32[1024,1536]{1,0:T(8,128)} %get-tuple-element.269.refs_0_.refs_1_, ...), custom_call_target="tpu_custom_call", output_to_operand_aliasing={{3}: (3, {}), {4}: (4, {})} | custom-call | flops 31457280 | bytes 18874368 | tf_op jit(solution)/shard_map/norm_two/pallas_call | solution.py:415
  459.7 52.8 %feed_forward.1 = (bf16[1024,2048]{1,0:T(8,128)(2,1)}, bf16[1024,2048]{1,0:T(8,128)(2,1)}, bf16[1024,2048]{1,0:T(8,128)(2,1)}, bf16[1024,2048]{1,0:T(8,128)(2,1)...) custom-call(bf16[1024,1536]{1,0:T(8,128)(2,1)} %get-tuple-element.335.n_ref, ...), custom_call_target="tpu_custom_call" | custom-call | flops 38654705664 | bytes 25165824 | tf_op jit(solution)/shard_map/feed_forward/pallas_call | solution.py:357
  512.5 20.5 %down_grad.1 = (bf16[1536,2048]{1,0:T(8,128)(2,1)}, bf16[1536,2048]{1,0:T(8,128)(2,1)}) custom-call(bf16[1536,1024]{1,0:T(8,128)(2,1)} %get-tuple-element.345.refs_0_.refs_2_, bf16[1024,2048]{1,0:T(8,128)(2,1)} %get-tuple-element.343.refs_1_.refs_0_, bf16[1536,1024]{1,0:T(8,128)(2,1)} %get-tuple-element.345.refs_0_.refs_2_, ...), custom_call_target="tpu_custom_call" | custom-call | flops 12884901888 | bytes 25165824 | tf_op jit(solution)/shard_map/down_grad/pallas_call | solution.py:357
  533.0 21.0 %gate_grad.1 = (bf16[1536,2048]{1,0:T(8,128)(2,1)}, bf16[1536,2048]{1,0:T(8,128)(2,1)}, bf16[2,8,48,1024]{3,2,1,0:T(8,128)(2,1)}, bf16[2,8,48,1024]{3,2,1,0:T(8,...) custom-call(bf16[1536,1024]{1,0:T(8,128)(2,1)} %get-tuple-element.347.refs_0_.refs_2_, ...), custom_call_target="tpu_custom_call" | custom-call | flops 12884901888 | bytes 25165824 | tf_op jit(solution)/shard_map/gate_grad/pallas_call | solution.py:415
  562.8 26.1 %up_grad.1 = (bf16[1536,2048]{1,0:T(8,128)(2,1)}, bf16[1536,2048]{1,0:T(8,128)(2,1)}, bf16[4,48,1024]{2,1,0:T(8,128)(2,1)}, bf16[4,48,1024]{2,1,0:T(8,128)(2,1)}...) custom-call(bf16[1536,1024]{1,0:T(8,128)(2,1)} %get-tuple-element.34, ...), custom_call_target="tpu_custom_call" | custom-call | flops 12884901888 | bytes 25165824 | tf_op jit(solution)/shard_map/up_grad/pallas_call | solution.py:415
  593.2 35.5 %project_down.1 = (f32[1024,1536]{1,0:T(8,128)}, bf16[4,48,1024]{2,1,0:T(8,128)(2,1)}, bf16[4,48,1024]{2,1,0:T(8,128)(2,1)}, bf16[8,48,1024]{2,1,0:T(8,128)(2,1)...) custom-call(bf16[1024,2048]{1,0:T(8,128)(2,1)} %get-tuple-element.34, ...), custom_call_target="tpu_custom_call" | custom-call | flops 12884901888 | bytes 6291456 | tf_op jit(solution)/shard_map/project_down/pallas_call | solution.py:415
  637.5 9.0 turn_out.1
  659.8 60.3 %two_back.1 = (f32[1024,1536]{1,0:T(8,128)}, bf16[4,48,1024]{2,1,0:T(8,128)(2,1)}, bf16[4,48,1024]{2,1,0:T(8,128)(2,1)}, bf16[8,48,1024]{2,1,0:T(8,128)(2,1)}, b...) custom-call(bf16[1024,2048]{1,0:T(8,128)(2,1)} %get-tuple-element.34, ...), custom_call_target="tpu_custom_call" | custom-call | flops 25769803776 | bytes 6291456 | tf_op jit(solution)/shard_map/two_back/pallas_call | solution.py:415
  727.0 21.0 %norm_two_back.1 = (bf16[1024,1536]{1,0:T(8,128)(2,1)}, bf16[1024,1536]{1,0:T(8,128)(2,1)}, f32[8,1536]{1,0:T(8,128)}, bf16[1536,1024]{1,0:T(8,128)(2,1)}, bf16[...) custom-call(f32[1024,1536]{1,0:T(8,128)} %get-tuple-element.373.refs, ...), custom_call_target="tpu_custom_call" | custom-call | flops 31457280 | bytes 25165824 | tf_op jit(solution)/shard_map/norm_two_back/pallas_call | solution.py:415
  764.3 26.2 %out_grad.1 = (bf16[1536,1536]{1,0:T(8,128)(2,1)}, bf16[1536,1536]{1,0:T(8,128)(2,1)}, bf16[4,48,1024]{2,1,0:T(8,128)(2,1)}, bf16[4,48,1024]{2,1,0:T(8,128)(2,1)...) custom-call(bf16[1536,1024]{1,0:T(8,128)(2,1)} %get-tuple-element.38, ...), custom_call_target="tpu_custom_call" | custom-call | flops 9663676416 | bytes 18874368 | tf_op jit(solution)/shard_map/out_grad/pallas_call | solution.py:415
  794.8 18.2 %gated_back.1 = (f32[1024,1536]{1,0:T(8,128)}, f32[1024,1536]{1,0:T(8,128)}, bf16[4,48,1024]{2,1,0:T(8,128)(2,1)}, bf16[4,48,1024]{2,1,0:T(8,128)(2,1)}, bf16[2,...) custom-call(bf16[1024,1536]{1,0:T(8,128)(2,1)} %get-tuple-element.379.refs_0_.refs_2_.refs_3_, ...), custom_call_target="tpu_custom_call" | custom-call | flops 9663676416 | bytes 12582912 | tf_op jit(solution)/shard_map/gated_back/pallas_call | solution.py:415
  822.8 20.9 %gate_backward0.1 = (f32[1024,1536]{1,0:T(8,128)}, bf16[1024,1536]{1,0:T(8,128)(2,1)}, f32[16,1536]{1,0:T(8,128)}, bf16[4,48,1024]{2,1,0:T(8,128)(2,1)}, bf16[4,...) custom-call(f32[1024,1536]{1,0:T(8,128)} %get-tuple-element.390.refs, ...), custom_call_target="tpu_custom_call" | custom-call | flops 7864320000 | bytes 15728640 | tf_op jit(solution)/shard_map/gate_backward0/pallas_call | solution.py:415
  846.2 13.1 %gate_backward1.1 = (f32[1024,1536]{1,0:T(8,128)}, bf16[1024,1536]{1,0:T(8,128)(2,1)}, f32[16,1536]{1,0:T(8,128)}) custom-call(f32[1024,1536]{1,0:T(8,128)} %get-tuple-element.400.gg_ref, f32[1024,1536]{1,0:T(8,128)} %get-tuple-element.319.refs_1_.z_ref, f32[1024,1536]{1,0:T(8,128)} %get-tuple-element.401.y_ref, ...), custom_call_target="tpu_custom_call" | custom-call | flops 7864320000 | bytes 15728640 | tf_op jit(solution)/shard_map/gate_backward1/pallas_call | solution.py:357
  861.6 29.6 %z_grad.1 = (bf16[1536,1536]{1,0:T(8,128)(2,1)}, bf16[1536,1536]{1,0:T(8,128)(2,1)}, bf16[4,48,1024]{2,1,0:T(8,128)(2,1)}, bf16[4,48,1024]{2,1,0:T(8,128)(2,1)},...) custom-call(bf16[1536,1024]{1,0:T(8,128)(2,1)} %get-tuple-element.40, ...), custom_call_target="tpu_custom_call" | custom-call | flops 9663676416 | bytes 18874368 | tf_op jit(solution)/shard_map/z_grad/pallas_call | solution.py:415
  900.1 52.0 %scan_backward0.1 = (bf16[1024,1536]{1,0:T(8,128)(2,1)}, f32[1024,128]{1,0:T(8,128)}, f32[8,1536]{1,0:T(8,128)}, f32[24,1536]{1,0:T(8,128)}, f32[8,128]{1,0:T(8,...) custom-call(f32[1024,1536]{1,0:T(8,128)} %get-tuple-element.293.refs, ...), custom_call_target="tpu_custom_call" | custom-call | flops 39321600000 | bytes 18874368 | tf_op jit(solution)/shard_map/scan_backward0/pallas_call | solution.py:415
  971.6 54.1 %scan_backward1.1 = (bf16[1024,1536]{1,0:T(8,128)(2,1)}, f32[1024,128]{1,0:T(8,128)}, f32[8,1536]{1,0:T(8,128)}, f32[24,1536]{1,0:T(8,128)}, f32[8,128]{1,0:T(8,...) custom-call(f32[1024,1536]{1,0:T(8,128)} %get-tuple-element.318.refs, ...), custom_call_target="tpu_custom_call" | custom-call | flops 39321600000 | bytes 18874368 | tf_op jit(solution)/shard_map/scan_backward1/pallas_call | solution.py:415
  1049.6 30.1 %x_grad.1 = (bf16[1536,1536]{1,0:T(8,128)(2,1)}, bf16[1536,1536]{1,0:T(8,128)(2,1)}, bf16[4,48,1536]{2,1,0:T(8,128)(2,1)}, bf16[4,48,1536]{2,1,0:T(8,128)(2,1)},...) custom-call(bf16[1536,1024]{1,0:T(8,128)(2,1)} %get-tuple-element.406.refs_0_.refs_2_, ...), custom_call_target="tpu_custom_call" | custom-call | flops 9663676416 | bytes 18874368 | tf_op jit(solution)/shard_map/x_grad/pallas_call | solution.py:415
  1082.1 33.7 %x_back.1 = (f32[1024,1536]{1,0:T(8,128)}, bf16[2,8,48,768]{3,2,1,0:T(8,128)(2,1)}, bf16[2,8,48,768]{3,2,1,0:T(8,128)(2,1)}, bf16[2,8,48,768]{3,2,1,0:T(8,128)(2...) custom-call(bf16[1024,1536]{1,0:T(8,128)(2,1)} %get-tuple-element.56, ...), custom_call_target="tpu_custom_call" | custom-call | flops 10468982784 | bytes 6291456 | tf_op jit(solution)/shard_map/x_back/pallas_call | solution.py:415
  1125.8 34.6 %z_back.1 = (f32[1024,1536]{1,0:T(8,128)}, bf16[4,48,768]{2,1,0:T(8,128)(2,1)}, bf16[4,48,768]{2,1,0:T(8,128)(2,1)}, bf16[8,48,768]{2,1,0:T(8,128)(2,1)}, bf16[4...) custom-call(bf16[1024,1536]{1,0:T(8,128)(2,1)} %get-tuple-element.40, ...), custom_call_target="tpu_custom_call" | custom-call | flops 9663676416 | bytes 6291456 | tf_op jit(solution)/shard_map/z_back/pallas_call | solution.py:415
  1177.3 17.6 %norm_one_back.1 = (bf16[1024,1536]{1,0:T(8,128)(2,1)}, bf16[1024,1536]{1,0:T(8,128)(2,1)}, f32[8,1536]{1,0:T(8,128)}, bf16[1536,1024]{1,0:T(8,128)(2,1)}, bf16[...) custom-call(f32[1024,1536]{1,0:T(8,128)} %add.708.refs_0_, ...), custom_call_target="tpu_custom_call" | custom-call | flops 31457280 | bytes 25165824 | tf_op jit(solution)/shard_map/norm_one_back/pallas_call | solution.py:415
  1210.6 41.4 %turn_back.1 = (f32[1024,1536]{1,0:T(8,128)}, bf16[2,48,768]{2,1,0:T(8,128)(2,1)}, bf16[2,48,768]{2,1,0:T(8,128)(2,1)}, bf16[2,48,768]{2,1,0:T(8,128)(2,1)}, bf1...) custom-call(bf16[1024,1536]{1,0:T(8,128)(2,1)} %get-tuple-element.45, ...), custom_call_target="tpu_custom_call" | custom-call | flops 9663676416 | bytes 6291456 | tf_op jit(solution)/shard_map/turn_back/pallas_call | solution.py:415
  (510 shorter events, 249.0 us)
Async XLA Ops:
  1.5 198.6 %collective-permute-start = (bf16[16,1536]{1,0:T(8,128)(2,1)S(1)}, bf16[16,1536]{1,0:T(8,128)(2,1)S(1)}, u32[]{:S(2)}, u32[]{:S(2)}) collective-permute-start(bf16[16,1536]{1,0:T(8,128)(2,1)S(1)} %slice.439), channel_id=1, source_target_pairs={{0,1},{2,3},{4,5},{6,7},{8,9},{10,11},{12,13},{14,15},{16,17},{18,... | collective-permute-start | bytes 147464 | tf_op jit(solution)/shard_map/ppermute | solution.py:852
  10.0 199.3 %collective-permute-start.1 = (f32[8,1536]{1,0:T(8,128)S(1)}, f32[8,1536]{1,0:T(8,128)S(1)}, u32[]{:S(2)}, u32[]{:S(2)}) collective-permute-start(f32[8,1536]{1,0:T(8,128)S(1)} %select_maximum_fusion.refs_3_.refs_7_.refs_5_), channel_id=1, source_target_pairs={{0,1},{1,0},{2,3},{3,2},{4,5},{5,4},{6,7},{7,6},{8,9},{9,8},{10,11... | collective-permute-start | bytes 147464 | tf_op jit(solution)/shard_map/ppermute | solution.py:807
  243.0 37.7 %copy-start.104 = (f32[16,1536]{1,0:T(8,128)S(1)}, f32[16,1536]{1,0:T(8,128)}, u32[]{:S(2)}) copy-start(f32[16,1536]{1,0:T(8,128)} %get-tuple-element.308) | copy-start | bytes 294916
  281.6 43.6 %collective-permute-start.2 = (f32[2,16,1536]{2,1,0:T(8,128)S(1)}, f32[2,16,1536]{2,1,0:T(8,128)S(1)}, u32[]{:S(2)}, u32[]{:S(2)}) collective-permute-start(f32[2,16,1536]{2,1,0:T(8,128)S(1)} %pad_maximum_fusion.5), channel_id=1, source_target_pairs={{0,1},{2,3},{4,5},{6,7},{8,9},{10,11},{12,13},{14,15},{16,17},{18,... | collective-permute-start | bytes 589832 | tf_op jit(solution)/shard_map/ppermute | solution.py:893
  593.2 38.8 %slice-start.2 = ((s8[6291456]{0:T(1024)(128)(4,1)}), s8[4194304]{0:T(1024)(128)(4,1)S(1)}, s32[]{:S(2)}) async-start(s8[6291456]{0:T(1024)(128)(4,1)} %bitcast.354), calls=%async_computation.2 | async-start | bytes 8388608
  593.2 35.5 %copy-start.6 = (bf16[8,48,1024]{2,1,0:T(8,128)(2,1)S(1)}, bf16[8,48,1024]{2,1,0:T(8,128)(2,1)}, u32[]{:S(2)}) copy-start(bf16[8,48,1024]{2,1,0:T(8,128)(2,1)} %fusion.11.refs_7_) | copy-start | bytes 2359300
  593.2 38.8 %slice-start.3 = ((s8[6291456]{0:T(1024)(128)(4,1)}), s8[2097152]{0:T(1024)(128)(4,1)S(1)}, s32[]{:S(2)}) async-start(s8[6291456]{0:T(1024)(128)(4,1)} %bitcast.354), calls=%async_computation.3 | async-start | bytes 4194304
  659.8 62.5 %copy-start.24 = (bf16[8,48,1024]{2,1,0:T(8,128)(2,1)S(1)}, bf16[8,48,1024]{2,1,0:T(8,128)(2,1)}, u32[]{:S(2)}) copy-start(bf16[8,48,1024]{2,1,0:T(8,128)(2,1)} %fusion.10.refs_13_) | copy-start | bytes 2359300
  860.3 39.2 %collective-permute-start.3 = (f32[2,16,1536]{2,1,0:T(8,128)S(1)}, f32[2,16,1536]{2,1,0:T(8,128)S(1)}, u32[]{:S(2)}, u32[]{:S(2)}) collective-permute-start(f32[2,16,1536]{2,1,0:T(8,128)S(1)} %pad_maximum_fusion.6), channel_id=1, source_target_pairs={{1,0},{3,2},{5,4},{7,6},{9,8},{11,10},{13,12},{15,14},{17,16},{19,... | collective-permute-start | bytes 589832 | tf_op jit(solution)/shard_map/ppermute | solution.py:931
  900.1 55.7 %slice-start.8 = ((s8[4718592]{0:T(1024)(128)(4,1)}), s8[4194304]{0:T(1024)(128)(4,1)S(1)}, s32[]{:S(2)}) async-start(s8[4718592]{0:T(1024)(128)(4,1)} %bitcast.395), calls=%async_computation.8 | async-start | bytes 8388608
  900.1 52.0 %copy-start.22 = (bf16[8,48,1024]{2,1,0:T(8,128)(2,1)S(1)}, bf16[8,48,1024]{2,1,0:T(8,128)(2,1)}, u32[]{:S(2)}) copy-start(bf16[8,48,1024]{2,1,0:T(8,128)(2,1)} %fusion.6.refs_20_) | copy-start | bytes 2359300
  900.1 55.7 %slice-start.9 = ((s8[4718592]{0:T(1024)(128)(4,1)}), s8[524288]{0:T(1024)(128)(4,1)S(1)}, s32[]{:S(2)}) async-start(s8[4718592]{0:T(1024)(128)(4,1)} %bitcast.395), calls=%async_computation.9 | async-start | bytes 1048576
  971.6 54.1 %copy-start.16 = (bf16[8,48,1536]{2,1,0:T(8,128)(2,1)S(1)}, bf16[8,48,1536]{2,1,0:T(8,128)(2,1)}, u32[]{:S(2)}) copy-start(bf16[8,48,1536]{2,1,0:T(8,128)(2,1)} %fusion.4.refs_20_) | copy-start | bytes 3538948
  1035.9 11.0 collective-permute-start.4
  1081.1 42.6 %slice-start.10 = ((s8[4718592]{0:T(1024)(128)(4,1)}), s8[524288]{0:T(1024)(128)(4,1)S(1)}, s32[]{:S(2)}) async-start(s8[4718592]{0:T(1024)(128)(4,1)} %bitcast.400), calls=%async_computation.10 | async-start | bytes 1048576
  1082.1 41.6 %slice-start.11 = ((s8[4718592]{0:T(1024)(128)(4,1)}), s8[4194304]{0:T(1024)(128)(4,1)S(1)}, s32[]{:S(2)}) async-start(s8[4718592]{0:T(1024)(128)(4,1)} %bitcast.400), calls=%async_computation.11 | async-start | bytes 8388608
  1125.7 44.6 %slice-start.4 = ((s8[6291456]{0:T(1024)(128)(4,1)}), s8[4194304]{0:T(1024)(128)(4,1)S(1)}, s32[]{:S(2)}) async-start(s8[6291456]{0:T(1024)(128)(4,1)} %bitcast.364), calls=%async_computation.4 | async-start | bytes 8388608
  1125.7 39.9 %copy-start.59 = (bf16[2,8,48,128]{3,2,1,0:T(8,128)(2,1)S(1)}, bf16[2,8,48,128]{3,2,1,0:T(8,128)(2,1)}, u32[]{:S(2)}) copy-start(bf16[2,8,48,128]{3,2,1,0:T(8,128)(2,1)} %add_convert_fusion.42.refs_8_) | copy-start | bytes 589828
  1125.7 44.6 %slice-start.5 = ((s8[6291456]{0:T(1024)(128)(4,1)}), s8[2097152]{0:T(1024)(128)(4,1)S(1)}, s32[]{:S(2)}) async-start(s8[6291456]{0:T(1024)(128)(4,1)} %bitcast.364), calls=%async_computation.5 | async-start | bytes 4194304
  1203.9 49.5 %collective-permute-start.5 = (f32[10824]{0:T(1024)}, f32[10824]{0:T(1024)S(1)}, u32[]{:S(2)}, u32[]{:S(2)}) collective-permute-start(f32[10824]{0:T(1024)} %concatenate.54), channel_id=1, source_target_pairs={{0,1},{1,0},{2,3},{3,2},{4,5},{5,4},{6,7},{7,6},{8,9},{9,8},{10,11... | collective-permute-start | bytes 129896 | tf_op jit(solution)/shard_map/ppermute | solution.py:807
  1210.6 41.5 %slice-start.27 = ((bf16[4,48,768]{2,1,0:T(8,128)(2,1)}), bf16[1,48,768]{2,1,0:T(8,128)(2,1)S(1)}, s32[]{:S(2)}) async-start(bf16[4,48,768]{2,1,0:T(8,128)(2,1)} %copy-done.65), calls=%async_computation.27 | async-start | bytes 147456 | tf_op jit(solution)/shard_map/slice | solution.py:629
  1210.6 41.5 %slice-start.28 = ((bf16[4,48,768]{2,1,0:T(8,128)(2,1)}), bf16[1,48,768]{2,1,0:T(8,128)(2,1)S(1)}, s32[]{:S(2)}) async-start(bf16[4,48,768]{2,1,0:T(8,128)(2,1)} %copy-done.66), calls=%async_computation.28 | async-start | bytes 147456 | tf_op jit(solution)/shard_map/slice | solution.py:629
  1210.6 42.6 %copy-start.101 = (f32[7680]{0:T(1024)S(1)}, f32[7680]{0:T(1024)}, u32[]{:S(2)}) copy-start(f32[7680]{0:T(1024)} %reshape.671) | copy-start | bytes 92164
  1210.6 42.6 %copy-start.111 = (f32[24]{0:T(128)S(1)}, f32[24]{0:T(128)}, u32[]{:S(2)}) copy-start(f32[24]{0:T(128)} %get-tuple-element.553) | copy-start | bytes 292
  1210.6 42.6 %copy-start.112 = (f32[24]{0:T(128)S(1)}, f32[24]{0:T(128)}, u32[]{:S(2)}) copy-start(f32[24]{0:T(128)} %get-tuple-element.554) | copy-start | bytes 292
  1210.6 42.6 %copy-start.115 = (f32[24]{0:T(128)S(1)}, f32[24]{0:T(128)}, u32[]{:S(2)}) copy-start(f32[24]{0:T(128)} %reduce_sum.28) | copy-start | bytes 292
  1210.6 42.8 %slice-start.26 = ((bf16[4,48,768]{2,1,0:T(8,128)(2,1)}), bf16[1,48,768]{2,1,0:T(8,128)(2,1)S(1)}, s32[]{:S(2)}) async-start(bf16[4,48,768]{2,1,0:T(8,128)(2,1)} %add_convert_fusion.37.refs_7_), calls=%async_computation.26 | async-start | bytes 147456 | tf_op jit(solution)/shard_map/slice | solution.py:629
  1210.6 42.8 %slice-start.29 = ((bf16[4,48,768]{2,1,0:T(8,128)(2,1)}), bf16[1,48,768]{2,1,0:T(8,128)(2,1)S(1)}, s32[]{:S(2)}) async-start(bf16[4,48,768]{2,1,0:T(8,128)(2,1)} %add_convert_fusion.38.refs_6_), calls=%async_computation.29 | async-start | bytes 147456 | tf_op jit(solution)/shard_map/slice | solution.py:629
  1253.4 1.3 collective-permute-start.6
  1254.7 4.1 collective-permute-start.7
  1258.8 4.1 collective-permute-start.8
  1262.9 5.5 collective-permute-start.9
  (129 other events, 1046.5 us)

commit v2 on v1

--- a/solution.py
+++ b/solution.py
@@ -1,3 +1,5 @@
+import functools
+
 import jax
 import jax.numpy as jnp
 from jax import lax
@@ -107,16 +109,16 @@
     row_ref[...] = col.T
     et = e.T
     et_ref[...] = et
-    bt = et[COLB:COLC, :].astype(bf16)
+    bt = wide_left(et[COLB:COLC, :])
     left = lane < HEADDIM
     for j in range(x_ref.shape[1] // 128):
         lanes = slice(128 * j, 128 * j + 128)
         _, _, acc = conv_rows(x_ref, xp_ref, halo_ref, cw_ref, col, q, lanes)
         u = acc * sigmoid(acc)
         u_ref[:, lanes] = u
-        scaled = (u * (pair_cols(col, DT, j, left) * pair_cols(col, TAIL, j, left))).astype(bf16)
+        scaled = u * (pair_cols(col, DT, j, left) * pair_cols(col, TAIL, j, left))
         keep = pair_cols(col[Q - 1 : Q, :], DEC, j, left[:1])
-        end_ref[:, lanes] = keep * end_ref[:, lanes] + dot(bt, scaled)
+        end_ref[:, lanes] = keep * end_ref[:, lanes] + dot(bt, stack_right(scaled))
 
 
 def scan_kernel(
@@ -132,27 +134,30 @@
     bt = et_ref[COLB:COLC, :]
     scores = dot(c, bt, highest)
     neg = jnp.where((col[:, SEG : SEG + 1] == row[SEG : SEG + 1, :]) & triangle(), 0.0, NEG)
-    c, bt = wide_left(c), bt.astype(bf16)
+    c, bt = wide_left(c), wide_left(bt)
     for j in range(u_ref.shape[1] // 128):
         lanes = slice(128 * j, 128 * j + 128)
         uf = u_ref[:, lanes]
-        u = uf.astype(bf16)
+        u, u_low = split(uf)
         state = S[:, lanes]
         st_ref[:, lanes] = state
-        parts = []
+        parts, rest = [], []
         for h in (2 * j, 2 * j + 1):
             gap = col[:, h : h + 1] - (row[h : h + 1, :] - row[LOGDT + h : LOGDT + h + 1, :])
-            parts.append((jnp.exp(gap + neg) * scores).astype(bf16))
+            high, low = split(jnp.exp(gap + neg) * scores)
+            parts.append(high)
+            rest.append(low)
         zero = jnp.zeros_like(u)
-        both = jnp.concatenate([jnp.where(left, u, zero), jnp.where(left, zero, u)], axis=0)
-        y = dot(jnp.concatenate(parts, axis=1), both)
+        both = [jnp.where(left, u, zero), jnp.where(left, zero, u)]
+        both_low = [jnp.where(left, u_low, zero), jnp.where(left, zero, u_low)]
+        y = dot(jnp.concatenate(parts + rest + parts, axis=1), jnp.concatenate(both + both + both_low, axis=0))
         y = y + dot(c, stack_right(state)) * pair_cols(col, DEC, j, left) + cw_ref[5:6, lanes] * uf
         z = z_ref[:, lanes]
         y_ref[:, lanes] = y
         gated_ref[:, lanes] = (y * (z * sigmoid(z))).astype(bf16)
-        scaled = (uf * (pair_cols(col, DT, j, left) * pair_cols(col, TAIL, j, left))).astype(bf16)
+        scaled = uf * (pair_cols(col, DT, j, left) * pair_cols(col, TAIL, j, left))
         keep = pair_cols(col[Q - 1 : Q, :], DEC, j, left[:1])
-        S[:, lanes] = keep * state + dot(bt, scaled)
+        S[:, lanes] = keep * state + dot(bt, stack_right(scaled))
 
 
 def gate_back_kernel(gg_ref, z_ref, y_ref, col_ref, et_ref, dy_ref, dz_ref, ds_ref):
@@ -302,20 +307,22 @@
     turned_ref[...] = normed.T.astype(bf16)
 
 
-def norm_back_kernel(grad_ref, rows_ref, gain_ref, *refs):
-    *base_refs, high_ref, low_ref, part_ref, turned_ref = refs
+def norm_back_kernel(n_grads, rows_ref, gain_ref, *refs):
+    *given, high_ref, low_ref, part_ref, turned_ref = refs
 
     @pl.when(pl.program_id(0) == 0)
     def _():
         part_ref[...] = jnp.zeros_like(part_ref)
 
-    rows, grad = rows_ref[...], grad_ref[...]
+    rows, grad = rows_ref[...], given[0][...]
+    for r in given[1:n_grads]:
+        grad = grad + r[...]
     scale = lax.rsqrt(jnp.mean(rows * rows, axis=-1, keepdims=True) + epsilon)
     unit = rows * scale
     part_ref[0:1, :] += jnp.sum(grad * unit, axis=0, keepdims=True)
     unit_grad = grad * gain_ref[...]
     total = scale * (unit_grad - unit * jnp.mean(unit_grad * unit, axis=-1, keepdims=True))
-    for r in base_refs:
+    for r in given[n_grads:]:
         total = total + r[...].astype(f32)
     high = total.astype(bf16)
     high_ref[...] = high
@@ -767,20 +774,20 @@
     )
 
 
-def norm_back(grad, rows, gain_row, bases, name, load=None):
+def norm_back(grads, rows, gain_row, bases, name, load=None):
     tokens, width = rows.shape
     main, turned, one = norm_specs(width)
     high, low, part, high_t = run(
-        norm_back_kernel,
+        functools.partial(norm_back_kernel, len(grads)),
         (tokens // Q,),
-        [main, main, one] + [main] * len(bases),
+        [main, one] + [main] * (len(grads) + len(bases)),
         [main, main, pl.BlockSpec((8, width), lambda q: (0, 0)), turned],
         [
             shape((tokens, width), bf16), shape((tokens, width), bf16), shape((8, width), f32),
             shape((width, tokens), bf16),
         ],
         [],
-        [grad, rows, gain_row, *bases],
+        [rows, gain_row, *grads, *bases],
         name,
         cost(tokens * width * 20, 16 * tokens * width),
         load,
@@ -807,7 +814,9 @@
     return lax.ppermute(x, axis, [(i, i ^ mask) for i in range(n)])
 
 
-def sum_all(x, n):
+def sum_all(x, n, over_tp=False):
+    if over_tp:
+        x = x + swap(x, "tp", 2, 1)
     bit = 1
     while bit < n:
         x = x + swap(x, "fsdp", n, bit)
@@ -885,24 +894,24 @@
             v = dict(x=xs[b], cw=smalls[b], hp=head_rows[b])
             v["e"] = bf_dot(normed, E.full[b])
             v["halo"] = bf_dot(normed_before, X.full[b])
-            load = Load(Z, O, U) if b == 0 else Load(G, O, D)
+            load = Load(Z, O, G, U) if b == 0 else Load(G, O, D)
             v["u"], v["end"], v["col"], v["row"], v["et"] = conv_state(
                 v["x"], v["halo"], v["cw"], v["e"], v["hp"], marks, tag=str(b), load=load
             )
             saved.append(v)
         starts = lax.ppermute(jnp.stack([v["end"] for v in saved]), "tp", [(0, 1)])[::-1]
-        zs = matmul([[(normed, w)] for w in Z.full], f32, 512, "project_z", Load(G))
+        zs = matmul([[(normed, w)] for w in Z.full], f32, 512, "project_z", Load(G, U, D))
         for b in (0, 1):
             v = saved[b]
             v["z"] = zs[b]
             v["gated"], v["y"], v["states"] = scan_forward(
                 v["u"], v["z"], v["col"], v["row"], v["e"], v["et"], starts[b], v["cw"],
-                tag=str(b), load=Load(G, U, D) if b == 0 else Load(U),
+                tag=str(b), load=Load(U) if b == 0 else Load(U, D),
             )
         (mixed,) = matmul(
-            [[(v["gated"], w) for v, w in zip(saved, O.full)]], f32, 512, "project_out", Load(U, D), nt=True
+            [[(v["gated"], w) for v, w in zip(saved, O.full)]], f32, 512, "project_out", Load(D), nt=True
         )
-        hidden, normed_two, two_t = norm_forward([rows_in, mixed], gain_two, "norm_two", Load(D))
+        hidden, normed_two, two_t = norm_forward([rows_in, mixed], gain_two, "norm_two")
 
         acts, gate_grads, up_grads = feed_forward(normed_two, cot_low, G.full, U.full, D.full)
         def halves(key, grads):
@@ -912,13 +921,13 @@
         ga, gb = halves("g", matmul([[(two_t, a)] for a in gate_grads], bf16, 512, "gate_grad", Load(da, db)))
         ua, ub = halves("u", matmul([[(two_t, a)] for a in up_grads], bf16, 512, "up_grad", Load(da, ga, gb)))
         (fed,) = matmul([list(zip(acts, D.full))], f32, 512, "project_down", Load(db, da, ua, ub), nt=True)
-        layer_out = matmul([[((hidden + fed).astype(bf16), turn)]], bf16, 512, "turn_out", nt=True)[0]
+        out_low = (hidden + fed).astype(bf16)
         (grad_two,) = matmul(
             [list(zip(gate_grads, G.full)) + list(zip(up_grads, U.full))], f32, 256, "two_back",
             Load(ga, gb, db, da), nt=True,
         )
         mixed_grad, mixed_low, mixed_t, gain_two_part = norm_back(
-            grad_two, hidden, gain_two, [cot_low], "norm_two_back", Load(ga, db)
+            [grad_two], hidden, gain_two, [cot_low], "norm_two_back", Load(ga, db)
         )
 
         so = Scatter("o", matmul([[(mixed_t, v["gated"])] for v in saved], bf16, 512, "out_grad", Load(ua, ga)), n)
@@ -929,14 +938,22 @@
                 gg[b], v["z"], v["y"], v["col"], v["et"], tag=str(b), load=Load(ua, gb) if b == 0 else None
             )
         ends = lax.ppermute(jnp.stack([v["ds"] for v in saved]), "tp", [(1, 0)])[::-1]
-        sz = Scatter("z", matmul([[(normed_t, v["dz"])] for v in saved], bf16, 512, "z_grad", Load(ub, ua)), n)
+        sz = Scatter("z", matmul([[(normed_t, v["dz"])] for v in saved], bf16, 512, "z_grad", Load(ua)), n)
+        (grad_z,) = matmul([[(v["dz"], w) for v, w in zip(saved, Z.full)]], f32, 512, "z_back", Load(sz), nt=True)
         for b in (0, 1):
             v = saved[b]
             v["dx"], v["de"], v["cg"], v["edge"], v["hg"] = scan_backward(
                 v["u"], v["dy"], v["x"], v["halo"], v["cw"], v["col"], v["row"], v["e"], v["et"], v["states"],
-                ends[b], v["hp"], tag=str(b), load=Load(sz, so, ub) if b else Load(so, ub, sz),
+                ends[b], v["hp"], tag=str(b), load=Load(ub, so, sz) if b else Load(ub, so),
             )
         edges = lax.ppermute(jnp.stack([v["edge"] for v in saved]), "tp", [(1, 0)])[::-1]
+        own, other = ([v["cg"][:6].reshape(-1), v["hg"][:2].reshape(-1)] for v in saved)
+        gain_two_part = to_global(gain_two_part)
+        own, other = jnp.concatenate(own + [gain_two_part]), jnp.concatenate(other + [gain_two_part])
+        total = sum_all(own + swap(other, "tp", 2, 1), n)
+        cg, hg = total[: 6 * ch].reshape(6, ch), total[6 * ch : 6 * ch + 256].reshape(2, 128)
+        gain_two_total = total[6 * ch + 256 :]
+
         shared = 0.5 * (saved[0]["de"] + saved[1]["de"])
         own_lane = jnp.arange(EXTRA)[None, :] < heads
         for b in (0, 1):
@@ -948,43 +965,34 @@
             last = v["dx"][tokens - HALO :].astype(f32) + jnp.concatenate(fix, axis=0)
             v["dx"] = lax.dynamic_update_slice(v["dx"], last.astype(bf16), (tokens - HALO, 0))
             v["de"] = jnp.where(own_lane, v["de"], shared).astype(bf16)
-        xa, xb = halves("x", matmul([[(normed_t, v["dx"])] for v in saved], bf16, 512, "x_grad", Load(sz, so)))
+        sx = Scatter("x", matmul([[(normed_t, v["dx"])] for v in saved], bf16, 512, "x_grad", Load(sz, ub)), n)
         se = Scatter("e", matmul([[(normed_t, v["de"])] for v in saved], bf16, 128, "e_grad"), n)
         pairs = [(v["dx"], w) for v, w in zip(saved, X.full)] + [(v["de"], w) for v, w in zip(saved, E.full)]
-        (grad_x,) = matmul([pairs], f32, 512, "x_back", Load(xa, xb, se, sz), nt=True)
-        (grad_z,) = matmul([[(v["dz"], w) for v, w in zip(saved, Z.full)]], f32, 512, "z_back", Load(xa, xb, se), nt=True)
+        (grad_x,) = matmul([pairs], f32, 512, "x_back", Load(sx, se, so), nt=True)
         high, low, _, gain_one_part = norm_back(
-            grad_x + grad_z, rows_in, gain_one, [mixed_grad, mixed_low], "norm_one_back", Load(xa, xb, se)
+            [grad_x, grad_z], rows_in, gain_one, [mixed_grad, mixed_low], "norm_one_back", Load(sx, se, sz)
         )
-        (input_grad,) = matmul([[(high, turn), (low, turn)]], f32, 512, "turn_back", Load(xa, xb, se), nt=True)
-
-        def small_row(v):
-            cg, hg = v["cg"], v["hg"]
-            skip = jnp.sum(cg[5].reshape(heads, HEADDIM), axis=1)
-            return jnp.concatenate([cg[:5].reshape(-1), hg[0, :heads], hg[1, :heads], skip])
-
-        gains = jnp.concatenate([to_global(gain_one_part), to_global(gain_two_part)])
-        own = jnp.concatenate([small_row(saved[0]), gains])
-        other = jnp.concatenate([small_row(saved[1]), gains])
-        total = sum_all(own + swap(other, "tp", 2, 1), n)
-        base = 5 * ch
-        dt_b_total, a_total, skip_total = (total[base + heads * i : base + heads * (i + 1)] for i in range(3))
-        base += 3 * heads
+        (layer_out,) = matmul([[(out_low, turn)]], bf16, 512, "turn_out", Load(sx, se), nt=True)
+        (input_grad,) = matmul([[(high, turn), (low, turn)]], f32, 512, "turn_back", Load(sx, se), nt=True)
+
+        gain_one_total = sum_all(to_global(gain_one_part), n, True)
+        dt_b_total, a_total = hg[0, :heads], hg[1, :heads]
+        skip_total = jnp.sum(cg[5].reshape(heads, HEADDIM), axis=1)
         return (
             layer_out,
             input_grad,
-            total[base : base + width],
-            jnp.concatenate([xa.out, xb.out], axis=1),
+            gain_one_total,
+            sx.out,
             sz.out,
             se.out[:, :heads],
             2.0 * se.out[:, heads : heads + 2 * states],
-            total[: 4 * ch].reshape(4, ch),
-            total[4 * ch : 5 * ch],
+            cg[:4],
+            cg[4],
             dt_b_total,
             a_total,
             skip_total,
             so.out,
-            total[base + width :],
+            gain_two_total,
             jnp.concatenate([ga.out, gb.out], axis=1),
             jnp.concatenate([ua.out, ub.out], axis=1),
             jnp.concatenate([da.out, db.out], axis=1),

time: 1290 us -> 1280 us (level)
    convert_element_type x58 -> x54, other arithmetic: 119 us -> 115 us  [low_sum(): return (a.astype(f32) + b.astype(f32)).astype(bf16)]
  transfers between devices with their start and end apart: 10 -> 15, of which waited for: 5 -> 5; matrix products, arithmetic and copies ran while one was open for 5% -> 6% of each run, Pallas kernels for 22% -> 25%
where the time goes in v2:
time: 1280 us; the launch traced here: 1270 us
  Pallas kernels  1040 us (81%)
  other arithmetic  156 us (12%)
  local copies, waits for them, and re-layouts  36.4 us (3%)
  starting transfers between devices  19.3 us (2%)
  matrix products  13.7 us (1%)
    pallas_call x28, Pallas kernels, run(): pl.pallas_call(kernel, name=name, grid=grid, in_specs=list(in_specs) + [h...  933 us
    convert_element_type x54, other arithmetic, low_sum(): return (a.astype(f32) + b.astype(f32)).astype(bf16)  115 us
    pallas_call x5, Pallas kernels, run(): pl.pallas_call(body, name=name, grid=grid, in_specs=in_specs, out_specs=o...  104 us
  transfers between devices with their start and end apart: 15, of which 5 were waited for; matrix products, arithmetic and copies ran while one was open for 6% of the time, Pallas kernels for 25%

profile of v2, /device:TPU:0, one launch (start us, length us, event | category | flops | bytes accessed | tf_op | source)
XLA Modules:
  0.0 1270.1 jit_solution(7547652003709929322)
XLA Ops:
  28.7 35.9 %turn_rows.1 = (f32[1024,1536]{1,0:T(8,128)}, bf16[2,16,48,1536]{3,2,1,0:T(8,128)(2,1)}, bf16[2,16,48,1536]{3,2,1,0:T(8,128)(2,1)}, bf16[2,16,48,128]{3,2,1,0:T(8,128)(2,1)}, bf16[2,16,48,128]{3,2,1,0:T(8,128)(2,1)}) custom-call(bf16[1024,1536]{1,0:T(8,128)(2,1)} %refs_0_.2, bf16[1536,1536]{1,0:T(8,128)(2,1)} %fusion.1.refs_1_.refs_3_, ...), custom_call_target="tpu_custom_call" | custom-call | flops 4831838208 | bytes 6291456 | tf_op jit(solution)/shard_map/turn_rows/pallas_call | solution.py:422
  64.6 26.9 %norm_one.1 = (f32[1024,1536]{1,0:T(8,128)}, bf16[1024,1536]{1,0:T(8,128)(2,1)}, bf16[1536,1024]{1,0:T(8,128)(2,1)}, bf16[2,16,48,1536]{3,2,1,0:T(8,128)(2,1)}, ...) custom-call(f32[1024,1536]{1,0:T(8,128)} %get-tuple-element.255.refs, ...), custom_call_target="tpu_custom_call", output_to_operand_aliasing={{3}: (3, {}), {4}: (4, {}), {5}: (5, {}), {6}: (6, {})} | custom-call | flops 31457280 | bytes 18874368 | tf_op jit(solution)/shard_map/norm_one/pallas_call | solution.py:422
  91.5 35.7 %turn_cotangent.1 = (bf16[1024,1536]{1,0:T(8,128)(2,1)}, bf16[1536,1024]{1,0:T(8,128)(2,1)}, bf16[2,16,48,1536]{3,2,1,0:T(8,128)(2,1)}, bf16[2,16,48,1536]{3,2,1...) custom-call(bf16[1024,1536]{1,0:T(8,128)(2,1)} %refs_0_.3, ...), custom_call_target="tpu_custom_call", output_to_operand_aliasing={{2}: (3, {}), {3}: (4, {}), {4}: (5, {}), {5}: (6, {})} | custom-call | flops 4831838208 | bytes 6291456 | tf_op jit(solution)/shard_map/turn_cotangent/pallas_call | solution.py:422
  127.2 15.5 %carry_one.1 = (bf16[2,16,48,1536]{3,2,1,0:T(8,128)(2,1)}, bf16[2,16,48,1536]{3,2,1,0:T(8,128)(2,1)}, bf16[2,16,48,128]{3,2,1,0:T(8,128)(2,1)}, bf16[2,16,48,128...) custom-call(bf16[2,16,48,1536]{3,2,1,0:T(8,128)(2,1)} %get-tuple-ele, ...), custom_call_target="tpu_custom_call", output_to_operand_aliasing={{0}: (0, {}), {1}: (1, {}), {2}: (2, {}), {3}: (3, {}), {4}... | custom-call | tf_op jit(solution)/shard_map/carry_one/pallas_call | solution.py:422
  148.2 47.8 %project_x.1 = (f32[1024,1536]{1,0:T(8,128)}, f32[1024,1536]{1,0:T(8,128)}, bf16[2,16,48,1536]{3,2,1,0:T(8,128)(2,1)}, bf16[2,16,48,1536]{3,2,1,0:T(8,128)(2,1)}...) custom-call(bf16[1024,1536]{1,0:T(8,128)(2,1)} %get-tuple-element.26, ...), custom_call_target="tpu_custom_call", output_to_operand_aliasing={{2}: (5, {}), {3}: (6, {}), {4}: (7, {}), {5}: (8, {})} | custom-call | flops 9663676416 | bytes 12582912 | tf_op jit(solution)/shard_map/project_x/pallas_call | solution.py:422
  209.8 46.8 %conv_state0.1 = (f32[1024,1536]{1,0:T(8,128)}, f32[16,1536]{1,0:T(8,128)}, f32[1024,128]{1,0:T(8,128)}, f32[1024,128]{1,0:T(8,128)}, f32[1024,128]{1,0:T(8,128)...) custom-call(f32[1024,1536]{1,0:T(8,128)} %get-tuple-element.278.refs, ...), custom_call_target="tpu_custom_call", output_to_operand_aliasing={{5}: (8, {}), {6}: (9, {}), {7}: (10, {}), {8}: (11, {}), {... | custom-call | flops 7864320000 | bytes 6291456 | tf_op jit(solution)/shard_map/conv_state0/pallas_call | solution.py:422
  256.6 40.1 %conv_state1.1 = (f32[1024,1536]{1,0:T(8,128)}, f32[16,1536]{1,0:T(8,128)}, f32[1024,128]{1,0:T(8,128)}, f32[1024,128]{1,0:T(8,128)}, f32[1024,128]{1,0:T(8,128)...) custom-call(f32[1024,1536]{1,0:T(8,128)} %get-tuple-element.289.refs, ...), custom_call_target="tpu_custom_call", output_to_operand_aliasing={{5}: (8, {}), {6}: (9, {}), {7}: (10, {}), {8}: (11, {})} | custom-call | flops 7864320000 | bytes 6291456 | tf_op jit(solution)/shard_map/conv_state1/pallas_call | solution.py:422
  299.6 43.8 %project_z.1 = (f32[1024,1536]{1,0:T(8,128)}, f32[1024,1536]{1,0:T(8,128)}, bf16[2,16,48,2048]{3,2,1,0:T(8,128)(2,1)}, bf16[2,16,48,2048]{3,2,1,0:T(8,128)(2,1)}...) custom-call(bf16[1024,1536]{1,0:T(8,128)(2,1)} %get-tuple-element.26, ...), custom_call_target="tpu_custom_call", output_to_operand_aliasing={{2}: (4, {}), {3}: (5, {}), {4}: (6, {}), {5}: (7, {}), {6}... | custom-call | flops 9663676416 | bytes 12582912 | tf_op jit(solution)/shard_map/project_z/pallas_call | solution.py:422
  344.1 39.6 %scan_forward0.1 = (bf16[1024,1536]{1,0:T(8,128)(2,1)}, f32[1024,1536]{1,0:T(8,128)}, f32[128,1536]{1,0:T(8,128)}, bf16[2,16,48,2048]{3,2,1,0:T(8,128)(2,1)}, bf16[2,16,48,2048]{3,2,1,0:T(8,128)(2,1)}) custom-call(f32[1024,1536]{1,0:T(8,128)} %get-tuple-element.286.refs_0_, ...), custom_call_target="tpu_custom_call", output_to_operand_aliasing={{3}: (8, {}), {4}: (9, {})} | custom-call | flops 15728640000 | bytes 12582912 | tf_op jit(solution)/shard_map/scan_forward0/pallas_call | solution.py:422
  383.7 38.9 %scan_forward1.1 = (bf16[1024,1536]{1,0:T(8,128)(2,1)}, f32[1024,1536]{1,0:T(8,128)}, f32[128,1536]{1,0:T(8,128)}, bf16[2,16,48,2048]{3,2,1,0:T(8,128)(2,1)}, bf...) custom-call(f32[1024,1536]{1,0:T(8,128)} %get-tuple-element.311.refs, ...), custom_call_target="tpu_custom_call", output_to_operand_aliasing={{3}: (8, {}), {4}: (9, {}), {5}: (10, {}), {6}: (11, {})} | custom-call | flops 15728640000 | bytes 12582912 | tf_op jit(solution)/shard_map/scan_forward1/pallas_call | solution.py:422
  422.7 15.7 %project_out.1 = (f32[1024,1536]{1,0:T(8,128)}, bf16[2,16,48,2048]{3,2,1,0:T(8,128)(2,1)}, bf16[2,16,48,2048]{3,2,1,0:T(8,128)(2,1)}) custom-call(bf16[1024,1536]{1,0:T(8,128)(2,1)} %get-tuple-element.309.refs_0_.refs_1_, bf16[1536,1536]{1,0:T(8,128)(2,1)} %bitcast.346, ...), custom_call_target="tpu_custom_call", output_to_operand_aliasing={{1}: (4, {}), {2}: (5, {})} | custom-call | flops 9663676416 | bytes 6291456 | tf_op jit(solution)/shard_map/project_out/pallas_call | solution.py:422
  438.4 11.5 norm_two.1
  449.9 52.8 %feed_forward.1 = (bf16[1024,2048]{1,0:T(8,128)(2,1)}, bf16[1024,2048]{1,0:T(8,128)(2,1)}, bf16[1024,2048]{1,0:T(8,128)(2,1)}, bf16[1024,2048]{1,0:T(8,128)(2,1)...) custom-call(bf16[1024,1536]{1,0:T(8,128)(2,1)} %get-tuple-element.326.n_ref, ...), custom_call_target="tpu_custom_call" | custom-call | flops 38654705664 | bytes 25165824 | tf_op jit(solution)/shard_map/feed_forward/pallas_call | solution.py:364
  502.6 20.4 %down_grad.1 = (bf16[1536,2048]{1,0:T(8,128)(2,1)}, bf16[1536,2048]{1,0:T(8,128)(2,1)}) custom-call(bf16[1536,1024]{1,0:T(8,128)(2,1)} %get-tuple-element.336.refs_0_.refs_2_, bf16[1024,2048]{1,0:T(8,128)(2,1)} %get-tuple-element.334.refs_1_.refs_0_, bf16[1536,1024]{1,0:T(8,128)(2,1)} %get-tuple-element.336.refs_0_.refs_2_, ...), custom_call_target="tpu_custom_call" | custom-call | flops 12884901888 | bytes 25165824 | tf_op jit(solution)/shard_map/down_grad/pallas_call | solution.py:364
  523.0 21.3 %gate_grad.1 = (bf16[1536,2048]{1,0:T(8,128)(2,1)}, bf16[1536,2048]{1,0:T(8,128)(2,1)}, bf16[2,8,48,1024]{3,2,1,0:T(8,128)(2,1)}, bf16[2,8,48,1024]{3,2,1,0:T(8,...) custom-call(bf16[1536,1024]{1,0:T(8,128)(2,1)} %get-tuple-element.338.refs_0_.refs_2_, ...), custom_call_target="tpu_custom_call" | custom-call | flops 12884901888 | bytes 25165824 | tf_op jit(solution)/shard_map/gate_grad/pallas_call | solution.py:422
  553.1 26.0 %up_grad.1 = (bf16[1536,2048]{1,0:T(8,128)(2,1)}, bf16[1536,2048]{1,0:T(8,128)(2,1)}, bf16[4,48,1024]{2,1,0:T(8,128)(2,1)}, bf16[4,48,1024]{2,1,0:T(8,128)(2,1)}...) custom-call(bf16[1536,1024]{1,0:T(8,128)(2,1)} %get-tuple-element.33, ...), custom_call_target="tpu_custom_call" | custom-call | flops 12884901888 | bytes 25165824 | tf_op jit(solution)/shard_map/up_grad/pallas_call | solution.py:422
  583.5 35.0 %project_down.1 = (f32[1024,1536]{1,0:T(8,128)}, bf16[4,48,1024]{2,1,0:T(8,128)(2,1)}, bf16[4,48,1024]{2,1,0:T(8,128)(2,1)}, bf16[8,48,1024]{2,1,0:T(8,128)(2,1)...) custom-call(bf16[1024,2048]{1,0:T(8,128)(2,1)} %get-tuple-element.33, ...), custom_call_target="tpu_custom_call" | custom-call | flops 12884901888 | bytes 6291456 | tf_op jit(solution)/shard_map/project_down/pallas_call | solution.py:422
  635.3 53.3 %two_back.1 = (f32[1024,1536]{1,0:T(8,128)}, bf16[4,48,1024]{2,1,0:T(8,128)(2,1)}, bf16[4,48,1024]{2,1,0:T(8,128)(2,1)}, bf16[8,48,1024]{2,1,0:T(8,128)(2,1)}, b...) custom-call(bf16[1024,2048]{1,0:T(8,128)(2,1)} %get-tuple-element.33, ...), custom_call_target="tpu_custom_call" | custom-call | flops 25769803776 | bytes 6291456 | tf_op jit(solution)/shard_map/two_back/pallas_call | solution.py:422
  701.8 20.0 %norm_two_back.1 = (bf16[1024,1536]{1,0:T(8,128)(2,1)}, bf16[1024,1536]{1,0:T(8,128)(2,1)}, f32[8,1536]{1,0:T(8,128)}, bf16[1536,1024]{1,0:T(8,128)(2,1)}, bf16[...) custom-call(f32[1024,1536]{1,0:T(8,128)} %get-tuple-element.325.refs, ...), custom_call_target="tpu_custom_call" | custom-call | flops 31457280 | bytes 25165824 | tf_op jit(solution)/shard_map/norm_two_back/pallas_call | solution.py:422
  738.1 25.5 %out_grad.1 = (bf16[1536,1536]{1,0:T(8,128)(2,1)}, bf16[1536,1536]{1,0:T(8,128)(2,1)}, bf16[4,48,1024]{2,1,0:T(8,128)(2,1)}, bf16[4,48,1024]{2,1,0:T(8,128)(2,1)...) custom-call(bf16[1536,1024]{1,0:T(8,128)(2,1)} %get-tuple-element.37, ...), custom_call_target="tpu_custom_call" | custom-call | flops 9663676416 | bytes 18874368 | tf_op jit(solution)/shard_map/out_grad/pallas_call | solution.py:422
  768.0 18.4 %gated_back.1 = (f32[1024,1536]{1,0:T(8,128)}, f32[1024,1536]{1,0:T(8,128)}, bf16[4,48,1024]{2,1,0:T(8,128)(2,1)}, bf16[4,48,1024]{2,1,0:T(8,128)(2,1)}, bf16[2,...) custom-call(bf16[1024,1536]{1,0:T(8,128)(2,1)} %get-tuple-element.371.refs_0_.refs_2_.refs_4_, ...), custom_call_target="tpu_custom_call" | custom-call | flops 9663676416 | bytes 12582912 | tf_op jit(solution)/shard_map/gated_back/pallas_call | solution.py:422
  796.1 21.0 %gate_backward0.1 = (f32[1024,1536]{1,0:T(8,128)}, bf16[1024,1536]{1,0:T(8,128)(2,1)}, f32[16,1536]{1,0:T(8,128)}, bf16[4,48,1024]{2,1,0:T(8,128)(2,1)}, bf16[4,...) custom-call(f32[1024,1536]{1,0:T(8,128)} %get-tuple-element.382.refs, ...), custom_call_target="tpu_custom_call" | custom-call | flops 7864320000 | bytes 15728640 | tf_op jit(solution)/shard_map/gate_backward0/pallas_call | solution.py:422
  819.6 13.1 %gate_backward1.1 = (f32[1024,1536]{1,0:T(8,128)}, bf16[1024,1536]{1,0:T(8,128)(2,1)}, f32[16,1536]{1,0:T(8,128)}) custom-call(f32[1024,1536]{1,0:T(8,128)} %get-tuple-element.392.gg_ref, f32[1024,1536]{1,0:T(8,128)} %get-tuple-element.312.refs_1_.z_ref, f32[1024,1536]{1,0:T(8,128)} %get-tuple-element.393.y_ref, ...), custom_call_target="tpu_custom_call" | custom-call | flops 7864320000 | bytes 15728640 | tf_op jit(solution)/shard_map/gate_backward1/pallas_call | solution.py:364
  835.6 25.6 %z_grad.1 = (bf16[1536,1536]{1,0:T(8,128)(2,1)}, bf16[1536,1536]{1,0:T(8,128)(2,1)}, bf16[2,48,1024]{2,1,0:T(8,128)(2,1)}, bf16[2,48,1024]{2,1,0:T(8,128)(2,1)}, bf16[2,48,1024]{2,1,0:T(8,128)(2,1)}) custom-call(bf16[1536,1024]{1,0:T(8,128)(2,1)} %get-tuple-element.355.refs_0_.refs_2_, bf16[1024,1536]{1,0:T(8,128)(2,1)} %get-tuple-element.407.refs_1_.refs_0_, ...), custom_call_target="tpu_custom_call" | custom-call | flops 9663676416 | bytes 18874368 | tf_op jit(solution)/shard_map/z_grad/pallas_call | solution.py:422
  861.3 15.8 %z_back.1 = (f32[1024,1536]{1,0:T(8,128)}, bf16[2,8,48,1536]{3,2,1,0:T(8,128)(2,1)}, bf16[2,8,48,1536]{3,2,1,0:T(8,128)(2,1)}) custom-call(bf16[1024,1536]{1,0:T(8,128)(2,1)} %get-tuple-element.407.refs_1_.refs_0_, bf16[1536,1536]{1,0:T(8,128)(2,1)} %bitcast.329, bf16[1024,1536]{1,0:T(8,128)(2,1)} %get-tuple-element.408.refs_3_.refs_2_, ...), custom_call_target="tpu_custom_call" | custom-call | flops 9663676416 | bytes 6291456 | tf_op jit(solution)/shard_map/z_back/pallas_call | solution.py:422
  888.8 55.2 %scan_backward0.1 = (bf16[1024,1536]{1,0:T(8,128)(2,1)}, f32[1024,128]{1,0:T(8,128)}, f32[8,1536]{1,0:T(8,128)}, f32[24,1536]{1,0:T(8,128)}, f32[8,128]{1,0:T(8,...) custom-call(f32[1024,1536]{1,0:T(8,128)} %get-tuple-element.286.refs, ...), custom_call_target="tpu_custom_call" | custom-call | flops 39321600000 | bytes 18874368 | tf_op jit(solution)/shard_map/scan_backward0/pallas_call | solution.py:422
  955.1 53.6 %scan_backward1.1 = (bf16[1024,1536]{1,0:T(8,128)(2,1)}, f32[1024,128]{1,0:T(8,128)}, f32[8,1536]{1,0:T(8,128)}, f32[24,1536]{1,0:T(8,128)}, f32[8,128]{1,0:T(8,...) custom-call(f32[1024,1536]{1,0:T(8,128)} %get-tuple-element.311.refs, ...), custom_call_target="tpu_custom_call" | custom-call | flops 39321600000 | bytes 18874368 | tf_op jit(solution)/shard_map/scan_backward1/pallas_call | solution.py:422
  1032.6 25.9 %x_grad.1 = (bf16[1536,1536]{1,0:T(8,128)(2,1)}, bf16[1536,1536]{1,0:T(8,128)(2,1)}, bf16[4,48,1536]{2,1,0:T(8,128)(2,1)}, bf16[4,48,1536]{2,1,0:T(8,128)(2,1)},...) custom-call(bf16[1536,1024]{1,0:T(8,128)(2,1)} %get-tuple-element.355.refs_0_.refs_2_, ...), custom_call_target="tpu_custom_call" | custom-call | flops 9663676416 | bytes 18874368 | tf_op jit(solution)/shard_map/x_grad/pallas_call | solution.py:422
  1059.8 36.3 %x_back.1 = (f32[1024,1536]{1,0:T(8,128)}, bf16[2,8,48,1536]{3,2,1,0:T(8,128)(2,1)}, bf16[2,8,48,1536]{3,2,1,0:T(8,128)(2,1)}, bf16[2,8,48,128]{3,2,1,0:T(8,128)...) custom-call(bf16[1024,1536]{1,0:T(8,128)(2,1)} %get-tuple-element.53, ...), custom_call_target="tpu_custom_call" | custom-call | flops 10468982784 | bytes 6291456 | tf_op jit(solution)/shard_map/x_back/pallas_call | solution.py:422
  1107.5 46.3 %norm_one_back.1 = (bf16[1024,1536]{1,0:T(8,128)(2,1)}, bf16[1024,1536]{1,0:T(8,128)(2,1)}, f32[8,1536]{1,0:T(8,128)}, bf16[1536,1024]{1,0:T(8,128)(2,1)}, bf16[...) custom-call(f32[1024,1536]{1,0:T(8,128)} %get-tuple-element.260.refs, ...), custom_call_target="tpu_custom_call" | custom-call | flops 31457280 | bytes 25165824 | tf_op jit(solution)/shard_map/norm_one_back/pallas_call | solution.py:422
  1167.7 24.3 %turn_out.1 = (bf16[1024,1536]{1,0:T(8,128)(2,1)}, bf16[4,48,1536]{2,1,0:T(8,128)(2,1)}, bf16[4,48,1536]{2,1,0:T(8,128)(2,1)}, bf16[4,48,128]{2,1,0:T(8,128)(2,1)}, bf16[4,48,128]{2,1,0:T(8,128)(2,1)}) custom-call(bf16[1024,1536]{1,0:T(8,128)(2,1)} %add_convert_fusion.refs_0_, bf16[1536,1536]{1,0:T(8,128)(2,1)} %fusion.1.refs_1_.refs_3_, ...), custom_call_target="tpu_custom_call" | custom-call | flops 4831838208 | bytes 6291456 | tf_op jit(solution)/shard_map/turn_out/pallas_call | solution.py:422
  1197.1 42.5 %turn_back.1 = (f32[1024,1536]{1,0:T(8,128)}, bf16[2,48,1536]{2,1,0:T(8,128)(2,1)}, bf16[2,48,1536]{2,1,0:T(8,128)(2,1)}, bf16[2,48,1536]{2,1,0:T(8,128)(2,1)}, ...) custom-call(bf16[1024,1536]{1,0:T(8,128)(2,1)} %get-tuple-element.447.refs_0_, ...), custom_call_target="tpu_custom_call" | custom-call | flops 9663676416 | bytes 6291456 | tf_op jit(solution)/shard_map/turn_back/pallas_call | solution.py:422
  (497 shorter events, 236.3 us)
Async XLA Ops:
  1.5 198.6 %collective-permute-start = (bf16[16,1536]{1,0:T(8,128)(2,1)S(1)}, bf16[16,1536]{1,0:T(8,128)(2,1)S(1)}, u32[]{:S(2)}, u32[]{:S(2)}) collective-permute-start(bf16[16,1536]{1,0:T(8,128)(2,1)S(1)} %slice.436), channel_id=1, source_target_pairs={{0,1},{2,3},{4,5},{6,7},{8,9},{10,11},{12,13},{14,15},{16,17},{18,... | collective-permute-start | bytes 147464 | tf_op jit(solution)/shard_map/ppermute | solution.py:861
  10.0 199.2 %collective-permute-start.1 = (f32[8,1536]{1,0:T(8,128)S(1)}, f32[8,1536]{1,0:T(8,128)S(1)}, u32[]{:S(2)}, u32[]{:S(2)}) collective-permute-start(f32[8,1536]{1,0:T(8,128)S(1)} %select_maximum_fusion.refs_3_.refs_7_.refs_5_), channel_id=1, source_target_pairs={{0,1},{1,0},{2,3},{3,2},{4,5},{5,4},{6,7},{7,6},{8,9},{9,8},{10,11... | collective-permute-start | bytes 147464 | tf_op jit(solution)/shard_map/ppermute | solution.py:814
  209.2 47.4 %copy-start.106 = (f32[8,1536]{1,0:T(8,128)}, f32[8,1536]{1,0:T(8,128)S(1)}, u32[]{:S(2)}) copy-start(f32[8,1536]{1,0:T(8,128)S(1)} %collective-permute-done.1.refs_3_.refs_7_.refs_5_) | copy-start | bytes 147460
  297.7 45.8 %collective-permute-start.2 = (f32[2,16,1536]{2,1,0:T(8,128)S(1)}, f32[2,16,1536]{2,1,0:T(8,128)S(1)}, u32[]{:S(2)}, u32[]{:S(2)}) collective-permute-start(f32[2,16,1536]{2,1,0:T(8,128)S(1)} %pad_maximum_fusion.4), channel_id=1, source_target_pairs={{0,1},{2,3},{4,5},{6,7},{8,9},{10,11},{12,13},{14,15},{16,17},{18,... | collective-permute-start | bytes 589832 | tf_op jit(solution)/shard_map/ppermute | solution.py:902
  635.3 61.1 %slice-start.2 = ((s8[6291456]{0:T(1024)(128)(4,1)}), s8[4194304]{0:T(1024)(128)(4,1)S(1)}, s32[]{:S(2)}) async-start(s8[6291456]{0:T(1024)(128)(4,1)} %bitcast.344), calls=%async_computation.2 | async-start | bytes 8388608
  635.3 61.1 %slice-start.3 = ((s8[6291456]{0:T(1024)(128)(4,1)}), s8[2097152]{0:T(1024)(128)(4,1)S(1)}, s32[]{:S(2)}) async-start(s8[6291456]{0:T(1024)(128)(4,1)} %bitcast.344), calls=%async_computation.3 | async-start | bytes 4194304
  834.3 52.8 %collective-permute-start.3 = (f32[2,16,1536]{2,1,0:T(8,128)}, f32[2,16,1536]{2,1,0:T(8,128)}, u32[]{:S(2)}, u32[]{:S(2)}) collective-permute-start(f32[2,16,1536]{2,1,0:T(8,128)} %pad_maximum_fusion.5), channel_id=1, source_target_pairs={{1,0},{3,2},{5,4},{7,6},{9,8},{11,10},{13,12},{15,14},{17,16},{19,... | collective-permute-start | bytes 589832 | tf_op jit(solution)/shard_map/ppermute | solution.py:940
  955.1 53.6 %copy-start.17 = (bf16[8,48,1536]{2,1,0:T(8,128)(2,1)S(1)}, bf16[8,48,1536]{2,1,0:T(8,128)(2,1)}, u32[]{:S(2)}) copy-start(bf16[8,48,1536]{2,1,0:T(8,128)(2,1)} %fusion.5.refs_20_) | copy-start | bytes 3538948
  955.1 54.9 %copy-start.26 = (bf16[8,48,1024]{2,1,0:T(8,128)(2,1)S(1)}, bf16[8,48,1024]{2,1,0:T(8,128)(2,1)}, u32[]{:S(2)}) copy-start(bf16[8,48,1024]{2,1,0:T(8,128)(2,1)} %fusion.7.refs_18_) | copy-start | bytes 2359300
  1019.1 10.9 collective-permute-start.4
  1058.5 45.7 %slice-start.8 = ((s8[4718592]{0:T(1024)(128)(4,1)}), s8[524288]{0:T(1024)(128)(4,1)S(1)}, s32[]{:S(2)}) async-start(s8[4718592]{0:T(1024)(128)(4,1)} %bitcast.377), calls=%async_computation.8 | async-start | bytes 1048576
  1059.8 46.7 %copy-start.14 = (bf16[4,48,1536]{2,1,0:T(8,128)(2,1)}, bf16[4,48,1536]{2,1,0:T(8,128)(2,1)S(1)}, u32[]{:S(2)}) copy-start(bf16[4,48,1536]{2,1,0:T(8,128)(2,1)S(1)} %add_convert_fusion.21.refs_11_) | copy-start | bytes 1769476
  1059.8 44.5 %slice-start.9 = ((s8[4718592]{0:T(1024)(128)(4,1)}), s8[4194304]{0:T(1024)(128)(4,1)S(1)}, s32[]{:S(2)}) async-start(s8[4718592]{0:T(1024)(128)(4,1)} %bitcast.377), calls=%async_computation.9 | async-start | bytes 8388608
  1107.5 56.0 %copy-start.39 = (bf16[2,8,48,128]{3,2,1,0:T(8,128)(2,1)S(1)}, bf16[2,8,48,128]{3,2,1,0:T(8,128)(2,1)}, u32[]{:S(2)}) copy-start(bf16[2,8,48,128]{3,2,1,0:T(8,128)(2,1)} %add_convert_fusion.38.refs_8_) | copy-start | bytes 589828
  1160.1 82.7 %collective-permute-start.5 = (f32[1536]{0:T(1024)S(1)}, f32[1536]{0:T(1024)}, u32[]{:S(2)}, u32[]{:S(2)}) collective-permute-start(f32[1536]{0:T(1024)S(1)} %reshape.690), channel_id=1, source_target_pairs={{0,1},{1,0},{2,3},{3,2},{4,5},{5,4},{6,7},{7,6},{8,9},{9,8},{10,11... | collective-permute-start | bytes 18440 | tf_op jit(solution)/shard_map/ppermute | solution.py:814
  1163.0 80.6 %collective-permute-start.10 = (f32[11008]{0:T(1024)}, f32[11008]{0:T(1024)}, u32[]{:S(2)}, u32[]{:S(2)}) collective-permute-start(f32[11008]{0:T(1024)} %pad_maximum_fusion.6), channel_id=1, source_target_pairs={{0,1},{1,0},{2,3},{3,2},{4,5},{5,4},{6,7},{7,6},{8,9},{9,8},{10,11... | collective-permute-start | bytes 132104 | tf_op jit(solution)/shard_map/ppermute | solution.py:814
  1197.0 42.8 %copy-start.75 = (bf16[2,48,1536]{2,1,0:T(8,128)(2,1)S(1)}, bf16[2,48,1536]{2,1,0:T(8,128)(2,1)}, u32[]{:S(2)}) copy-start(bf16[2,48,1536]{2,1,0:T(8,128)(2,1)} %get-tuple-element.460) | copy-start | bytes 884740
  1197.0 42.8 %copy-start.76 = (bf16[2,48,1536]{2,1,0:T(8,128)(2,1)S(1)}, bf16[2,48,1536]{2,1,0:T(8,128)(2,1)}, u32[]{:S(2)}) copy-start(bf16[2,48,1536]{2,1,0:T(8,128)(2,1)} %get-tuple-element.461) | copy-start | bytes 884740
  1197.0 42.8 %copy-start.77 = (bf16[2,48,1536]{2,1,0:T(8,128)(2,1)S(1)}, bf16[2,48,1536]{2,1,0:T(8,128)(2,1)}, u32[]{:S(2)}) copy-start(bf16[2,48,1536]{2,1,0:T(8,128)(2,1)} %get-tuple-element.462) | copy-start | bytes 884740
  1197.0 43.7 %slice-start.10 = ((bf16[4,48,1536]{2,1,0:T(8,128)(2,1)}), bf16[1,48,1536]{2,1,0:T(8,128)(2,1)S(1)}, s32[]{:S(2)}) async-start(bf16[4,48,1536]{2,1,0:T(8,128)(2,1)} %copy-done.44), calls=%async_computation.10 | async-start | bytes 294912 | tf_op jit(solution)/shard_map/slice | solution.py:636
  1197.1 43.7 %slice-start.12 = ((bf16[4,48,1536]{2,1,0:T(8,128)(2,1)}), bf16[1,48,1536]{2,1,0:T(8,128)(2,1)S(1)}, s32[]{:S(2)}) async-start(bf16[4,48,1536]{2,1,0:T(8,128)(2,1)} %copy-done.46), calls=%async_computation.12 | async-start | bytes 294912 | tf_op jit(solution)/shard_map/slice | solution.py:636
  1197.1 43.7 %copy-start.72 = (bf16[2,48,1536]{2,1,0:T(8,128)(2,1)S(1)}, bf16[2,48,1536]{2,1,0:T(8,128)(2,1)}, u32[]{:S(2)}) copy-start(bf16[2,48,1536]{2,1,0:T(8,128)(2,1)} %get-tuple-element.471) | copy-start | bytes 884740
  1197.1 43.7 %copy-start.73 = (bf16[2,48,1536]{2,1,0:T(8,128)(2,1)S(1)}, bf16[2,48,1536]{2,1,0:T(8,128)(2,1)}, u32[]{:S(2)}) copy-start(bf16[2,48,1536]{2,1,0:T(8,128)(2,1)} %get-tuple-element.472) | copy-start | bytes 884740
  1197.1 43.7 %copy-start.74 = (bf16[2,48,1536]{2,1,0:T(8,128)(2,1)S(1)}, bf16[2,48,1536]{2,1,0:T(8,128)(2,1)}, u32[]{:S(2)}) copy-start(bf16[2,48,1536]{2,1,0:T(8,128)(2,1)} %get-tuple-element.473) | copy-start | bytes 884740
  1243.7 1.5 collective-permute-start.6
  1244.5 2.3 collective-permute-start.11
  1245.2 3.7 collective-permute-start.7
  1246.8 4.1 collective-permute-start.12
  1248.9 3.7 collective-permute-start.8
  1250.9 4.2 collective-permute-start.13
  1252.7 5.4 collective-permute-start.9
  1255.1 5.5 collective-permute-start.14
  (126 other events, 1038.3 us)

commit v3 on v2

--- a/solution.py
+++ b/solution.py
@@ -66,14 +66,18 @@
     return (i > k) if strict else (i >= k)
 
 
-def conv_rows(x_ref, xp_ref, halo_ref, cw_ref, col, q, lanes):
+def spread_marks(col):
+    return [jnp.broadcast_to(col[:, SEG + k : SEG + k + 1], (Q, 128)) for k in (1, 2, 3)]
+
+
+def conv_rows(x_ref, xp_ref, halo_ref, cw_ref, marks, q, lanes):
     x = x_ref[:, lanes]
     prev = jnp.where(q == 0, halo_ref[:, lanes], xp_ref[:, lanes])
     cat = jnp.concatenate([prev, x], axis=0)
     acc = cw_ref[4:5, lanes] + cw_ref[0:1, lanes] * x
     shifted = []
     for k in (1, 2, 3):
-        back = pltpu.roll(cat, k, 0)[HALO:, :] * col[:, SEG + k : SEG + k + 1]
+        back = pltpu.roll(cat, k, 0)[HALO:, :] * marks[k - 1]
         shifted.append(back)
         acc = acc + cw_ref[k : k + 1, lanes] * back
     return x, shifted, acc
@@ -111,9 +115,10 @@
     et_ref[...] = et
     bt = wide_left(et[COLB:COLC, :])
     left = lane < HEADDIM
+    spread = spread_marks(col)
     for j in range(x_ref.shape[1] // 128):
         lanes = slice(128 * j, 128 * j + 128)
-        _, _, acc = conv_rows(x_ref, xp_ref, halo_ref, cw_ref, col, q, lanes)
+        _, _, acc = conv_rows(x_ref, xp_ref, halo_ref, cw_ref, spread, q, lanes)
         u = acc * sigmoid(acc)
         u_ref[:, lanes] = u
         scaled = u * (pair_cols(col, DT, j, left) * pair_cols(col, TAIL, j, left))
@@ -209,6 +214,7 @@
     scores = dot(b, ct, highest)
     neg = jnp.where((col[:, SEG : SEG + 1] == row[SEG : SEG + 1, :]) & triangle(transposed=True), 0.0, NEG)
     b, ct, c = wide_left(b), ct.astype(bf16), wide_left(e[:, COLC : COLC + STATES])
+    spread = spread_marks(col)
     DG[...] = jnp.zeros_like(DG)
     SUMS[...] = jnp.zeros_like(SUMS)
     for j in range(u_ref.shape[1] // 128):
@@ -252,13 +258,13 @@
         CONST[0:1, lanes] = keep * jnp.sum(state * grad_state, axis=0, keepdims=True)
         D[:, lanes] = keep * grad_state + dot(ct, low_dec)
 
-        x, shifted, acc = conv_rows(x_ref, xp_ref, halo_ref, cw_ref, col, q, lanes)
+        x, shifted, acc = conv_rows(x_ref, xp_ref, halo_ref, cw_ref, spread, q, lanes)
         sig = sigmoid(acc)
         dconv = (dxs * dt + cw_ref[5:6, lanes] * dyf) * (sig * (1.0 + acc * (1.0 - sig)))
         dx = cw_ref[0:1, lanes] * dconv
         cg_ref[0:1, lanes] += jnp.sum(dconv * x, axis=0, keepdims=True)
         for k in (1, 2, 3):
-            masked = dconv * col[:, SEG + k : SEG + k + 1]
+            masked = dconv * spread[k - 1]
             after = edge_ref[8 * (k - 1) : 8 * k, lanes]
             cat = jnp.concatenate([masked, after], axis=0)
             dx = dx + cw_ref[k : k + 1, lanes] * pltpu.roll(cat, Q + 8 - k, 0)[:Q, :]
@@ -437,7 +443,7 @@
     return result[:n_out]
 
 
-def matmul(jobs, dtype, tile, name, load=None, nt=False, turned=False):
+def matmul(jobs, dtype, tile, name, load=None, nt=False, turned=False, beside=None):
     n_jobs, n_pairs = len(jobs), len(jobs[0])
     rows = jobs[0][0][0].shape[0]
     columns = jobs[0][0][1].shape[0 if nt else 1]
@@ -464,9 +470,18 @@
     if turned:
         out_specs += [pl.BlockSpec((tile, rows), lambda j, t, p=at(job): (p(j, t), 0)) for job in range(n_jobs)]
         out_shape += [jax.ShapeDtypeStruct((columns, rows), dtype)] * n_jobs
+    if beside:
+        few, narrow = beside
+        args += [few, *narrow]
+        in_specs += [pl.BlockSpec(v.shape, lambda j, t: (0, 0), pipeline_mode=pl.Buffered(1)) for v in (few, *narrow)]
+        out_specs += [pl.BlockSpec((few.shape[0], tile), lambda j, t, p=at(job): (0, p(j, t))) for job in range(n_jobs)]
+        out_shape += [jax.ShapeDtypeStruct((few.shape[0], columns), dtype)] * n_jobs
+        out_specs += [pl.BlockSpec((rows, v.shape[1]), lambda j, t: (0, 0)) for v in narrow]
+        out_shape += [jax.ShapeDtypeStruct((rows, v.shape[1]), dtype) for v in narrow]
+    n_in = len(args)
 
     def body(*refs):
-        ins, outs = refs[: 2 * n_jobs * n_pairs], refs[2 * n_jobs * n_pairs :]
+        ins, outs = refs[:n_in], refs[n_in:]
         for job in range(n_jobs):
 
             @pl.when(pl.program_id(0) == job)
@@ -479,6 +494,14 @@
                 outs[job][...] = total.astype(dtype)
                 if turned:
                     outs[n_jobs + job][...] = total.T.astype(dtype)
+                if beside:
+                    left, right, few = ins[2 * job * n_pairs], ins[2 * job * n_pairs + 1], ins[2 * n_jobs * n_pairs]
+                    outs[n_jobs + job][...] = dot(few[...], right[...]).astype(dtype)
+
+                    @pl.when(pl.program_id(1) == 0)
+                    def _():
+                        narrow = ins[2 * n_jobs * n_pairs + 1 + job]
+                        outs[2 * n_jobs + job][...] = dot(left[...], narrow[...]).astype(dtype)
 
     depth = sum(p[0].shape[1] for p in jobs[0])
     return run(
@@ -488,6 +511,59 @@
         ),
         load,
     )
+
+
+class LateScatter:
+    def __init__(self, key, n, other):
+        self.key, self.n, self.phase = key, n, 0
+        self.given(other)
+
+    def given(self, grad):
+        self.rows, self.cols = grad.shape[0] // self.n, grad.shape[1]
+        self.now = grad.reshape(2, self.n, self.rows // 2, self.cols)
+
+    def moves(self):
+        k, q, v = self.key, self.n // 4, self.now
+        far, rest = slice(q, 2 * q), slice(2 * q, 4 * q)
+
+        def new(*dims):
+            return jax.ShapeDtypeStruct(dims + (self.rows // 2, self.cols), bf16)
+
+        core = [(k + "v", (i, rest), k + "r", (i,), ("fsdp", 1)) for i in (0, 1)]
+        if self.phase == 0:
+            return {k + "v": v}, {}, {k + "r": new(2, 2 * q)}, core
+        if self.phase == 1:
+            copies = [(k + "v", (0, far), k + "r", ALL, ("fsdp", 2)), (k + "v", (1,), k + "s", ALL, ("tp", 1))]
+            return {k + "v": v}, {}, {k + "r": new(q), k + "s": new(2 * q)}, copies
+        if self.phase == 2:
+            copies = core + [(k + "a", ALL, k + "s", ALL, ("tp", 1))]
+            return {k + "v": v, k + "a": self.other}, {}, {k + "r": new(2, 2 * q), k + "s": new(q)}, copies
+        if self.phase == 3:
+            copies = [(k + "v", (far,), k + "r", ALL, ("fsdp", 2)), (k + "a", (far,), k + "s", ALL, ("fsdp", 2))]
+            return {k + "v": v[0], k + "a": v[1]}, {}, {k + "r": new(q), k + "s": new(q)}, copies
+        news = {f"{k}r{m}": new(2) for m in range(1, q)}
+        copies = [(f"{k}v{i}", (m,), f"{k}r{m}", (i,), ("fsdp", m << 2)) for m in range(1, q) for i in (0, 1)]
+        return {k + "v0": v[0], k + "v1": v[1]}, {}, news, copies
+
+    def take(self, got):
+        k, q, v = self.key, self.n // 4, self.now
+        if self.phase == 0:
+            self.now = low_sum(v[:, : 2 * q], got[k + "r"])
+        elif self.phase == 1:
+            self.other, self.lower = low_sum(v[0, :q], got[k + "r"]), got[k + "s"]
+        elif self.phase == 2:
+            own = [v[i, : 2 * q].astype(f32) + got[k + "r"][i].astype(f32) for i in (0, 1)]
+            self.now = [own[0].astype(bf16), (own[1] + self.lower.astype(f32)).astype(bf16)]
+            self.other = got[k + "s"]
+        elif self.phase == 3:
+            upper = v[0][:q].astype(f32) + got[k + "r"].astype(f32) + self.other.astype(f32)
+            self.now = [upper.astype(bf16), low_sum(v[1][:q], got[k + "s"])]
+        else:
+            total = jnp.stack([v[0][0], v[1][0]]).astype(f32)
+            for m in range(1, q):
+                total = total + got[f"{k}r{m}"].astype(f32)
+            self.out = total.reshape(self.rows, self.cols)
+        self.phase += 1
 
 
 def feed_forward(normed, cot, gate_w, up_w, down_w):
@@ -539,7 +615,7 @@
 
 
 def low_sum(a, b):
-    return (a.astype(f32) + b.astype(f32)).astype(bf16)
+    return a + b
 
 
 class Gather:
@@ -888,12 +964,14 @@
         normed_before = (halo_rows * halo_scale * gain_one).astype(bf16)
         marks = token_marks(seg, seg_before)
 
-        xs = matmul([[(normed, w)] for w in X.full], f32, 512, "project_x", Load(Z, O, G))
+        found = matmul(
+            [[(normed, w)] for w in X.full], f32, 512, "project_x", Load(Z, O, G), beside=(normed_before, E.full)
+        )
+        xs, halos, es = found[:2], found[2:4], found[4:]
         saved = []
         for b in (0, 1):
             v = dict(x=xs[b], cw=smalls[b], hp=head_rows[b])
-            v["e"] = bf_dot(normed, E.full[b])
-            v["halo"] = bf_dot(normed_before, X.full[b])
+            v["e"], v["halo"] = es[b], halos[b]
             load = Load(Z, O, G, U) if b == 0 else Load(G, O, D)
             v["u"], v["end"], v["col"], v["row"], v["et"] = conv_state(
                 v["x"], v["halo"], v["cw"], v["e"], v["hp"], marks, tag=str(b), load=load
@@ -939,14 +1017,34 @@
             )
         ends = lax.ppermute(jnp.stack([v["ds"] for v in saved]), "tp", [(1, 0)])[::-1]
         sz = Scatter("z", matmul([[(normed_t, v["dz"])] for v in saved], bf16, 512, "z_grad", Load(ua)), n)
-        (grad_z,) = matmul([[(v["dz"], w) for v, w in zip(saved, Z.full)]], f32, 512, "z_back", Load(sz), nt=True)
-        for b in (0, 1):
+
+        def back(b, load):
             v = saved[b]
             v["dx"], v["de"], v["cg"], v["edge"], v["hg"] = scan_backward(
                 v["u"], v["dy"], v["x"], v["halo"], v["cw"], v["col"], v["row"], v["e"], v["et"], v["states"],
-                ends[b], v["hp"], tag=str(b), load=Load(ub, so, sz) if b else Load(ub, so),
+                ends[b], v["hp"], tag=str(b), load=load,
             )
-        edges = lax.ppermute(jnp.stack([v["edge"] for v in saved]), "tp", [(1, 0)])[::-1]
+            cw, edge = v["cw"], v["edge"].reshape(3, 8, ch)
+            fix = [jnp.zeros((HALO - 3, ch), f32)]
+            for j in (3, 2, 1):
+                fix.append(sum(cw[k : k + 1] * edge[k - 1, k - j : k - j + 1] for k in range(j, 4)))
+            v["fix"] = jnp.concatenate(fix, axis=0)
+
+        def x_gradient(b, load):
+            v = saved[b]
+            return matmul(
+                [[(normed_t, v["dx"]), (before_t, v["fix"].astype(bf16))]], bf16, 512, f"x_grad{b}", load
+            )[0]
+
+        before_t = normed_before.T
+        back(1, Load(so, ub, sz))
+        sx = LateScatter("x", n, x_gradient(1, Load(so)))
+        (grad_z,) = matmul(
+            [[(v["dz"], w) for v, w in zip(saved, Z.full)]], f32, 512, "z_back", Load(sx, ub), nt=True
+        )
+        back(0, Load(sz, sx, so, ub))
+        sx.given(x_gradient(0, Load(sz)))
+        fixes = lax.ppermute(jnp.stack([v["fix"] for v in saved]), "tp", [(1, 0)])[::-1]
         own, other = ([v["cg"][:6].reshape(-1), v["hg"][:2].reshape(-1)] for v in saved)
         gain_two_part = to_global(gain_two_part)
         own, other = jnp.concatenate(own + [gain_two_part]), jnp.concatenate(other + [gain_two_part])
@@ -958,19 +1056,14 @@
         own_lane = jnp.arange(EXTRA)[None, :] < heads
         for b in (0, 1):
             v = saved[b]
-            cw, edge = v["cw"], edges[b].reshape(3, 8, ch)
-            fix = [jnp.zeros((HALO - 3, ch), f32)]
-            for j in (3, 2, 1):
-                fix.append(sum(cw[k : k + 1] * edge[k - 1, k - j : k - j + 1] for k in range(j, 4)))
-            last = v["dx"][tokens - HALO :].astype(f32) + jnp.concatenate(fix, axis=0)
+            last = v["dx"][tokens - HALO :].astype(f32) + fixes[b]
             v["dx"] = lax.dynamic_update_slice(v["dx"], last.astype(bf16), (tokens - HALO, 0))
             v["de"] = jnp.where(own_lane, v["de"], shared).astype(bf16)
-        sx = Scatter("x", matmul([[(normed_t, v["dx"])] for v in saved], bf16, 512, "x_grad", Load(sz, ub)), n)
         se = Scatter("e", matmul([[(normed_t, v["de"])] for v in saved], bf16, 128, "e_grad"), n)
         pairs = [(v["dx"], w) for v, w in zip(saved, X.full)] + [(v["de"], w) for v, w in zip(saved, E.full)]
-        (grad_x,) = matmul([pairs], f32, 512, "x_back", Load(sx, se, so), nt=True)
+        (grad_x,) = matmul([pairs], f32, 512, "x_back", Load(sx, se, sz), nt=True)
         high, low, _, gain_one_part = norm_back(
-            [grad_x, grad_z], rows_in, gain_one, [mixed_grad, mixed_low], "norm_one_back", Load(sx, se, sz)
+            [grad_x, grad_z], rows_in, gain_one, [mixed_grad, mixed_low], "norm_one_back", Load(se)
         )
         (layer_out,) = matmul([[(out_low, turn)]], bf16, 512, "turn_out", Load(sx, se), nt=True)
         (input_grad,) = matmul([[(high, turn), (low, turn)]], f32, 512, "turn_back", Load(sx, se), nt=True)

time: 1280 us -> 1270 us (level)
  Pallas kernels: 1040 us -> 1060 us
  other arithmetic: 156 us -> 137 us
    convert_element_type x54 -> x7, other arithmetic: 115 us -> 9.01 us  [the longest x1 2.73 us: take(): own[0].astype(bf16)]
    add x0 -> x52, other arithmetic: none -> 91 us  [the longest x51 90 us: low_sum(): return a + b]
    pallas_call x28 -> x29, Pallas kernels: 933 us -> 952 us  [run(): pl.pallas_call(kernel, name=name, grid=grid, in_specs=list(in_specs) + [h...]
  transfers between devices with their start and end apart: 15 -> 15, of which waited for: 5 -> 5; matrix products, arithmetic and copies ran while one was open for 6% -> 4% of each run, Pallas kernels for 25% -> 23%
where the time goes in v3:
time: 1270 us; the launch traced here: 1260 us
  Pallas kernels  1060 us (83%)
  other arithmetic  137 us (11%)
  local copies, waits for them, and re-layouts  41.1 us (3%)
  starting transfers between devices  19.4 us (2%)
    pallas_call x29, Pallas kernels, run(): pl.pallas_call(kernel, name=name, grid=grid, in_specs=list(in_specs) + [h...  952 us
    pallas_call x5, Pallas kernels, run(): pl.pallas_call(body, name=name, grid=grid, in_specs=in_specs, out_specs=o...  104 us
    add x51, other arithmetic, low_sum(): return a + b  90 us
  transfers between devices with their start and end apart: 15, of which 5 were waited for; matrix products, arithmetic and copies ran while one was open for 4% of the time, Pallas kernels for 23%

profile of v3, /device:TPU:0, one launch (start us, length us, event | category | flops | bytes accessed | tf_op | source)
XLA Modules:
  0.0 1262.6 jit_solution(2296801397530794848)
XLA Ops:
  29.4 35.9 %turn_rows.1 = (f32[1024,1536]{1,0:T(8,128)}, bf16[2,16,48,1536]{3,2,1,0:T(8,128)(2,1)}, bf16[2,16,48,1536]{3,2,1,0:T(8,128)(2,1)}, bf16[2,16,48,128]{3,2,1,0:T(8,128)(2,1)}, bf16[2,16,48,128]{3,2,1,0:T(8,128)(2,1)}) custom-call(bf16[1024,1536]{1,0:T(8,128)(2,1)} %refs_0_.2, bf16[1536,1536]{1,0:T(8,128)(2,1)} %fusion.1.refs_1_.refs_3_, ...), custom_call_target="tpu_custom_call" | custom-call | flops 4831838208 | bytes 6291456 | tf_op jit(solution)/shard_map/turn_rows/pallas_call | solution.py:428
  65.3 26.9 %norm_one.1 = (f32[1024,1536]{1,0:T(8,128)}, bf16[1024,1536]{1,0:T(8,128)(2,1)}, bf16[1536,1024]{1,0:T(8,128)(2,1)}, bf16[2,16,48,1536]{3,2,1,0:T(8,128)(2,1)}, ...) custom-call(f32[1024,1536]{1,0:T(8,128)} %get-tuple-element.259.refs, ...), custom_call_target="tpu_custom_call", output_to_operand_aliasing={{3}: (3, {}), {4}: (4, {}), {5}: (5, {}), {6}: (6, {})} | custom-call | flops 31457280 | bytes 18874368 | tf_op jit(solution)/shard_map/norm_one/pallas_call | solution.py:428
  92.2 35.7 %turn_cotangent.1 = (bf16[1024,1536]{1,0:T(8,128)(2,1)}, bf16[1536,1024]{1,0:T(8,128)(2,1)}, bf16[2,16,48,1536]{3,2,1,0:T(8,128)(2,1)}, bf16[2,16,48,1536]{3,2,1...) custom-call(bf16[1024,1536]{1,0:T(8,128)(2,1)} %refs_0_.3, ...), custom_call_target="tpu_custom_call", output_to_operand_aliasing={{2}: (3, {}), {3}: (4, {}), {4}: (5, {}), {5}: (6, {})} | custom-call | flops 4831838208 | bytes 6291456 | tf_op jit(solution)/shard_map/turn_cotangent/pallas_call | solution.py:428
  132.0 15.5 %carry_one.1 = (bf16[2,16,48,1536]{3,2,1,0:T(8,128)(2,1)}, bf16[2,16,48,1536]{3,2,1,0:T(8,128)(2,1)}, bf16[2,16,48,128]{3,2,1,0:T(8,128)(2,1)}, bf16[2,16,48,128...) custom-call(bf16[2,16,48,1536]{3,2,1,0:T(8,128)(2,1)} %get-tuple-ele, ...), custom_call_target="tpu_custom_call", output_to_operand_aliasing={{0}: (0, {}), {1}: (1, {}), {2}: (2, {}), {3}: (3, {}), {4}... | custom-call | tf_op jit(solution)/shard_map/carry_one/pallas_call | solution.py:428
  151.1 48.5 %project_x.1 = (f32[1024,1536]{1,0:T(8,128)}, f32[1024,1536]{1,0:T(8,128)}, f32[16,1536]{1,0:T(8,128)}, f32[16,1536]{1,0:T(8,128)}, f32[1024,128]{1,0:T(8,128)},...) custom-call(bf16[1024,1536]{1,0:T(8,128)(2,1)} %get-tuple-element.26, ...), custom_call_target="tpu_custom_call", output_to_operand_aliasing={{6}: (8, {}), {7}: (9, {}), {8}: (10, {}), {9}: (11, {})} | custom-call | flops 9663676416 | bytes 12582912 | tf_op jit(solution)/shard_map/project_x/pallas_call | solution.py:428
  199.7 47.0 %conv_state0.1 = (f32[1024,1536]{1,0:T(8,128)}, f32[16,1536]{1,0:T(8,128)}, f32[1024,128]{1,0:T(8,128)}, f32[1024,128]{1,0:T(8,128)}, f32[1024,128]{1,0:T(8,128)...) custom-call(f32[1024,1536]{1,0:T(8,128)} %get-tuple-element.284.refs, ...), custom_call_target="tpu_custom_call", output_to_operand_aliasing={{5}: (8, {}), {6}: (9, {}), {7}: (10, {}), {8}: (11, {}), {... | custom-call | flops 7864320000 | bytes 6291456 | tf_op jit(solution)/shard_map/conv_state0/pallas_call | solution.py:428
  246.7 40.1 %conv_state1.1 = (f32[1024,1536]{1,0:T(8,128)}, f32[16,1536]{1,0:T(8,128)}, f32[1024,128]{1,0:T(8,128)}, f32[1024,128]{1,0:T(8,128)}, f32[1024,128]{1,0:T(8,128)...) custom-call(f32[1024,1536]{1,0:T(8,128)} %get-tuple-element.296.refs, ...), custom_call_target="tpu_custom_call", output_to_operand_aliasing={{5}: (8, {}), {6}: (9, {}), {7}: (10, {}), {8}: (11, {})} | custom-call | flops 7864320000 | bytes 6291456 | tf_op jit(solution)/shard_map/conv_state1/pallas_call | solution.py:428
  289.7 43.8 %project_z.1 = (f32[1024,1536]{1,0:T(8,128)}, f32[1024,1536]{1,0:T(8,128)}, bf16[2,16,48,2048]{3,2,1,0:T(8,128)(2,1)}, bf16[2,16,48,2048]{3,2,1,0:T(8,128)(2,1)}...) custom-call(bf16[1024,1536]{1,0:T(8,128)(2,1)} %get-tuple-element.26, ...), custom_call_target="tpu_custom_call", output_to_operand_aliasing={{2}: (4, {}), {3}: (5, {}), {4}: (6, {}), {5}: (7, {}), {6}... | custom-call | flops 9663676416 | bytes 12582912 | tf_op jit(solution)/shard_map/project_z/pallas_call | solution.py:428
  335.1 39.6 %scan_forward0.1 = (bf16[1024,1536]{1,0:T(8,128)(2,1)}, f32[1024,1536]{1,0:T(8,128)}, f32[128,1536]{1,0:T(8,128)}, bf16[2,16,48,2048]{3,2,1,0:T(8,128)(2,1)}, bf16[2,16,48,2048]{3,2,1,0:T(8,128)(2,1)}) custom-call(f32[1024,1536]{1,0:T(8,128)} %get-tuple-element.293.refs_0_, ...), custom_call_target="tpu_custom_call", output_to_operand_aliasing={{3}: (8, {}), {4}: (9, {})} | custom-call | flops 15728640000 | bytes 12582912 | tf_op jit(solution)/shard_map/scan_forward0/pallas_call | solution.py:428
  374.8 38.9 %scan_forward1.1 = (bf16[1024,1536]{1,0:T(8,128)(2,1)}, f32[1024,1536]{1,0:T(8,128)}, f32[128,1536]{1,0:T(8,128)}, bf16[2,16,48,2048]{3,2,1,0:T(8,128)(2,1)}, bf...) custom-call(f32[1024,1536]{1,0:T(8,128)} %get-tuple-element.319.refs, ...), custom_call_target="tpu_custom_call", output_to_operand_aliasing={{3}: (8, {}), {4}: (9, {}), {5}: (10, {}), {6}: (11, {})} | custom-call | flops 15728640000 | bytes 12582912 | tf_op jit(solution)/shard_map/scan_forward1/pallas_call | solution.py:428
  413.7 15.9 %project_out.1 = (f32[1024,1536]{1,0:T(8,128)}, bf16[2,16,48,2048]{3,2,1,0:T(8,128)(2,1)}, bf16[2,16,48,2048]{3,2,1,0:T(8,128)(2,1)}) custom-call(bf16[1024,1536]{1,0:T(8,128)(2,1)} %get-tuple-element.317.refs_0_.refs_1_, bf16[1536,1536]{1,0:T(8,128)(2,1)} %bitcast.332, ...), custom_call_target="tpu_custom_call", output_to_operand_aliasing={{1}: (4, {}), {2}: (5, {})} | custom-call | flops 9663676416 | bytes 6291456 | tf_op jit(solution)/shard_map/project_out/pallas_call | solution.py:428
  441.0 52.7 %feed_forward.1 = (bf16[1024,2048]{1,0:T(8,128)(2,1)}, bf16[1024,2048]{1,0:T(8,128)(2,1)}, bf16[1024,2048]{1,0:T(8,128)(2,1)}, bf16[1024,2048]{1,0:T(8,128)(2,1)...) custom-call(bf16[1024,1536]{1,0:T(8,128)(2,1)} %get-tuple-element.334.n_ref, ...), custom_call_target="tpu_custom_call" | custom-call | flops 38654705664 | bytes 25165824 | tf_op jit(solution)/shard_map/feed_forward/pallas_call | solution.py:370
  493.8 20.4 %down_grad.1 = (bf16[1536,2048]{1,0:T(8,128)(2,1)}, bf16[1536,2048]{1,0:T(8,128)(2,1)}) custom-call(bf16[1536,1024]{1,0:T(8,128)(2,1)} %get-tuple-element.344.refs_0_.refs_2_, bf16[1024,2048]{1,0:T(8,128)(2,1)} %get-tuple-element.342.refs_1_.refs_0_, bf16[1536,1024]{1,0:T(8,128)(2,1)} %get-tuple-element.344.refs_0_.refs_2_, ...), custom_call_target="tpu_custom_call" | custom-call | flops 12884901888 | bytes 25165824 | tf_op jit(solution)/shard_map/down_grad/pallas_call | solution.py:370
  514.2 21.3 %gate_grad.1 = (bf16[1536,2048]{1,0:T(8,128)(2,1)}, bf16[1536,2048]{1,0:T(8,128)(2,1)}, bf16[2,8,48,1024]{3,2,1,0:T(8,128)(2,1)}, bf16[2,8,48,1024]{3,2,1,0:T(8,...) custom-call(bf16[1536,1024]{1,0:T(8,128)(2,1)} %get-tuple-element.346.refs_0_.refs_2_, ...), custom_call_target="tpu_custom_call" | custom-call | flops 12884901888 | bytes 25165824 | tf_op jit(solution)/shard_map/gate_grad/pallas_call | solution.py:428
  543.4 26.0 %up_grad.1 = (bf16[1536,2048]{1,0:T(8,128)(2,1)}, bf16[1536,2048]{1,0:T(8,128)(2,1)}, bf16[4,48,1024]{2,1,0:T(8,128)(2,1)}, bf16[4,48,1024]{2,1,0:T(8,128)(2,1)}...) custom-call(bf16[1536,1024]{1,0:T(8,128)(2,1)} %get-tuple-element.34, ...), custom_call_target="tpu_custom_call" | custom-call | flops 12884901888 | bytes 25165824 | tf_op jit(solution)/shard_map/up_grad/pallas_call | solution.py:428
  573.4 34.7 %project_down.1 = (f32[1024,1536]{1,0:T(8,128)}, bf16[4,48,1024]{2,1,0:T(8,128)(2,1)}, bf16[4,48,1024]{2,1,0:T(8,128)(2,1)}, bf16[8,48,1024]{2,1,0:T(8,128)(2,1)...) custom-call(bf16[1024,2048]{1,0:T(8,128)(2,1)} %get-tuple-element.34, ...), custom_call_target="tpu_custom_call" | custom-call | flops 12884901888 | bytes 6291456 | tf_op jit(solution)/shard_map/project_down/pallas_call | solution.py:428
  622.4 53.7 %two_back.1 = (f32[1024,1536]{1,0:T(8,128)}, bf16[4,48,1024]{2,1,0:T(8,128)(2,1)}, bf16[4,48,1024]{2,1,0:T(8,128)(2,1)}, bf16[8,48,1024]{2,1,0:T(8,128)(2,1)}, b...) custom-call(bf16[1024,2048]{1,0:T(8,128)(2,1)} %get-tuple-element.34, ...), custom_call_target="tpu_custom_call" | custom-call | flops 25769803776 | bytes 6291456 | tf_op jit(solution)/shard_map/two_back/pallas_call | solution.py:428
  688.6 20.0 %norm_two_back.1 = (bf16[1024,1536]{1,0:T(8,128)(2,1)}, bf16[1024,1536]{1,0:T(8,128)(2,1)}, f32[8,1536]{1,0:T(8,128)}, bf16[1536,1024]{1,0:T(8,128)(2,1)}, bf16[...) custom-call(f32[1024,1536]{1,0:T(8,128)} %get-tuple-element.333.refs, ...), custom_call_target="tpu_custom_call" | custom-call | flops 31457280 | bytes 25165824 | tf_op jit(solution)/shard_map/norm_two_back/pallas_call | solution.py:428
  722.1 25.6 %out_grad.1 = (bf16[1536,1536]{1,0:T(8,128)(2,1)}, bf16[1536,1536]{1,0:T(8,128)(2,1)}, bf16[4,48,1024]{2,1,0:T(8,128)(2,1)}, bf16[4,48,1024]{2,1,0:T(8,128)(2,1)...) custom-call(bf16[1536,1024]{1,0:T(8,128)(2,1)} %get-tuple-element.38, ...), custom_call_target="tpu_custom_call" | custom-call | flops 9663676416 | bytes 18874368 | tf_op jit(solution)/shard_map/out_grad/pallas_call | solution.py:428
  751.7 18.3 %gated_back.1 = (f32[1024,1536]{1,0:T(8,128)}, f32[1024,1536]{1,0:T(8,128)}, bf16[4,48,1024]{2,1,0:T(8,128)(2,1)}, bf16[4,48,1024]{2,1,0:T(8,128)(2,1)}, bf16[2,...) custom-call(bf16[1024,1536]{1,0:T(8,128)(2,1)} %get-tuple-element.379.refs_0_.refs_2_.refs_4_, ...), custom_call_target="tpu_custom_call" | custom-call | flops 9663676416 | bytes 12582912 | tf_op jit(solution)/shard_map/gated_back/pallas_call | solution.py:428
  778.7 20.9 %gate_backward0.1 = (f32[1024,1536]{1,0:T(8,128)}, bf16[1024,1536]{1,0:T(8,128)(2,1)}, f32[16,1536]{1,0:T(8,128)}, bf16[4,48,1024]{2,1,0:T(8,128)(2,1)}, bf16[4,...) custom-call(f32[1024,1536]{1,0:T(8,128)} %get-tuple-element.390.refs, ...), custom_call_target="tpu_custom_call" | custom-call | flops 7864320000 | bytes 15728640 | tf_op jit(solution)/shard_map/gate_backward0/pallas_call | solution.py:428
  802.0 13.3 %gate_backward1.1 = (f32[1024,1536]{1,0:T(8,128)}, bf16[1024,1536]{1,0:T(8,128)(2,1)}, f32[16,1536]{1,0:T(8,128)}) custom-call(f32[1024,1536]{1,0:T(8,128)} %get-tuple-element.400.gg_ref, f32[1024,1536]{1,0:T(8,128)} %get-tuple-element.320.refs_1_.z_ref, f32[1024,1536]{1,0:T(8,128)} %get-tuple-element.401.y_ref, ...), custom_call_target="tpu_custom_call" | custom-call | flops 7864320000 | bytes 15728640 | tf_op jit(solution)/shard_map/gate_backward1/pallas_call | solution.py:370
  820.1 25.5 %z_grad.1 = (bf16[1536,1536]{1,0:T(8,128)(2,1)}, bf16[1536,1536]{1,0:T(8,128)(2,1)}, bf16[2,48,1024]{2,1,0:T(8,128)(2,1)}, bf16[2,48,1024]{2,1,0:T(8,128)(2,1)}, bf16[2,48,1024]{2,1,0:T(8,128)(2,1)}) custom-call(bf16[1536,1024]{1,0:T(8,128)(2,1)} %get-tuple-element.363.refs_0_.refs_2_, bf16[1024,1536]{1,0:T(8,128)(2,1)} %get-tuple-element.403.refs_1_.refs_0_, ...), custom_call_target="tpu_custom_call" | custom-call | flops 9663676416 | bytes 18874368 | tf_op jit(solution)/shard_map/z_grad/pallas_call | solution.py:428
  848.6 54.4 %scan_backward1.1 = (bf16[1024,1536]{1,0:T(8,128)(2,1)}, f32[1024,128]{1,0:T(8,128)}, f32[8,1536]{1,0:T(8,128)}, f32[24,1536]{1,0:T(8,128)}, f32[8,128]{1,0:T(8,...) custom-call(f32[1024,1536]{1,0:T(8,128)} %get-tuple-element.319.refs, ...), custom_call_target="tpu_custom_call" | custom-call | flops 39321600000 | bytes 18874368 | tf_op jit(solution)/shard_map/scan_backward1/pallas_call | solution.py:428
  917.6 18.1 %x_grad1.1 = (bf16[1536,1536]{1,0:T(8,128)(2,1)}, bf16[4,48,1536]{2,1,0:T(8,128)(2,1)}, bf16[4,48,1536]{2,1,0:T(8,128)(2,1)}) custom-call(bf16[1536,1024]{1,0:T(8,128)(2,1)} %get-tuple-element.363.refs_0_.refs_2_, bf16[1024,1536]{1,0:T(8,128)(2,1)} %get-tuple-element.418.refs_1_, bf16[1536,16]{1,0:T(8,128)(2,1)} %multiply_convert_fusion.refs_2_, ...), custom_call_target="tpu_custom_call" | custom-call | flops 4907335680 | bytes 9437184 | tf_op jit(solution)/shard_map/x_grad1/pallas_call | solution.py:428
  936.9 17.7 %z_back.1 = (f32[1024,1536]{1,0:T(8,128)}, bf16[2,8,48,1536]{3,2,1,0:T(8,128)(2,1)}, bf16[4,48,1024]{2,1,0:T(8,128)(2,1)}, bf16[4,48,1024]{2,1,0:T(8,128)(2,1)}) custom-call(bf16[1024,1536]{1,0:T(8,128)(2,1)} %get-tuple-element.403.refs_1_.refs_0_, bf16[1536,1536]{1,0:T(8,128)(2,1)} %bitcast.321, bf16[1024,1536]{1,0:T(8,128)(2,1)} %get-tuple-element.404.refs_3_.refs_2_, ...), custom_call_target="tpu_custom_call" | custom-call | flops 9663676416 | bytes 6291456 | tf_op jit(solution)/shard_map/z_back/pallas_call | solution.py:428
  962.0 59.2 %scan_backward0.1 = (bf16[1024,1536]{1,0:T(8,128)(2,1)}, f32[1024,128]{1,0:T(8,128)}, f32[8,1536]{1,0:T(8,128)}, f32[24,1536]{1,0:T(8,128)}, f32[8,128]{1,0:T(8,...) custom-call(f32[1024,1536]{1,0:T(8,128)} %get-tuple-element.293.refs, ...), custom_call_target="tpu_custom_call" | custom-call | flops 39321600000 | bytes 18874368 | tf_op jit(solution)/shard_map/scan_backward0/pallas_call | solution.py:428
  1033.8 26.0 %x_grad0.1 = (bf16[1536,1536]{1,0:T(8,128)(2,1)}, bf16[4,48,1536]{2,1,0:T(8,128)(2,1)}, bf16[4,48,1536]{2,1,0:T(8,128)(2,1)}) custom-call(bf16[1536,1024]{1,0:T(8,128)(2,1)} %get-tuple-element.363.refs_0_.refs_2_, bf16[1024,1536]{1,0:T(8,128)(2,1)} %get-tuple-element.432.refs_1_, bf16[1536,16]{1,0:T(8,128)(2,1)} %multiply_convert_fusion.refs_2_, ...), custom_call_target="tpu_custom_call" | custom-call | flops 4907335680 | bytes 9437184 | tf_op jit(solution)/shard_map/x_grad0/pallas_call | solution.py:428
  1073.7 35.7 %x_back.1 = (f32[1024,1536]{1,0:T(8,128)}, bf16[2,8,48,1536]{3,2,1,0:T(8,128)(2,1)}, bf16[4,48,1536]{2,1,0:T(8,128)(2,1)}, bf16[2,8,48,128]{3,2,1,0:T(8,128)(2,1...) custom-call(bf16[1024,1536]{1,0:T(8,128)(2,1)} %get-tuple-element.51, ...), custom_call_target="tpu_custom_call" | custom-call | flops 10468982784 | bytes 6291456 | tf_op jit(solution)/shard_map/x_back/pallas_call | solution.py:428
  1115.1 26.0 %norm_one_back.1 = (bf16[1024,1536]{1,0:T(8,128)(2,1)}, bf16[1024,1536]{1,0:T(8,128)(2,1)}, f32[8,1536]{1,0:T(8,128)}, bf16[1536,1024]{1,0:T(8,128)(2,1)}, bf16[...) custom-call(f32[1024,1536]{1,0:T(8,128)} %get-tuple-element.264.refs_0_, ...), custom_call_target="tpu_custom_call" | custom-call | flops 31457280 | bytes 25165824 | tf_op jit(solution)/shard_map/norm_one_back/pallas_call | solution.py:428
  1148.1 38.6 %turn_out.1 = (bf16[1024,1536]{1,0:T(8,128)(2,1)}, bf16[4,48,1536]{2,1,0:T(8,128)(2,1)}, bf16[4,48,1536]{2,1,0:T(8,128)(2,1)}, bf16[4,48,128]{2,1,0:T(8,128)(2,1)}, bf16[4,48,128]{2,1,0:T(8,128)(2,1)}) custom-call(bf16[1024,1536]{1,0:T(8,128)(2,1)} %add_convert_fusion.refs_0_, bf16[1536,1536]{1,0:T(8,128)(2,1)} %fusion.1.refs_1_.refs_3_, ...), custom_call_target="tpu_custom_call" | custom-call | flops 4831838208 | bytes 6291456 | tf_op jit(solution)/shard_map/turn_out/pallas_call | solution.py:428
  1193.8 42.5 %turn_back.1 = (f32[1024,1536]{1,0:T(8,128)}, bf16[2,48,1536]{2,1,0:T(8,128)(2,1)}, bf16[2,48,1536]{2,1,0:T(8,128)(2,1)}, bf16[2,48,1536]{2,1,0:T(8,128)(2,1)}, ...) custom-call(bf16[1024,1536]{1,0:T(8,128)(2,1)} %get-tuple-element.455.refs_0_, ...), custom_call_target="tpu_custom_call" | custom-call | flops 9663676416 | bytes 6291456 | tf_op jit(solution)/shard_map/turn_back/pallas_call | solution.py:428
  (517 shorter events, 221.4 us)
Async XLA Ops:
  1.5 146.1 %collective-permute-start = (bf16[16,1536]{1,0:T(8,128)(2,1)S(1)}, bf16[16,1536]{1,0:T(8,128)(2,1)S(1)}, u32[]{:S(2)}, u32[]{:S(2)}) collective-permute-start(bf16[16,1536]{1,0:T(8,128)(2,1)S(1)} %slice.443), channel_id=1, source_target_pairs={{0,1},{2,3},{4,5},{6,7},{8,9},{10,11},{12,13},{14,15},{16,17},{18,... | collective-permute-start | bytes 147464 | tf_op jit(solution)/shard_map/ppermute | solution.py:937
  10.0 139.2 %collective-permute-start.1 = (f32[8,1536]{1,0:T(8,128)S(1)}, f32[8,1536]{1,0:T(8,128)S(1)}, u32[]{:S(2)}, u32[]{:S(2)}) collective-permute-start(f32[8,1536]{1,0:T(8,128)S(1)} %select_maximum_fusion.refs_3_.refs_7_.refs_5_), channel_id=1, source_target_pairs={{0,1},{1,0},{2,3},{3,2},{4,5},{5,4},{6,7},{7,6},{8,9},{9,8},{10,11... | collective-permute-start | bytes 147464 | tf_op jit(solution)/shard_map/ppermute | solution.py:890
  149.2 50.5 %copy-start.111 = (f32[8,1536]{1,0:T(8,128)}, f32[8,1536]{1,0:T(8,128)S(1)}, u32[]{:S(2)}) copy-start(f32[8,1536]{1,0:T(8,128)S(1)} %collective-permute-done.1.refs_3_.refs_7_.refs_5_) | copy-start | bytes 147460
  246.7 40.1 %copy-start.109 = (f32[16,1536]{1,0:T(8,128)S(1)}, f32[16,1536]{1,0:T(8,128)}, u32[]{:S(2)}) copy-start(f32[16,1536]{1,0:T(8,128)} %get-tuple-element.313) | copy-start | bytes 294916
  287.7 46.7 %collective-permute-start.2 = (f32[2,16,1536]{2,1,0:T(8,128)S(1)}, f32[2,16,1536]{2,1,0:T(8,128)S(1)}, u32[]{:S(2)}, u32[]{:S(2)}) collective-permute-start(f32[2,16,1536]{2,1,0:T(8,128)S(1)} %pad_maximum_fusion.3), channel_id=1, source_target_pairs={{0,1},{2,3},{4,5},{6,7},{8,9},{10,11},{12,13},{14,15},{16,17},{18,... | collective-permute-start | bytes 589832 | tf_op jit(solution)/shard_map/ppermute | solution.py:980
  622.4 60.8 %slice-start.2 = ((s8[6291456]{0:T(1024)(128)(4,1)}), s8[4194304]{0:T(1024)(128)(4,1)S(1)}, s32[]{:S(2)}) async-start(s8[6291456]{0:T(1024)(128)(4,1)} %bitcast.348), calls=%async_computation.2 | async-start | bytes 8388608
  622.4 60.8 %slice-start.3 = ((s8[6291456]{0:T(1024)(128)(4,1)}), s8[2097152]{0:T(1024)(128)(4,1)S(1)}, s32[]{:S(2)}) async-start(s8[6291456]{0:T(1024)(128)(4,1)} %bitcast.348), calls=%async_computation.3 | async-start | bytes 4194304
  816.2 31.7 %collective-permute-start.3 = (f32[2,16,1536]{2,1,0:T(8,128)S(1)}, f32[2,16,1536]{2,1,0:T(8,128)S(1)}, u32[]{:S(2)}, u32[]{:S(2)}) collective-permute-start(f32[2,16,1536]{2,1,0:T(8,128)S(1)} %pad_maximum_fusion.4), channel_id=1, source_target_pairs={{1,0},{3,2},{5,4},{7,6},{9,8},{11,10},{13,12},{15,14},{17,16},{19,... | collective-permute-start | bytes 589832 | tf_op jit(solution)/shard_map/ppermute | solution.py:1018
  846.9 63.7 %slice-start.6 = ((s8[4718592]{0:T(1024)(128)(4,1)}), s8[4194304]{0:T(1024)(128)(4,1)S(1)}, s32[]{:S(2)}) async-start(s8[4718592]{0:T(1024)(128)(4,1)} %bitcast.378), calls=%async_computation.6 | async-start | bytes 8388608
  848.6 62.1 %slice-start.7 = ((s8[4718592]{0:T(1024)(128)(4,1)}), s8[524288]{0:T(1024)(128)(4,1)S(1)}, s32[]{:S(2)}) async-start(s8[4718592]{0:T(1024)(128)(4,1)} %bitcast.378), calls=%async_computation.7 | async-start | bytes 1048576
  962.0 59.3 %copy-start.112 = (f32[4,1536]{1,0:T(4,128)S(1)}, f32[4,1536]{1,0:T(4,128)}, u32[]{:S(2)}) copy-start(f32[4,1536]{1,0:T(4,128)} %param.27) | copy-start | bytes 73732
  962.0 61.9 %copy-start.114 = (f32[8,1536]{1,0:T(8,128)S(1)}, f32[8,1536]{1,0:T(8,128)}, u32[]{:S(2)}) copy-start(f32[8,1536]{1,0:T(8,128)} %get-tuple-element.477) | copy-start | bytes 147460
  1030.1 42.1 %collective-permute-start.4 = (f32[2,16,1536]{2,1,0:T(8,128)}, f32[2,16,1536]{2,1,0:T(8,128)S(1)}, u32[]{:S(2)}, u32[]{:S(2)}) collective-permute-start(f32[2,16,1536]{2,1,0:T(8,128)} %pad_maximum_fusion.5), channel_id=1, source_target_pairs={{1,0},{3,2},{5,4},{7,6},{9,8},{11,10},{13,12},{15,14},{17,16},{19,... | collective-permute-start | bytes 589832 | tf_op jit(solution)/shard_map/ppermute | solution.py:1047
  1070.0 39.4 %slice-start.8 = ((s8[4718592]{0:T(1024)(128)(4,1)}), s8[4194304]{0:T(1024)(128)(4,1)S(1)}, s32[]{:S(2)}) async-start(s8[4718592]{0:T(1024)(128)(4,1)} %bitcast.390), calls=%async_computation.8 | async-start | bytes 8388608
  1144.4 92.0 %collective-permute-start.5 = (f32[1536]{0:T(1024)S(1)}, f32[1536]{0:T(1024)S(1)}, u32[]{:S(2)}, u32[]{:S(2)}) collective-permute-start(f32[1536]{0:T(1024)S(1)} %reshape.648), channel_id=1, source_target_pairs={{0,1},{1,0},{2,3},{3,2},{4,5},{5,4},{6,7},{7,6},{8,9},{9,8},{10,11... | collective-permute-start | bytes 18440 | tf_op jit(solution)/shard_map/ppermute | solution.py:890
  1145.9 90.6 %collective-permute-start.10 = (f32[11008]{0:T(1024)S(1)}, f32[11008]{0:T(1024)S(1)}, u32[]{:S(2)}, u32[]{:S(2)}) collective-permute-start(f32[11008]{0:T(1024)S(1)} %pad_maximum_fusion.8), channel_id=1, source_target_pairs={{0,1},{1,0},{2,3},{3,2},{4,5},{5,4},{6,7},{7,6},{8,9},{9,8},{10,11... | collective-permute-start | bytes 132104 | tf_op jit(solution)/shard_map/ppermute | solution.py:890
  1148.1 40.2 %copy-start.15 = (bf16[8,48,1536]{2,1,0:T(8,128)(2,1)S(1)}, bf16[8,48,1536]{2,1,0:T(8,128)(2,1)}, u32[]{:S(2)}) copy-start(bf16[8,48,1536]{2,1,0:T(8,128)(2,1)} %fusion.3.refs_3_) | copy-start | bytes 3538948
  1148.1 42.2 %copy-start.116 = (bf16[4,48,128]{2,1,0:T(8,128)(2,1)S(1)}, bf16[4,48,128]{2,1,0:T(8,128)(2,1)}, u32[]{:S(2)}) copy-start(bf16[4,48,128]{2,1,0:T(8,128)(2,1)} %get-tuple-element.460) | copy-start | bytes 147460
  1193.8 42.7 %copy-start.106 = (f32[9216]{0:T(1024)S(1)}, f32[9216]{0:T(1024)}, u32[]{:S(2)}) copy-start(f32[9216]{0:T(1024)} %reshape.652) | copy-start | bytes 110596
  1193.8 43.3 %slice-start.11 = ((bf16[4,48,1536]{2,1,0:T(8,128)(2,1)}), bf16[1,48,1536]{2,1,0:T(8,128)(2,1)S(1)}, s32[]{:S(2)}) async-start(bf16[4,48,1536]{2,1,0:T(8,128)(2,1)} %copy-done.41), calls=%async_computation.11 | async-start | bytes 294912 | tf_op jit(solution)/shard_map/slice | solution.py:712
  1193.8 43.3 %slice-start.13 = ((bf16[4,48,1536]{2,1,0:T(8,128)(2,1)}), bf16[1,48,1536]{2,1,0:T(8,128)(2,1)S(1)}, s32[]{:S(2)}) async-start(bf16[4,48,1536]{2,1,0:T(8,128)(2,1)} %copy-done.42), calls=%async_computation.13 | async-start | bytes 294912 | tf_op jit(solution)/shard_map/slice | solution.py:712
  1193.8 43.3 %copy-start.74 = (bf16[2,48,1536]{2,1,0:T(8,128)(2,1)S(1)}, bf16[2,48,1536]{2,1,0:T(8,128)(2,1)}, u32[]{:S(2)}) copy-start(bf16[2,48,1536]{2,1,0:T(8,128)(2,1)} %get-tuple-element.468) | copy-start | bytes 884740
  1193.8 43.3 %copy-start.75 = (bf16[2,48,1536]{2,1,0:T(8,128)(2,1)S(1)}, bf16[2,48,1536]{2,1,0:T(8,128)(2,1)}, u32[]{:S(2)}) copy-start(bf16[2,48,1536]{2,1,0:T(8,128)(2,1)} %get-tuple-element.469) | copy-start | bytes 884740
  1193.8 43.3 %copy-start.76 = (bf16[2,48,1536]{2,1,0:T(8,128)(2,1)S(1)}, bf16[2,48,1536]{2,1,0:T(8,128)(2,1)}, u32[]{:S(2)}) copy-start(bf16[2,48,1536]{2,1,0:T(8,128)(2,1)} %get-tuple-element.470) | copy-start | bytes 884740
  1236.4 1.7 collective-permute-start.6
  1236.5 3.0 collective-permute-start.11
  1238.1 3.7 collective-permute-start.7
  1239.6 4.1 collective-permute-start.12
  1241.7 3.7 collective-permute-start.8
  1243.7 4.1 collective-permute-start.13
  1245.5 5.4 collective-permute-start.9
  1247.8 5.5 collective-permute-start.14
  (134 other events, 1335.7 us)

commit v4 on v3

--- a/solution.py
+++ b/solution.py
@@ -313,8 +313,8 @@
     turned_ref[...] = normed.T.astype(bf16)
 
 
-def norm_back_kernel(n_grads, rows_ref, gain_ref, *refs):
-    *given, high_ref, low_ref, part_ref, turned_ref = refs
+def norm_back_kernel(n_grads, n_given, rows_ref, gain_ref, *refs):
+    given, (high_ref, low_ref, part_ref), turned_refs = refs[:n_given], refs[n_given : n_given + 3], refs[n_given + 3 :]
 
     @pl.when(pl.program_id(0) == 0)
     def _():
@@ -333,7 +333,8 @@
     high = total.astype(bf16)
     high_ref[...] = high
     low_ref[...] = (total - high.astype(f32)).astype(bf16)
-    turned_ref[...] = total.T.astype(bf16)
+    for r in turned_refs:
+        r[...] = total.T.astype(bf16)
 
 
 def flip(i, mask):
@@ -389,7 +390,7 @@
         mine, (send, recv) = rest[:n_scratch], rest[n_scratch:]
 
         def device(route):
-            return {route[0]: flip(lax.axis_index(route[0]), route[1])}
+            return {axis: flip(lax.axis_index(axis), mask) for axis, mask in zip(route[::2], route[1::2])}
 
         def make(i, c):
             src, dst = held[c[0]].at[c[1]], held[c[2]].at[c[3]]
@@ -564,6 +565,37 @@
                 total = total + got[f"{k}r{m}"].astype(f32)
             self.out = total.reshape(self.rows, self.cols)
         self.phase += 1
+
+
+class SumAll:
+    def __init__(self, key, own, other, n):
+        self.key, self.n, self.phase, self.size = key, n, 0, own.shape[0]
+        rows = -(-self.size // 1024) * 8
+        self.own, self.other = (jnp.pad(v, (0, rows * 128 - self.size)).reshape(rows, 128) for v in (own, other))
+
+    def moves(self):
+        k = self.key
+        new = jax.ShapeDtypeStruct(self.own.shape, f32)
+        if self.phase == 0:
+            reads = {k + "v": self.own, k + "w": self.other}
+            steps = [(m % 4, m // 4) for m in range(1, 8)]
+            routes = [(("fsdp", f) if f else ()) + (("tp", t) if t else ()) for f, t in steps]
+            sources = [k + ("w" if t else "v") for f, t in steps]
+        else:
+            reads, routes = {k + "v": self.own}, [("fsdp", m << 2) for m in range(1, self.n // 4)]
+            sources = [k + "v"] * len(routes)
+        names = [f"{k}r{i}" for i in range(len(routes))]
+        copies = [(a, ALL, b, ALL, c) for a, b, c in zip(sources, names, routes)]
+        return reads, {}, {b: new for b in names}, copies
+
+    def take(self, got):
+        count = 8 if self.phase == 0 else self.n // 4
+        terms = [self.own] + [got[f"{self.key}r{i}"] for i in range(count - 1)]
+        while len(terms) > 1:
+            terms = [a + b for a, b in zip(terms[::2], terms[1::2])]
+        self.own = terms[0]
+        self.phase += 1
+        self.out = self.own.reshape(-1)[: self.size]
 
 
 def feed_forward(normed, cot, gate_w, up_w, down_w):
@@ -850,25 +882,23 @@
     )
 
 
-def norm_back(grads, rows, gain_row, bases, name, load=None):
+def norm_back(grads, rows, gain_row, bases, name, load=None, transpose=False):
     tokens, width = rows.shape
     main, turned, one = norm_specs(width)
-    high, low, part, high_t = run(
-        functools.partial(norm_back_kernel, len(grads)),
+    high, low, part, *high_t = run(
+        functools.partial(norm_back_kernel, len(grads), len(grads) + len(bases)),
         (tokens // Q,),
         [main, one] + [main] * (len(grads) + len(bases)),
-        [main, main, pl.BlockSpec((8, width), lambda q: (0, 0)), turned],
-        [
-            shape((tokens, width), bf16), shape((tokens, width), bf16), shape((8, width), f32),
-            shape((width, tokens), bf16),
-        ],
+        [main, main, pl.BlockSpec((8, width), lambda q: (0, 0))] + [turned] * transpose,
+        [shape((tokens, width), bf16), shape((tokens, width), bf16), shape((8, width), f32)]
+        + [shape((width, tokens), bf16)] * transpose,
         [],
         [rows, gain_row, *grads, *bases],
         name,
         cost(tokens * width * 20, 16 * tokens * width),
         load,
     )
-    return high, low, high_t, part[0]
+    return high, low, part[0], *high_t
 
 
 def token_marks(seg, seg_before):
@@ -888,16 +918,6 @@
 
 def swap(x, axis, n, mask):
     return lax.ppermute(x, axis, [(i, i ^ mask) for i in range(n)])
-
-
-def sum_all(x, n, over_tp=False):
-    if over_tp:
-        x = x + swap(x, "tp", 2, 1)
-    bit = 1
-    while bit < n:
-        x = x + swap(x, "fsdp", n, bit)
-        bit *= 2
-    return x
 
 
 def bf_dot(a, b):
@@ -1004,8 +1024,8 @@
             [list(zip(gate_grads, G.full)) + list(zip(up_grads, U.full))], f32, 256, "two_back",
             Load(ga, gb, db, da), nt=True,
         )
-        mixed_grad, mixed_low, mixed_t, gain_two_part = norm_back(
-            [grad_two], hidden, gain_two, [cot_low], "norm_two_back", Load(ga, db)
+        mixed_grad, mixed_low, gain_two_part, mixed_t = norm_back(
+            [grad_two], hidden, gain_two, [cot_low], "norm_two_back", Load(ga, db), True
         )
 
         so = Scatter("o", matmul([[(mixed_t, v["gated"])] for v in saved], bf16, 512, "out_grad", Load(ua, ga)), n)
@@ -1043,14 +1063,12 @@
             [[(v["dz"], w) for v, w in zip(saved, Z.full)]], f32, 512, "z_back", Load(sx, ub), nt=True
         )
         back(0, Load(sz, sx, so, ub))
-        sx.given(x_gradient(0, Load(sz)))
+        sx.given(x_gradient(0, None))
         fixes = lax.ppermute(jnp.stack([v["fix"] for v in saved]), "tp", [(1, 0)])[::-1]
         own, other = ([v["cg"][:6].reshape(-1), v["hg"][:2].reshape(-1)] for v in saved)
         gain_two_part = to_global(gain_two_part)
         own, other = jnp.concatenate(own + [gain_two_part]), jnp.concatenate(other + [gain_two_part])
-        total = sum_all(own + swap(other, "tp", 2, 1), n)
-        cg, hg = total[: 6 * ch].reshape(6, ch), total[6 * ch : 6 * ch + 256].reshape(2, 128)
-        gain_two_total = total[6 * ch + 256 :]
+        smalls_sum = SumAll("p", own, other, n)
 
         shared = 0.5 * (saved[0]["de"] + saved[1]["de"])
         own_lane = jnp.arange(EXTRA)[None, :] < heads
@@ -1061,14 +1079,18 @@
             v["de"] = jnp.where(own_lane, v["de"], shared).astype(bf16)
         se = Scatter("e", matmul([[(normed_t, v["de"])] for v in saved], bf16, 128, "e_grad"), n)
         pairs = [(v["dx"], w) for v, w in zip(saved, X.full)] + [(v["de"], w) for v, w in zip(saved, E.full)]
-        (grad_x,) = matmul([pairs], f32, 512, "x_back", Load(sx, se, sz), nt=True)
-        high, low, _, gain_one_part = norm_back(
-            [grad_x, grad_z], rows_in, gain_one, [mixed_grad, mixed_low], "norm_one_back", Load(se)
+        (grad_x,) = matmul([pairs], f32, 512, "x_back", Load(sx, se, sz, smalls_sum), nt=True)
+        high, low, gain_one_part = norm_back(
+            [grad_x, grad_z], rows_in, gain_one, [mixed_grad, mixed_low], "norm_one_back", Load(se, smalls_sum)
         )
-        (layer_out,) = matmul([[(out_low, turn)]], bf16, 512, "turn_out", Load(sx, se), nt=True)
-        (input_grad,) = matmul([[(high, turn), (low, turn)]], f32, 512, "turn_back", Load(sx, se), nt=True)
-
-        gain_one_total = sum_all(to_global(gain_one_part), n, True)
+        gain_one_part = to_global(gain_one_part)
+        gain_sum = SumAll("q", gain_one_part, gain_one_part, n)
+        (layer_out,) = matmul([[(out_low, turn)]], bf16, 512, "turn_out", Load(sx, se, sz, gain_sum), nt=True)
+        (input_grad,) = matmul([[(high, turn), (low, turn)]], f32, 512, "turn_back", Load(sx, se, gain_sum), nt=True)
+
+        total = smalls_sum.out
+        cg, hg = total[: 6 * ch].reshape(6, ch), total[6 * ch : 6 * ch + 256].reshape(2, 128)
+        gain_one_total, gain_two_total = gain_sum.out, total[6 * ch + 256 :]
         dt_b_total, a_total = hg[0, :heads], hg[1, :heads]
         skip_total = jnp.sum(cg[5].reshape(heads, HEADDIM), axis=1)
         return (

time: 1270 us -> 1240 us (0.976)
  Pallas kernels: 1060 us -> 1030 us
    pallas_call x29 -> x28, Pallas kernels: 952 us -> 914 us  [run(): pl.pallas_call(kernel, name=name, grid=grid, in_specs=list(in_specs) + [h...]
    pallas_call x5 -> x6, Pallas kernels: 104 us -> 115 us  [run(): pl.pallas_call(body, name=name, grid=grid, in_specs=in_specs, out_specs=o...]
  transfers between devices with their start and end apart: 15 -> 5, of which waited for: 5 -> 0; matrix products, arithmetic and copies ran while one was open for 4% -> 3% of each run, Pallas kernels for 23% -> 16%
where the time goes in v4:
time: 1240 us; the launch traced here: 1230 us
  Pallas kernels  1030 us (83%)
  other arithmetic  143 us (12%)
  local copies, waits for them, and re-layouts  46.4 us (4%)
    pallas_call x28, Pallas kernels, run(): pl.pallas_call(kernel, name=name, grid=grid, in_specs=list(in_specs) + [h...  914 us
    pallas_call x6, Pallas kernels, run(): pl.pallas_call(body, name=name, grid=grid, in_specs=in_specs, out_specs=o...  115 us
    add x51, other arithmetic, low_sum(): return a + b  88.1 us
  transfers between devices with their start and end apart: 5, of which 0 were waited for; matrix products, arithmetic and copies ran while one was open for 3% of the time, Pallas kernels for 16%

profile of v4, /device:TPU:0, one launch (start us, length us, event | category | flops | bytes accessed | tf_op | source)
XLA Modules:
  0.0 1231.9 jit_solution(6706052876887790718)
XLA Ops:
  29.4 35.9 %turn_rows.1 = (f32[1024,1536]{1,0:T(8,128)}, bf16[2,16,48,1536]{3,2,1,0:T(8,128)(2,1)}, bf16[2,16,48,1536]{3,2,1,0:T(8,128)(2,1)}, bf16[2,16,48,128]{3,2,1,0:T(8,128)(2,1)}, bf16[2,16,48,128]{3,2,1,0:T(8,128)(2,1)}) custom-call(bf16[1024,1536]{1,0:T(8,128)(2,1)} %refs_0_.2, bf16[1536,1536]{1,0:T(8,128)(2,1)} %fusion.1.refs_1_.refs_3_, ...), custom_call_target="tpu_custom_call" | custom-call | flops 4831838208 | bytes 6291456 | tf_op jit(solution)/shard_map/turn_rows/pallas_call | solution.py:429
  65.3 26.9 %norm_one.1 = (f32[1024,1536]{1,0:T(8,128)}, bf16[1024,1536]{1,0:T(8,128)(2,1)}, bf16[1536,1024]{1,0:T(8,128)(2,1)}, bf16[2,16,48,1536]{3,2,1,0:T(8,128)(2,1)}, ...) custom-call(f32[1024,1536]{1,0:T(8,128)} %get-tuple-element.278.refs, ...), custom_call_target="tpu_custom_call", output_to_operand_aliasing={{3}: (3, {}), {4}: (4, {}), {5}: (5, {}), {6}: (6, {})} | custom-call | flops 31457280 | bytes 18874368 | tf_op jit(solution)/shard_map/norm_one/pallas_call | solution.py:429
  92.3 35.6 %turn_cotangent.1 = (bf16[1024,1536]{1,0:T(8,128)(2,1)}, bf16[1536,1024]{1,0:T(8,128)(2,1)}, bf16[2,16,48,1536]{3,2,1,0:T(8,128)(2,1)}, bf16[2,16,48,1536]{3,2,1...) custom-call(bf16[1024,1536]{1,0:T(8,128)(2,1)} %refs_0_.3, ...), custom_call_target="tpu_custom_call", output_to_operand_aliasing={{2}: (3, {}), {3}: (4, {}), {4}: (5, {}), {5}: (6, {})} | custom-call | flops 4831838208 | bytes 6291456 | tf_op jit(solution)/shard_map/turn_cotangent/pallas_call | solution.py:429
  132.0 15.5 %carry_one.1 = (bf16[2,16,48,1536]{3,2,1,0:T(8,128)(2,1)}, bf16[2,16,48,1536]{3,2,1,0:T(8,128)(2,1)}, bf16[2,16,48,128]{3,2,1,0:T(8,128)(2,1)}, bf16[2,16,48,128...) custom-call(bf16[2,16,48,1536]{3,2,1,0:T(8,128)(2,1)} %get-tuple-ele, ...), custom_call_target="tpu_custom_call", output_to_operand_aliasing={{0}: (0, {}), {1}: (1, {}), {2}: (2, {}), {3}: (3, {}), {4}... | custom-call | tf_op jit(solution)/shard_map/carry_one/pallas_call | solution.py:429
  151.1 48.7 %project_x.1 = (f32[1024,1536]{1,0:T(8,128)}, f32[1024,1536]{1,0:T(8,128)}, f32[16,1536]{1,0:T(8,128)}, f32[16,1536]{1,0:T(8,128)}, f32[1024,128]{1,0:T(8,128)},...) custom-call(bf16[1024,1536]{1,0:T(8,128)(2,1)} %get-tuple-element.28, ...), custom_call_target="tpu_custom_call", output_to_operand_aliasing={{6}: (8, {}), {7}: (9, {}), {8}: (10, {}), {9}: (11, {})} | custom-call | flops 9663676416 | bytes 12582912 | tf_op jit(solution)/shard_map/project_x/pallas_call | solution.py:429
  199.8 47.0 %conv_state0.1 = (f32[1024,1536]{1,0:T(8,128)}, f32[16,1536]{1,0:T(8,128)}, f32[1024,128]{1,0:T(8,128)}, f32[1024,128]{1,0:T(8,128)}, f32[1024,128]{1,0:T(8,128)...) custom-call(f32[1024,1536]{1,0:T(8,128)} %get-tuple-element.303.refs, ...), custom_call_target="tpu_custom_call", output_to_operand_aliasing={{5}: (8, {}), {6}: (9, {}), {7}: (10, {}), {8}: (11, {}), {... | custom-call | flops 7864320000 | bytes 6291456 | tf_op jit(solution)/shard_map/conv_state0/pallas_call | solution.py:429
  246.8 40.1 %conv_state1.1 = (f32[1024,1536]{1,0:T(8,128)}, f32[16,1536]{1,0:T(8,128)}, f32[1024,128]{1,0:T(8,128)}, f32[1024,128]{1,0:T(8,128)}, f32[1024,128]{1,0:T(8,128)...) custom-call(f32[1024,1536]{1,0:T(8,128)} %get-tuple-element.315.refs, ...), custom_call_target="tpu_custom_call", output_to_operand_aliasing={{5}: (8, {}), {6}: (9, {}), {7}: (10, {}), {8}: (11, {})} | custom-call | flops 7864320000 | bytes 6291456 | tf_op jit(solution)/shard_map/conv_state1/pallas_call | solution.py:429
  289.7 43.8 %project_z.1 = (f32[1024,1536]{1,0:T(8,128)}, f32[1024,1536]{1,0:T(8,128)}, bf16[2,16,48,2048]{3,2,1,0:T(8,128)(2,1)}, bf16[2,16,48,2048]{3,2,1,0:T(8,128)(2,1)}...) custom-call(bf16[1024,1536]{1,0:T(8,128)(2,1)} %get-tuple-element.28, ...), custom_call_target="tpu_custom_call", output_to_operand_aliasing={{2}: (4, {}), {3}: (5, {}), {4}: (6, {}), {5}: (7, {}), {6}... | custom-call | flops 9663676416 | bytes 12582912 | tf_op jit(solution)/shard_map/project_z/pallas_call | solution.py:429
  335.3 39.6 %scan_forward0.1 = (bf16[1024,1536]{1,0:T(8,128)(2,1)}, f32[1024,1536]{1,0:T(8,128)}, f32[128,1536]{1,0:T(8,128)}, bf16[2,16,48,2048]{3,2,1,0:T(8,128)(2,1)}, bf16[2,16,48,2048]{3,2,1,0:T(8,128)(2,1)}) custom-call(f32[1024,1536]{1,0:T(8,128)} %get-tuple-element.312.refs_0_, ...), custom_call_target="tpu_custom_call", output_to_operand_aliasing={{3}: (8, {}), {4}: (9, {})} | custom-call | flops 15728640000 | bytes 12582912 | tf_op jit(solution)/shard_map/scan_forward0/pallas_call | solution.py:429
  374.9 38.8 %scan_forward1.1 = (bf16[1024,1536]{1,0:T(8,128)(2,1)}, f32[1024,1536]{1,0:T(8,128)}, f32[128,1536]{1,0:T(8,128)}, bf16[2,16,48,2048]{3,2,1,0:T(8,128)(2,1)}, bf...) custom-call(f32[1024,1536]{1,0:T(8,128)} %get-tuple-element.338.refs, ...), custom_call_target="tpu_custom_call", output_to_operand_aliasing={{3}: (8, {}), {4}: (9, {}), {5}: (10, {}), {6}: (11, {})} | custom-call | flops 15728640000 | bytes 12582912 | tf_op jit(solution)/shard_map/scan_forward1/pallas_call | solution.py:429
  413.7 15.8 %project_out.1 = (f32[1024,1536]{1,0:T(8,128)}, bf16[2,16,48,2048]{3,2,1,0:T(8,128)(2,1)}, bf16[2,16,48,2048]{3,2,1,0:T(8,128)(2,1)}) custom-call(bf16[1024,1536]{1,0:T(8,128)(2,1)} %get-tuple-element.336.refs_0_.refs_1_, bf16[1536,1536]{1,0:T(8,128)(2,1)} %bitcast.346, ...), custom_call_target="tpu_custom_call", output_to_operand_aliasing={{1}: (4, {}), {2}: (5, {})} | custom-call | flops 9663676416 | bytes 6291456 | tf_op jit(solution)/shard_map/project_out/pallas_call | solution.py:429
  429.6 11.5 norm_two.1
  441.1 52.7 %feed_forward.1 = (bf16[1024,2048]{1,0:T(8,128)(2,1)}, bf16[1024,2048]{1,0:T(8,128)(2,1)}, bf16[1024,2048]{1,0:T(8,128)(2,1)}, bf16[1024,2048]{1,0:T(8,128)(2,1)...) custom-call(bf16[1024,1536]{1,0:T(8,128)(2,1)} %get-tuple-element.353.n_ref, ...), custom_call_target="tpu_custom_call" | custom-call | flops 38654705664 | bytes 25165824 | tf_op jit(solution)/shard_map/feed_forward/pallas_call | solution.py:371
  493.8 20.5 %down_grad.1 = (bf16[1536,2048]{1,0:T(8,128)(2,1)}, bf16[1536,2048]{1,0:T(8,128)(2,1)}) custom-call(bf16[1536,1024]{1,0:T(8,128)(2,1)} %get-tuple-element.363.refs_0_.refs_2_, bf16[1024,2048]{1,0:T(8,128)(2,1)} %get-tuple-element.361.refs_1_.refs_0_, bf16[1536,1024]{1,0:T(8,128)(2,1)} %get-tuple-element.363.refs_0_.refs_2_, ...), custom_call_target="tpu_custom_call" | custom-call | flops 12884901888 | bytes 25165824 | tf_op jit(solution)/shard_map/down_grad/pallas_call | solution.py:371
  514.3 21.4 %gate_grad.1 = (bf16[1536,2048]{1,0:T(8,128)(2,1)}, bf16[1536,2048]{1,0:T(8,128)(2,1)}, bf16[2,8,48,1024]{3,2,1,0:T(8,128)(2,1)}, bf16[2,8,48,1024]{3,2,1,0:T(8,...) custom-call(bf16[1536,1024]{1,0:T(8,128)(2,1)} %get-tuple-element.365.refs_0_.refs_2_, ...), custom_call_target="tpu_custom_call" | custom-call | flops 12884901888 | bytes 25165824 | tf_op jit(solution)/shard_map/gate_grad/pallas_call | solution.py:429
  543.6 25.9 %up_grad.1 = (bf16[1536,2048]{1,0:T(8,128)(2,1)}, bf16[1536,2048]{1,0:T(8,128)(2,1)}, bf16[4,48,1024]{2,1,0:T(8,128)(2,1)}, bf16[4,48,1024]{2,1,0:T(8,128)(2,1)}...) custom-call(bf16[1536,1024]{1,0:T(8,128)(2,1)} %get-tuple-element.36, ...), custom_call_target="tpu_custom_call" | custom-call | flops 12884901888 | bytes 25165824 | tf_op jit(solution)/shard_map/up_grad/pallas_call | solution.py:429
  573.5 34.7 %project_down.1 = (f32[1024,1536]{1,0:T(8,128)}, bf16[4,48,1024]{2,1,0:T(8,128)(2,1)}, bf16[4,48,1024]{2,1,0:T(8,128)(2,1)}, bf16[8,48,1024]{2,1,0:T(8,128)(2,1)...) custom-call(bf16[1024,2048]{1,0:T(8,128)(2,1)} %get-tuple-element.36, ...), custom_call_target="tpu_custom_call" | custom-call | flops 12884901888 | bytes 6291456 | tf_op jit(solution)/shard_map/project_down/pallas_call | solution.py:429
  622.6 53.7 %two_back.1 = (f32[1024,1536]{1,0:T(8,128)}, bf16[4,48,1024]{2,1,0:T(8,128)(2,1)}, bf16[4,48,1024]{2,1,0:T(8,128)(2,1)}, bf16[8,48,1024]{2,1,0:T(8,128)(2,1)}, b...) custom-call(bf16[1024,2048]{1,0:T(8,128)(2,1)} %get-tuple-element.36, ...), custom_call_target="tpu_custom_call" | custom-call | flops 25769803776 | bytes 6291456 | tf_op jit(solution)/shard_map/two_back/pallas_call | solution.py:429
  688.8 20.0 %norm_two_back.1 = (bf16[1024,1536]{1,0:T(8,128)(2,1)}, bf16[1024,1536]{1,0:T(8,128)(2,1)}, f32[8,1536]{1,0:T(8,128)}, bf16[1536,1024]{1,0:T(8,128)(2,1)}, bf16[...) custom-call(f32[1024,1536]{1,0:T(8,128)} %get-tuple-element.352.refs, ...), custom_call_target="tpu_custom_call" | custom-call | flops 31457280 | bytes 25165824 | tf_op jit(solution)/shard_map/norm_two_back/pallas_call | solution.py:429
  725.1 25.6 %out_grad.1 = (bf16[1536,1536]{1,0:T(8,128)(2,1)}, bf16[1536,1536]{1,0:T(8,128)(2,1)}, bf16[4,48,1024]{2,1,0:T(8,128)(2,1)}, bf16[4,48,1024]{2,1,0:T(8,128)(2,1)...) custom-call(bf16[1536,1024]{1,0:T(8,128)(2,1)} %get-tuple-element.40, ...), custom_call_target="tpu_custom_call" | custom-call | flops 9663676416 | bytes 18874368 | tf_op jit(solution)/shard_map/out_grad/pallas_call | solution.py:429
  754.8 18.4 %gated_back.1 = (f32[1024,1536]{1,0:T(8,128)}, f32[1024,1536]{1,0:T(8,128)}, bf16[4,48,1024]{2,1,0:T(8,128)(2,1)}, bf16[4,48,1024]{2,1,0:T(8,128)(2,1)}, bf16[2,...) custom-call(bf16[1024,1536]{1,0:T(8,128)(2,1)} %get-tuple-element.398.refs_0_.refs_2_.refs_4_, ...), custom_call_target="tpu_custom_call" | custom-call | flops 9663676416 | bytes 12582912 | tf_op jit(solution)/shard_map/gated_back/pallas_call | solution.py:429
  781.8 20.9 %gate_backward0.1 = (f32[1024,1536]{1,0:T(8,128)}, bf16[1024,1536]{1,0:T(8,128)(2,1)}, f32[16,1536]{1,0:T(8,128)}, bf16[4,48,1024]{2,1,0:T(8,128)(2,1)}, bf16[4,...) custom-call(f32[1024,1536]{1,0:T(8,128)} %get-tuple-element.409.refs, ...), custom_call_target="tpu_custom_call" | custom-call | flops 7864320000 | bytes 15728640 | tf_op jit(solution)/shard_map/gate_backward0/pallas_call | solution.py:429
  805.1 13.3 %gate_backward1.1 = (f32[1024,1536]{1,0:T(8,128)}, bf16[1024,1536]{1,0:T(8,128)(2,1)}, f32[16,1536]{1,0:T(8,128)}) custom-call(f32[1024,1536]{1,0:T(8,128)} %get-tuple-element.419.gg_ref, f32[1024,1536]{1,0:T(8,128)} %get-tuple-element.339.refs_1_.z_ref, f32[1024,1536]{1,0:T(8,128)} %get-tuple-element.420.y_ref, ...), custom_call_target="tpu_custom_call" | custom-call | flops 7864320000 | bytes 15728640 | tf_op jit(solution)/shard_map/gate_backward1/pallas_call | solution.py:371
  822.0 25.5 %z_grad.1 = (bf16[1536,1536]{1,0:T(8,128)(2,1)}, bf16[1536,1536]{1,0:T(8,128)(2,1)}, bf16[2,48,1024]{2,1,0:T(8,128)(2,1)}, bf16[2,48,1024]{2,1,0:T(8,128)(2,1)}, bf16[2,48,1024]{2,1,0:T(8,128)(2,1)}) custom-call(bf16[1536,1024]{1,0:T(8,128)(2,1)} %get-tuple-element.382.refs_0_.refs_2_, bf16[1024,1536]{1,0:T(8,128)(2,1)} %get-tuple-element.422.refs_1_.refs_0_, ...), custom_call_target="tpu_custom_call" | custom-call | flops 9663676416 | bytes 18874368 | tf_op jit(solution)/shard_map/z_grad/pallas_call | solution.py:429
  850.5 54.4 %scan_backward1.1 = (bf16[1024,1536]{1,0:T(8,128)(2,1)}, f32[1024,128]{1,0:T(8,128)}, f32[8,1536]{1,0:T(8,128)}, f32[24,1536]{1,0:T(8,128)}, f32[8,128]{1,0:T(8,...) custom-call(f32[1024,1536]{1,0:T(8,128)} %get-tuple-element.338.refs, ...), custom_call_target="tpu_custom_call" | custom-call | flops 39321600000 | bytes 18874368 | tf_op jit(solution)/shard_map/scan_backward1/pallas_call | solution.py:429
  919.5 18.1 %x_grad1.1 = (bf16[1536,1536]{1,0:T(8,128)(2,1)}, bf16[4,48,1536]{2,1,0:T(8,128)(2,1)}, bf16[4,48,1536]{2,1,0:T(8,128)(2,1)}) custom-call(bf16[1536,1024]{1,0:T(8,128)(2,1)} %get-tuple-element.382.refs_0_.refs_2_, bf16[1024,1536]{1,0:T(8,128)(2,1)} %get-tuple-element.437.refs_1_, bf16[1536,16]{1,0:T(8,128)(2,1)} %multiply_convert_fusion.refs_2_, ...), custom_call_target="tpu_custom_call" | custom-call | flops 4907335680 | bytes 9437184 | tf_op jit(solution)/shard_map/x_grad1/pallas_call | solution.py:429
  938.8 17.7 %z_back.1 = (f32[1024,1536]{1,0:T(8,128)}, bf16[2,8,48,1536]{3,2,1,0:T(8,128)(2,1)}, bf16[4,48,1024]{2,1,0:T(8,128)(2,1)}, bf16[4,48,1024]{2,1,0:T(8,128)(2,1)}) custom-call(bf16[1024,1536]{1,0:T(8,128)(2,1)} %get-tuple-element.422.refs_1_.refs_0_, bf16[1536,1536]{1,0:T(8,128)(2,1)} %bitcast.335, bf16[1024,1536]{1,0:T(8,128)(2,1)} %get-tuple-element.423.refs_3_.refs_2_, ...), custom_call_target="tpu_custom_call" | custom-call | flops 9663676416 | bytes 6291456 | tf_op jit(solution)/shard_map/z_back/pallas_call | solution.py:429
  963.9 59.2 %scan_backward0.1 = (bf16[1024,1536]{1,0:T(8,128)(2,1)}, f32[1024,128]{1,0:T(8,128)}, f32[8,1536]{1,0:T(8,128)}, f32[24,1536]{1,0:T(8,128)}, f32[8,128]{1,0:T(8,...) custom-call(f32[1024,1536]{1,0:T(8,128)} %get-tuple-element.312.refs, ...), custom_call_target="tpu_custom_call" | custom-call | flops 39321600000 | bytes 18874368 | tf_op jit(solution)/shard_map/scan_backward0/pallas_call | solution.py:429
  1060.5 39.7 %x_back.1 = (f32[1024,1536]{1,0:T(8,128)}, bf16[2,8,48,1536]{3,2,1,0:T(8,128)(2,1)}, bf16[4,48,1536]{2,1,0:T(8,128)(2,1)}, bf16[2,8,48,128]{3,2,1,0:T(8,128)(2,1...) custom-call(bf16[1024,1536]{1,0:T(8,128)(2,1)} %get-tuple-element.55, ...), custom_call_target="tpu_custom_call" | custom-call | flops 10468982784 | bytes 6291456 | tf_op jit(solution)/shard_map/x_back/pallas_call | solution.py:429
  1105.0 17.7 %norm_one_back.1 = (bf16[1024,1536]{1,0:T(8,128)(2,1)}, bf16[1024,1536]{1,0:T(8,128)(2,1)}, f32[8,1536]{1,0:T(8,128)}, bf16[4,48,128]{2,1,0:T(8,128)(2,1)}, bf16...) custom-call(f32[1024,1536]{1,0:T(8,128)} %get-tuple-element.283.refs, ...), custom_call_target="tpu_custom_call" | custom-call | flops 31457280 | bytes 25165824 | tf_op jit(solution)/shard_map/norm_one_back/pallas_call | solution.py:429
  1138.5 35.1 %turn_out.1 = (bf16[1024,1536]{1,0:T(8,128)(2,1)}, bf16[4,48,1536]{2,1,0:T(8,128)(2,1)}, bf16[4,48,1536]{2,1,0:T(8,128)(2,1)}, bf16[4,48,128]{2,1,0:T(8,128)(2,1...) custom-call(bf16[1024,1536]{1,0:T(8,128)(2,1)} %add_convert_fusion.r, ...), custom_call_target="tpu_custom_call" | custom-call | flops 4831838208 | bytes 6291456 | tf_op jit(solution)/shard_map/turn_out/pallas_call | solution.py:429
  1179.4 37.7 %turn_back.1 = (f32[1024,1536]{1,0:T(8,128)}, bf16[2,48,1536]{2,1,0:T(8,128)(2,1)}, bf16[2,48,1536]{2,1,0:T(8,128)(2,1)}, bf16[2,48,1536]{2,1,0:T(8,128)(2,1)}, ...) custom-call(bf16[1024,1536]{1,0:T(8,128)(2,1)} %get-tuple-element.48, ...), custom_call_target="tpu_custom_call" | custom-call | flops 9663676416 | bytes 6291456 | tf_op jit(solution)/shard_map/turn_back/pallas_call | solution.py:429
  (492 shorter events, 217.3 us)
Async XLA Ops:
  1.5 146.0 %collective-permute-start = (bf16[16,1536]{1,0:T(8,128)(2,1)S(1)}, bf16[16,1536]{1,0:T(8,128)(2,1)S(1)}, u32[]{:S(2)}, u32[]{:S(2)}) collective-permute-start(bf16[16,1536]{1,0:T(8,128)(2,1)S(1)} %slice.435), channel_id=1, source_target_pairs={{0,1},{2,3},{4,5},{6,7},{8,9},{10,11},{12,13},{14,15},{16,17},{18,... | collective-permute-start | bytes 147464 | tf_op jit(solution)/shard_map/ppermute | solution.py:957
  10.0 139.2 %collective-permute-start.1 = (f32[8,1536]{1,0:T(8,128)S(1)}, f32[8,1536]{1,0:T(8,128)S(1)}, u32[]{:S(2)}, u32[]{:S(2)}) collective-permute-start(f32[8,1536]{1,0:T(8,128)S(1)} %select_maximum_fusion.refs_3_.refs_7_.refs_5_), channel_id=1, source_target_pairs={{0,1},{1,0},{2,3},{3,2},{4,5},{5,4},{6,7},{7,6},{8,9},{9,8},{10,11... | collective-permute-start | bytes 147464 | tf_op jit(solution)/shard_map/ppermute | solution.py:920
  149.2 50.6 %copy-start.105 = (f32[8,1536]{1,0:T(8,128)}, f32[8,1536]{1,0:T(8,128)S(1)}, u32[]{:S(2)}) copy-start(f32[8,1536]{1,0:T(8,128)S(1)} %collective-permute-done.1.refs_3_.refs_7_.refs_5_) | copy-start | bytes 147460
  246.8 40.1 %copy-start.103 = (f32[16,1536]{1,0:T(8,128)S(1)}, f32[16,1536]{1,0:T(8,128)}, u32[]{:S(2)}) copy-start(f32[16,1536]{1,0:T(8,128)} %get-tuple-element.332) | copy-start | bytes 294916
  287.8 46.8 %collective-permute-start.2 = (f32[2,16,1536]{2,1,0:T(8,128)S(1)}, f32[2,16,1536]{2,1,0:T(8,128)S(1)}, u32[]{:S(2)}, u32[]{:S(2)}) collective-permute-start(f32[2,16,1536]{2,1,0:T(8,128)S(1)} %pad_maximum_fusion.3), channel_id=1, source_target_pairs={{0,1},{2,3},{4,5},{6,7},{8,9},{10,11},{12,13},{14,15},{16,17},{18,... | collective-permute-start | bytes 589832 | tf_op jit(solution)/shard_map/ppermute | solution.py:1000
  543.6 27.9 %copy-start.10 = (bf16[2,8,48,1024]{3,2,1,0:T(8,128)(2,1)S(1)}, bf16[2,8,48,1024]{3,2,1,0:T(8,128)(2,1)}, u32[]{:S(2)}) copy-start(bf16[2,8,48,1024]{3,2,1,0:T(8,128)(2,1)} %get-tuple-element.550.refs_4_) | copy-start | bytes 4718596
  573.5 34.8 %copy-start.5 = (bf16[8,48,1024]{2,1,0:T(8,128)(2,1)S(1)}, bf16[8,48,1024]{2,1,0:T(8,128)(2,1)}, u32[]{:S(2)}) copy-start(bf16[8,48,1024]{2,1,0:T(8,128)(2,1)} %fusion.14.refs_7_) | copy-start | bytes 2359300
  573.5 38.0 %copy-start.71 = (bf16[4,48,1024]{2,1,0:T(8,128)(2,1)S(1)}, bf16[4,48,1024]{2,1,0:T(8,128)(2,1)}, u32[]{:S(2)}) copy-start(bf16[4,48,1024]{2,1,0:T(8,128)(2,1)} %get-tuple-element.389) | copy-start | bytes 1179652
  622.6 60.8 %slice-start.2 = ((s8[6291456]{0:T(1024)(128)(4,1)}), s8[4194304]{0:T(1024)(128)(4,1)S(1)}, s32[]{:S(2)}) async-start(s8[6291456]{0:T(1024)(128)(4,1)} %bitcast.362), calls=%async_computation.2 | async-start | bytes 8388608
  622.6 60.8 %slice-start.3 = ((s8[6291456]{0:T(1024)(128)(4,1)}), s8[2097152]{0:T(1024)(128)(4,1)S(1)}, s32[]{:S(2)}) async-start(s8[6291456]{0:T(1024)(128)(4,1)} %bitcast.362), calls=%async_computation.3 | async-start | bytes 4194304
  725.1 27.6 %copy-start.9 = (bf16[2,8,48,1024]{3,2,1,0:T(8,128)(2,1)S(1)}, bf16[2,8,48,1024]{3,2,1,0:T(8,128)(2,1)}, u32[]{:S(2)}) copy-start(bf16[2,8,48,1024]{3,2,1,0:T(8,128)(2,1)} %get-tuple-element.543.refs_4_) | copy-start | bytes 4718596
  819.4 30.4 %collective-permute-start.3 = (f32[2,16,1536]{2,1,0:T(8,128)S(1)}, f32[2,16,1536]{2,1,0:T(8,128)S(1)}, u32[]{:S(2)}, u32[]{:S(2)}) collective-permute-start(f32[2,16,1536]{2,1,0:T(8,128)S(1)} %pad_maximum_fusion.4), channel_id=1, source_target_pairs={{1,0},{3,2},{5,4},{7,6},{9,8},{11,10},{13,12},{15,14},{17,16},{19,... | collective-permute-start | bytes 589832 | tf_op jit(solution)/shard_map/ppermute | solution.py:1038
  821.9 25.7 %copy-start.89 = (bf16[2,48,1024]{2,1,0:T(8,128)(2,1)S(1)}, bf16[2,48,1024]{2,1,0:T(8,128)(2,1)}, u32[]{:S(2)}) copy-start(bf16[2,48,1024]{2,1,0:T(8,128)(2,1)} %get-tuple-element.522) | copy-start | bytes 589828
  821.9 25.8 %slice-start.20 = ((bf16[4,48,1024]{2,1,0:T(8,128)(2,1)}), bf16[1,48,1024]{2,1,0:T(8,128)(2,1)S(1)}, s32[]{:S(2)}) async-start(bf16[4,48,1024]{2,1,0:T(8,128)(2,1)} %copy-done.57), calls=%async_computation.20 | async-start | bytes 196608 | tf_op jit(solution)/shard_map/slice | solution.py:744
  821.9 25.8 %slice-start.21 = ((bf16[4,48,1024]{2,1,0:T(8,128)(2,1)}), bf16[1,48,1024]{2,1,0:T(8,128)(2,1)S(1)}, s32[]{:S(2)}) async-start(bf16[4,48,1024]{2,1,0:T(8,128)(2,1)} %copy-done.58), calls=%async_computation.21 | async-start | bytes 196608 | tf_op jit(solution)/shard_map/slice | solution.py:744
  822.0 25.8 %copy-start.93 = (bf16[2,48,1024]{2,1,0:T(8,128)(2,1)S(1)}, bf16[2,48,1024]{2,1,0:T(8,128)(2,1)}, u32[]{:S(2)}) copy-start(bf16[2,48,1024]{2,1,0:T(8,128)(2,1)} %get-tuple-element.523) | copy-start | bytes 589828
  822.0 25.8 %copy-start.94 = (bf16[2,48,1024]{2,1,0:T(8,128)(2,1)S(1)}, bf16[2,48,1024]{2,1,0:T(8,128)(2,1)}, u32[]{:S(2)}) copy-start(bf16[2,48,1024]{2,1,0:T(8,128)(2,1)} %get-tuple-element.524) | copy-start | bytes 589828
  822.0 25.8 %copy-start.95 = (bf16[2,48,1024]{2,1,0:T(8,128)(2,1)S(1)}, bf16[2,48,1024]{2,1,0:T(8,128)(2,1)}, u32[]{:S(2)}) copy-start(bf16[2,48,1024]{2,1,0:T(8,128)(2,1)} %get-tuple-element.525) | copy-start | bytes 589828
  848.8 63.7 %slice-start.6 = ((s8[4718592]{0:T(1024)(128)(4,1)}), s8[4194304]{0:T(1024)(128)(4,1)S(1)}, s32[]{:S(2)}) async-start(s8[4718592]{0:T(1024)(128)(4,1)} %bitcast.392), calls=%async_computation.6 | async-start | bytes 8388608
  850.5 62.1 %slice-start.7 = ((s8[4718592]{0:T(1024)(128)(4,1)}), s8[524288]{0:T(1024)(128)(4,1)S(1)}, s32[]{:S(2)}) async-start(s8[4718592]{0:T(1024)(128)(4,1)} %bitcast.392), calls=%async_computation.7 | async-start | bytes 1048576
  963.9 59.3 %copy-start.108 = (f32[4,1536]{1,0:T(4,128)S(1)}, f32[4,1536]{1,0:T(4,128)}, u32[]{:S(2)}) copy-start(f32[4,1536]{1,0:T(4,128)} %param.27) | copy-start | bytes 73732
  963.9 61.0 %copy-start.110 = (f32[1,1536]{1,0:T(1,128)S(1)}, f32[1,1536]{1,0:T(1,128)}, u32[]{:S(2)}) copy-start(f32[1,1536]{1,0:T(1,128)} %copy-done.109) | copy-start | bytes 18436
  963.9 61.0 %copy-start.123 = (f32[16]{0:T(128)S(1)}, f32[16]{0:T(128)}, u32[]{:S(2)}) copy-start(f32[16]{0:T(128)} %pad.69.clone) | copy-start | bytes 196
  1035.7 23.3 %collective-permute-start.4 = (f32[2,16,1536]{2,1,0:T(8,128)S(1)}, f32[2,16,1536]{2,1,0:T(8,128)S(1)}, u32[]{:S(2)}, u32[]{:S(2)}) collective-permute-start(f32[2,16,1536]{2,1,0:T(8,128)S(1)} %pad_maximum_fusion.5), channel_id=1, source_target_pairs={{1,0},{3,2},{5,4},{7,6},{9,8},{11,10},{13,12},{15,14},{17,16},{19,... | collective-permute-start | bytes 589832 | tf_op jit(solution)/shard_map/ppermute | solution.py:1067
  1060.5 39.7 %copy-start.101 = (bf16[1536,128]{1,0:T(8,128)(2,1)S(1)}, bf16[1536,128]{1,0:T(8,128)(2,1)}, u32[]{:S(2)}) copy-start(bf16[1536,128]{1,0:T(8,128)(2,1)} %get-tuple-element.456) | copy-start | bytes 1179652
  1060.5 41.4 %copy-start.100 = (bf16[1536,128]{1,0:T(8,128)(2,1)S(1)}, bf16[1536,128]{1,0:T(8,128)(2,1)}, u32[]{:S(2)}) copy-start(bf16[1536,128]{1,0:T(8,128)(2,1)} %get-tuple-element.457) | copy-start | bytes 1179652
  1138.5 35.1 %copy-start.80 = (bf16[8,48,128]{2,1,0:T(8,128)(2,1)S(1)}, bf16[8,48,128]{2,1,0:T(8,128)(2,1)}, u32[]{:S(2)}) copy-start(bf16[8,48,128]{2,1,0:T(8,128)(2,1)} %fusion.44.refs_5_) | copy-start | bytes 294916
  1138.5 36.0 %copy-start.15 = (bf16[8,48,1536]{2,1,0:T(8,128)(2,1)S(1)}, bf16[8,48,1536]{2,1,0:T(8,128)(2,1)}, u32[]{:S(2)}) copy-start(bf16[8,48,1536]{2,1,0:T(8,128)(2,1)} %fusion.3.refs_3_) | copy-start | bytes 3538948
  1179.3 37.7 %slice-start.22 = ((bf16[4,48,128]{2,1,0:T(8,128)(2,1)}), bf16[1,48,128]{2,1,0:T(8,128)(2,1)S(1)}, s32[]{:S(2)}) async-start(bf16[4,48,128]{2,1,0:T(8,128)(2,1)} %copy-done.106), calls=%async_computation.22 | async-start | bytes 24576 | tf_op jit(solution)/shard_map/slice | solution.py:744
  1179.3 40.1 %copy-start.114 = (f32[16,128]{1,0:T(8,128)S(1)}, f32[16,128]{1,0:T(8,128)}, u32[]{:S(2)}) copy-start(f32[16,128]{1,0:T(8,128)} %add_add_fusion.3.refs_8_) | copy-start | bytes 24580
  1179.3 43.7 %slice-start.9 = ((bf16[4,48,1536]{2,1,0:T(8,128)(2,1)}), bf16[1,48,1536]{2,1,0:T(8,128)(2,1)S(1)}, s32[]{:S(2)}) async-start(bf16[4,48,1536]{2,1,0:T(8,128)(2,1)} %copy-done.41), calls=%async_computation.9 | async-start | bytes 294912 | tf_op jit(solution)/shard_map/slice | solution.py:744
  1179.4 43.6 %slice-start.11 = ((bf16[4,48,1536]{2,1,0:T(8,128)(2,1)}), bf16[1,48,1536]{2,1,0:T(8,128)(2,1)S(1)}, s32[]{:S(2)}) async-start(bf16[4,48,1536]{2,1,0:T(8,128)(2,1)} %copy-done.45), calls=%async_computation.11 | async-start | bytes 294912 | tf_op jit(solution)/shard_map/slice | solution.py:744
  (122 other events, 962.9 us)

commit v5 on v4

--- a/solution.py
+++ b/solution.py
@@ -1033,10 +1033,10 @@
         for b in (0, 1):
             v = saved[b]
             v["dy"], v["dz"], v["ds"] = gate_backward(
-                gg[b], v["z"], v["y"], v["col"], v["et"], tag=str(b), load=Load(ua, gb) if b == 0 else None
+                gg[b], v["z"], v["y"], v["col"], v["et"], tag=str(b), load=Load(ua) if b == 0 else None
             )
         ends = lax.ppermute(jnp.stack([v["ds"] for v in saved]), "tp", [(1, 0)])[::-1]
-        sz = Scatter("z", matmul([[(normed_t, v["dz"])] for v in saved], bf16, 512, "z_grad", Load(ua)), n)
+        sz = Scatter("z", matmul([[(normed_t, v["dz"])] for v in saved], bf16, 512, "z_grad"), n)
 
         def back(b, load):
             v = saved[b]
@@ -1057,7 +1057,7 @@
             )[0]
 
         before_t = normed_before.T
-        back(1, Load(so, ub, sz))
+        back(1, Load(so, ub, sz, ua, gb))
         sx = LateScatter("x", n, x_gradient(1, Load(so)))
         (grad_z,) = matmul(
             [[(v["dz"], w) for v, w in zip(saved, Z.full)]], f32, 512, "z_back", Load(sx, ub), nt=True

time: 1240 us -> 1230 us (level)
  Pallas kernels: 1030 us -> 1010 us
    pallas_call x28 -> x27, Pallas kernels: 914 us -> 882 us  [run(): pl.pallas_call(kernel, name=name, grid=grid, in_specs=list(in_specs) + [h...]
    pallas_call x6 -> x7, Pallas kernels: 115 us -> 131 us  [run(): pl.pallas_call(body, name=name, grid=grid, in_specs=in_specs, out_specs=o...]
where the time goes in v5:
time: 1230 us; the launch traced here: 1220 us
  Pallas kernels  1010 us (82%)
  other arithmetic  145 us (12%)
  local copies, waits for them, and re-layouts  46.4 us (4%)
    pallas_call x27, Pallas kernels, run(): pl.pallas_call(kernel, name=name, grid=grid, in_specs=list(in_specs) + [h...  882 us
    pallas_call x7, Pallas kernels, run(): pl.pallas_call(body, name=name, grid=grid, in_specs=in_specs, out_specs=o...  131 us
    add x51, other arithmetic, low_sum(): return a + b  89.1 us
  transfers between devices with their start and end apart: 5, of which 0 were waited for; matrix products, arithmetic and copies ran while one was open for 3% of the time, Pallas kernels for 16%

profile of v5, /device:TPU:0, one launch (start us, length us, event | category | flops | bytes accessed | tf_op | source)
XLA Modules:
  0.0 1217.4 jit_solution(13416768938040576391)
XLA Ops:
  29.4 35.8 %turn_rows.1 = (f32[1024,1536]{1,0:T(8,128)}, bf16[2,16,48,1536]{3,2,1,0:T(8,128)(2,1)}, bf16[2,16,48,1536]{3,2,1,0:T(8,128)(2,1)}, bf16[2,16,48,128]{3,2,1,0:T(8,128)(2,1)}, bf16[2,16,48,128]{3,2,1,0:T(8,128)(2,1)}) custom-call(bf16[1024,1536]{1,0:T(8,128)(2,1)} %refs_0_.2, bf16[1536,1536]{1,0:T(8,128)(2,1)} %fusion.1.refs_1_.refs_3_, ...), custom_call_target="tpu_custom_call" | custom-call | flops 4831838208 | bytes 6291456 | tf_op jit(solution)/shard_map/turn_rows/pallas_call | solution.py:429
  65.3 26.9 %norm_one.1 = (f32[1024,1536]{1,0:T(8,128)}, bf16[1024,1536]{1,0:T(8,128)(2,1)}, bf16[1536,1024]{1,0:T(8,128)(2,1)}, bf16[2,16,48,1536]{3,2,1,0:T(8,128)(2,1)}, ...) custom-call(f32[1024,1536]{1,0:T(8,128)} %get-tuple-element.278.refs, ...), custom_call_target="tpu_custom_call", output_to_operand_aliasing={{3}: (3, {}), {4}: (4, {}), {5}: (5, {}), {6}: (6, {})} | custom-call | flops 31457280 | bytes 18874368 | tf_op jit(solution)/shard_map/norm_one/pallas_call | solution.py:429
  92.2 35.7 %turn_cotangent.1 = (bf16[1024,1536]{1,0:T(8,128)(2,1)}, bf16[1536,1024]{1,0:T(8,128)(2,1)}, bf16[2,16,48,1536]{3,2,1,0:T(8,128)(2,1)}, bf16[2,16,48,1536]{3,2,1...) custom-call(bf16[1024,1536]{1,0:T(8,128)(2,1)} %refs_0_.3, ...), custom_call_target="tpu_custom_call", output_to_operand_aliasing={{2}: (3, {}), {3}: (4, {}), {4}: (5, {}), {5}: (6, {})} | custom-call | flops 4831838208 | bytes 6291456 | tf_op jit(solution)/shard_map/turn_cotangent/pallas_call | solution.py:429
  132.0 15.5 %carry_one.1 = (bf16[2,16,48,1536]{3,2,1,0:T(8,128)(2,1)}, bf16[2,16,48,1536]{3,2,1,0:T(8,128)(2,1)}, bf16[2,16,48,128]{3,2,1,0:T(8,128)(2,1)}, bf16[2,16,48,128...) custom-call(bf16[2,16,48,1536]{3,2,1,0:T(8,128)(2,1)} %get-tuple-ele, ...), custom_call_target="tpu_custom_call", output_to_operand_aliasing={{0}: (0, {}), {1}: (1, {}), {2}: (2, {}), {3}: (3, {}), {4}... | custom-call | tf_op jit(solution)/shard_map/carry_one/pallas_call | solution.py:429
  151.1 48.6 %project_x.1 = (f32[1024,1536]{1,0:T(8,128)}, f32[1024,1536]{1,0:T(8,128)}, f32[16,1536]{1,0:T(8,128)}, f32[16,1536]{1,0:T(8,128)}, f32[1024,128]{1,0:T(8,128)},...) custom-call(bf16[1024,1536]{1,0:T(8,128)(2,1)} %get-tuple-element.28, ...), custom_call_target="tpu_custom_call", output_to_operand_aliasing={{6}: (8, {}), {7}: (9, {}), {8}: (10, {}), {9}: (11, {})} | custom-call | flops 9663676416 | bytes 12582912 | tf_op jit(solution)/shard_map/project_x/pallas_call | solution.py:429
  199.7 47.0 %conv_state0.1 = (f32[1024,1536]{1,0:T(8,128)}, f32[16,1536]{1,0:T(8,128)}, f32[1024,128]{1,0:T(8,128)}, f32[1024,128]{1,0:T(8,128)}, f32[1024,128]{1,0:T(8,128)...) custom-call(f32[1024,1536]{1,0:T(8,128)} %get-tuple-element.303.refs, ...), custom_call_target="tpu_custom_call", output_to_operand_aliasing={{5}: (8, {}), {6}: (9, {}), {7}: (10, {}), {8}: (11, {}), {... | custom-call | flops 7864320000 | bytes 6291456 | tf_op jit(solution)/shard_map/conv_state0/pallas_call | solution.py:429
  246.7 40.1 %conv_state1.1 = (f32[1024,1536]{1,0:T(8,128)}, f32[16,1536]{1,0:T(8,128)}, f32[1024,128]{1,0:T(8,128)}, f32[1024,128]{1,0:T(8,128)}, f32[1024,128]{1,0:T(8,128)...) custom-call(f32[1024,1536]{1,0:T(8,128)} %get-tuple-element.315.refs, ...), custom_call_target="tpu_custom_call", output_to_operand_aliasing={{5}: (8, {}), {6}: (9, {}), {7}: (10, {}), {8}: (11, {})} | custom-call | flops 7864320000 | bytes 6291456 | tf_op jit(solution)/shard_map/conv_state1/pallas_call | solution.py:429
  289.7 43.9 %project_z.1 = (f32[1024,1536]{1,0:T(8,128)}, f32[1024,1536]{1,0:T(8,128)}, bf16[2,16,48,2048]{3,2,1,0:T(8,128)(2,1)}, bf16[2,16,48,2048]{3,2,1,0:T(8,128)(2,1)}...) custom-call(bf16[1024,1536]{1,0:T(8,128)(2,1)} %get-tuple-element.28, ...), custom_call_target="tpu_custom_call", output_to_operand_aliasing={{2}: (4, {}), {3}: (5, {}), {4}: (6, {}), {5}: (7, {}), {6}... | custom-call | flops 9663676416 | bytes 12582912 | tf_op jit(solution)/shard_map/project_z/pallas_call | solution.py:429
  335.3 39.6 %scan_forward0.1 = (bf16[1024,1536]{1,0:T(8,128)(2,1)}, f32[1024,1536]{1,0:T(8,128)}, f32[128,1536]{1,0:T(8,128)}, bf16[2,16,48,2048]{3,2,1,0:T(8,128)(2,1)}, bf16[2,16,48,2048]{3,2,1,0:T(8,128)(2,1)}) custom-call(f32[1024,1536]{1,0:T(8,128)} %get-tuple-element.312.refs_0_, ...), custom_call_target="tpu_custom_call", output_to_operand_aliasing={{3}: (8, {}), {4}: (9, {})} | custom-call | flops 15728640000 | bytes 12582912 | tf_op jit(solution)/shard_map/scan_forward0/pallas_call | solution.py:429
  374.9 38.8 %scan_forward1.1 = (bf16[1024,1536]{1,0:T(8,128)(2,1)}, f32[1024,1536]{1,0:T(8,128)}, f32[128,1536]{1,0:T(8,128)}, bf16[2,16,48,2048]{3,2,1,0:T(8,128)(2,1)}, bf...) custom-call(f32[1024,1536]{1,0:T(8,128)} %get-tuple-element.338.refs, ...), custom_call_target="tpu_custom_call", output_to_operand_aliasing={{3}: (8, {}), {4}: (9, {}), {5}: (10, {}), {6}: (11, {})} | custom-call | flops 15728640000 | bytes 12582912 | tf_op jit(solution)/shard_map/scan_forward1/pallas_call | solution.py:429
  413.8 15.8 %project_out.1 = (f32[1024,1536]{1,0:T(8,128)}, bf16[2,16,48,2048]{3,2,1,0:T(8,128)(2,1)}, bf16[2,16,48,2048]{3,2,1,0:T(8,128)(2,1)}) custom-call(bf16[1024,1536]{1,0:T(8,128)(2,1)} %get-tuple-element.336.refs_0_.refs_1_, bf16[1536,1536]{1,0:T(8,128)(2,1)} %bitcast.346, ...), custom_call_target="tpu_custom_call", output_to_operand_aliasing={{1}: (4, {}), {2}: (5, {})} | custom-call | flops 9663676416 | bytes 6291456 | tf_op jit(solution)/shard_map/project_out/pallas_call | solution.py:429
  429.5 11.5 norm_two.1
  441.0 52.8 %feed_forward.1 = (bf16[1024,2048]{1,0:T(8,128)(2,1)}, bf16[1024,2048]{1,0:T(8,128)(2,1)}, bf16[1024,2048]{1,0:T(8,128)(2,1)}, bf16[1024,2048]{1,0:T(8,128)(2,1)...) custom-call(bf16[1024,1536]{1,0:T(8,128)(2,1)} %get-tuple-element.353.n_ref, ...), custom_call_target="tpu_custom_call" | custom-call | flops 38654705664 | bytes 25165824 | tf_op jit(solution)/shard_map/feed_forward/pallas_call | solution.py:371
  493.8 20.4 %down_grad.1 = (bf16[1536,2048]{1,0:T(8,128)(2,1)}, bf16[1536,2048]{1,0:T(8,128)(2,1)}) custom-call(bf16[1536,1024]{1,0:T(8,128)(2,1)} %get-tuple-element.363.refs_0_.refs_2_, bf16[1024,2048]{1,0:T(8,128)(2,1)} %get-tuple-element.361.refs_1_.refs_0_, bf16[1536,1024]{1,0:T(8,128)(2,1)} %get-tuple-element.363.refs_0_.refs_2_, ...), custom_call_target="tpu_custom_call" | custom-call | flops 12884901888 | bytes 25165824 | tf_op jit(solution)/shard_map/down_grad/pallas_call | solution.py:371
  514.2 21.4 %gate_grad.1 = (bf16[1536,2048]{1,0:T(8,128)(2,1)}, bf16[1536,2048]{1,0:T(8,128)(2,1)}, bf16[2,8,48,1024]{3,2,1,0:T(8,128)(2,1)}, bf16[2,8,48,1024]{3,2,1,0:T(8,...) custom-call(bf16[1536,1024]{1,0:T(8,128)(2,1)} %get-tuple-element.365.refs_0_.refs_2_, ...), custom_call_target="tpu_custom_call" | custom-call | flops 12884901888 | bytes 25165824 | tf_op jit(solution)/shard_map/gate_grad/pallas_call | solution.py:429
  543.4 26.1 %up_grad.1 = (bf16[1536,2048]{1,0:T(8,128)(2,1)}, bf16[1536,2048]{1,0:T(8,128)(2,1)}, bf16[4,48,1024]{2,1,0:T(8,128)(2,1)}, bf16[4,48,1024]{2,1,0:T(8,128)(2,1)}...) custom-call(bf16[1536,1024]{1,0:T(8,128)(2,1)} %get-tuple-element.36, ...), custom_call_target="tpu_custom_call" | custom-call | flops 12884901888 | bytes 25165824 | tf_op jit(solution)/shard_map/up_grad/pallas_call | solution.py:429
  573.6 34.7 %project_down.1 = (f32[1024,1536]{1,0:T(8,128)}, bf16[4,48,1024]{2,1,0:T(8,128)(2,1)}, bf16[4,48,1024]{2,1,0:T(8,128)(2,1)}, bf16[8,48,1024]{2,1,0:T(8,128)(2,1)...) custom-call(bf16[1024,2048]{1,0:T(8,128)(2,1)} %get-tuple-element.36, ...), custom_call_target="tpu_custom_call" | custom-call | flops 12884901888 | bytes 6291456 | tf_op jit(solution)/shard_map/project_down/pallas_call | solution.py:429
  622.6 53.7 %two_back.1 = (f32[1024,1536]{1,0:T(8,128)}, bf16[4,48,1024]{2,1,0:T(8,128)(2,1)}, bf16[4,48,1024]{2,1,0:T(8,128)(2,1)}, bf16[8,48,1024]{2,1,0:T(8,128)(2,1)}, b...) custom-call(bf16[1024,2048]{1,0:T(8,128)(2,1)} %get-tuple-element.36, ...), custom_call_target="tpu_custom_call" | custom-call | flops 25769803776 | bytes 6291456 | tf_op jit(solution)/shard_map/two_back/pallas_call | solution.py:429
  688.8 20.0 %norm_two_back.1 = (bf16[1024,1536]{1,0:T(8,128)(2,1)}, bf16[1024,1536]{1,0:T(8,128)(2,1)}, f32[8,1536]{1,0:T(8,128)}, bf16[1536,1024]{1,0:T(8,128)(2,1)}, bf16[...) custom-call(f32[1024,1536]{1,0:T(8,128)} %get-tuple-element.352.refs, ...), custom_call_target="tpu_custom_call" | custom-call | flops 31457280 | bytes 25165824 | tf_op jit(solution)/shard_map/norm_two_back/pallas_call | solution.py:429
  725.1 25.6 %out_grad.1 = (bf16[1536,1536]{1,0:T(8,128)(2,1)}, bf16[1536,1536]{1,0:T(8,128)(2,1)}, bf16[4,48,1024]{2,1,0:T(8,128)(2,1)}, bf16[4,48,1024]{2,1,0:T(8,128)(2,1)...) custom-call(bf16[1536,1024]{1,0:T(8,128)(2,1)} %get-tuple-element.40, ...), custom_call_target="tpu_custom_call" | custom-call | flops 9663676416 | bytes 18874368 | tf_op jit(solution)/shard_map/out_grad/pallas_call | solution.py:429
  754.7 18.3 %gated_back.1 = (f32[1024,1536]{1,0:T(8,128)}, f32[1024,1536]{1,0:T(8,128)}, bf16[4,48,1024]{2,1,0:T(8,128)(2,1)}, bf16[4,48,1024]{2,1,0:T(8,128)(2,1)}, bf16[2,...) custom-call(bf16[1024,1536]{1,0:T(8,128)(2,1)} %get-tuple-element.398.refs_0_.refs_2_.refs_4_, ...), custom_call_target="tpu_custom_call" | custom-call | flops 9663676416 | bytes 12582912 | tf_op jit(solution)/shard_map/gated_back/pallas_call | solution.py:429
  781.5 15.8 %gate_backward0.1 = (f32[1024,1536]{1,0:T(8,128)}, bf16[1024,1536]{1,0:T(8,128)(2,1)}, f32[16,1536]{1,0:T(8,128)}, bf16[4,48,1024]{2,1,0:T(8,128)(2,1)}, bf16[4,48,1024]{2,1,0:T(8,128)(2,1)}) custom-call(f32[1024,1536]{1,0:T(8,128)} %get-tuple-element.409.refs_0_, f32[1024,1536]{1,0:T(8,128)} %get-tuple-element.328.refs_1_, ...), custom_call_target="tpu_custom_call" | custom-call | flops 7864320000 | bytes 15728640 | tf_op jit(solution)/shard_map/gate_backward0/pallas_call | solution.py:429
  799.9 13.2 %gate_backward1.1 = (f32[1024,1536]{1,0:T(8,128)}, bf16[1024,1536]{1,0:T(8,128)(2,1)}, f32[16,1536]{1,0:T(8,128)}) custom-call(f32[1024,1536]{1,0:T(8,128)} %get-tuple-element.416.gg_ref, f32[1024,1536]{1,0:T(8,128)} %get-tuple-element.339.refs_1_.z_ref, f32[1024,1536]{1,0:T(8,128)} %get-tuple-element.417.y_ref, ...), custom_call_target="tpu_custom_call" | custom-call | flops 7864320000 | bytes 15728640 | tf_op jit(solution)/shard_map/gate_backward1/pallas_call | solution.py:371
  815.4 16.6 %z_grad.1 = (bf16[1536,1536]{1,0:T(8,128)(2,1)}, bf16[1536,1536]{1,0:T(8,128)(2,1)}) custom-call(bf16[1536,1024]{1,0:T(8,128)(2,1)} %get-tuple-element.382.refs_0_.refs_2_, bf16[1024,1536]{1,0:T(8,128)(2,1)} %get-tuple-element.419.refs_1_.refs_0_, bf16[1536,1024]{1,0:T(8,128)(2,1)} %get-tuple-element.382.refs_0_.refs_2_, ...), custom_call_target="tpu_custom_call" | custom-call | flops 9663676416 | bytes 18874368 | tf_op jit(solution)/shard_map/z_grad/pallas_call | solution.py:371
  835.0 54.9 %scan_backward1.1 = (bf16[1024,1536]{1,0:T(8,128)(2,1)}, f32[1024,128]{1,0:T(8,128)}, f32[8,1536]{1,0:T(8,128)}, f32[24,1536]{1,0:T(8,128)}, f32[8,128]{1,0:T(8,...) custom-call(f32[1024,1536]{1,0:T(8,128)} %get-tuple-element.338.refs, ...), custom_call_target="tpu_custom_call" | custom-call | flops 39321600000 | bytes 18874368 | tf_op jit(solution)/shard_map/scan_backward1/pallas_call | solution.py:429
  904.6 18.6 %x_grad1.1 = (bf16[1536,1536]{1,0:T(8,128)(2,1)}, bf16[4,48,1536]{2,1,0:T(8,128)(2,1)}, bf16[4,48,1536]{2,1,0:T(8,128)(2,1)}) custom-call(bf16[1536,1024]{1,0:T(8,128)(2,1)} %get-tuple-element.382.refs_0_.refs_2_, bf16[1024,1536]{1,0:T(8,128)(2,1)} %get-tuple-element.437.refs_1_, bf16[1536,16]{1,0:T(8,128)(2,1)} %multiply_convert_fusion.refs_2_, ...), custom_call_target="tpu_custom_call" | custom-call | flops 4907335680 | bytes 9437184 | tf_op jit(solution)/shard_map/x_grad1/pallas_call | solution.py:429
  924.3 17.2 %z_back.1 = (f32[1024,1536]{1,0:T(8,128)}, bf16[2,8,48,1536]{3,2,1,0:T(8,128)(2,1)}, bf16[4,48,1024]{2,1,0:T(8,128)(2,1)}, bf16[4,48,1024]{2,1,0:T(8,128)(2,1)}) custom-call(bf16[1024,1536]{1,0:T(8,128)(2,1)} %get-tuple-element.419.refs_1_.refs_0_, bf16[1536,1536]{1,0:T(8,128)(2,1)} %bitcast.335, bf16[1024,1536]{1,0:T(8,128)(2,1)} %get-tuple-element.420.refs_3_.refs_2_, ...), custom_call_target="tpu_custom_call" | custom-call | flops 9663676416 | bytes 6291456 | tf_op jit(solution)/shard_map/z_back/pallas_call | solution.py:429
  949.0 57.5 %scan_backward0.1 = (bf16[1024,1536]{1,0:T(8,128)(2,1)}, f32[1024,128]{1,0:T(8,128)}, f32[8,1536]{1,0:T(8,128)}, f32[24,1536]{1,0:T(8,128)}, f32[8,128]{1,0:T(8,...) custom-call(f32[1024,1536]{1,0:T(8,128)} %get-tuple-element.312.refs, ...), custom_call_target="tpu_custom_call" | custom-call | flops 39321600000 | bytes 18874368 | tf_op jit(solution)/shard_map/scan_backward0/pallas_call | solution.py:429
  1046.1 40.1 %x_back.1 = (f32[1024,1536]{1,0:T(8,128)}, bf16[2,8,48,1536]{3,2,1,0:T(8,128)(2,1)}, bf16[4,48,1536]{2,1,0:T(8,128)(2,1)}, bf16[2,8,48,128]{3,2,1,0:T(8,128)(2,1...) custom-call(bf16[1024,1536]{1,0:T(8,128)(2,1)} %get-tuple-element.55, ...), custom_call_target="tpu_custom_call" | custom-call | flops 10468982784 | bytes 6291456 | tf_op jit(solution)/shard_map/x_back/pallas_call | solution.py:429
  1091.0 16.9 %norm_one_back.1 = (bf16[1024,1536]{1,0:T(8,128)(2,1)}, bf16[1024,1536]{1,0:T(8,128)(2,1)}, f32[8,1536]{1,0:T(8,128)}, bf16[4,48,128]{2,1,0:T(8,128)(2,1)}, bf16...) custom-call(f32[1024,1536]{1,0:T(8,128)} %get-tuple-element.283.refs, ...), custom_call_target="tpu_custom_call" | custom-call | flops 31457280 | bytes 25165824 | tf_op jit(solution)/shard_map/norm_one_back/pallas_call | solution.py:429
  1123.7 35.4 %turn_out.1 = (bf16[1024,1536]{1,0:T(8,128)(2,1)}, bf16[4,48,1536]{2,1,0:T(8,128)(2,1)}, bf16[4,48,1536]{2,1,0:T(8,128)(2,1)}, bf16[4,48,128]{2,1,0:T(8,128)(2,1...) custom-call(bf16[1024,1536]{1,0:T(8,128)(2,1)} %add_convert_fusion.r, ...), custom_call_target="tpu_custom_call" | custom-call | flops 4831838208 | bytes 6291456 | tf_op jit(solution)/shard_map/turn_out/pallas_call | solution.py:429
  1164.8 37.7 %turn_back.1 = (f32[1024,1536]{1,0:T(8,128)}, bf16[2,48,1536]{2,1,0:T(8,128)(2,1)}, bf16[2,48,1536]{2,1,0:T(8,128)(2,1)}, bf16[2,48,1536]{2,1,0:T(8,128)(2,1)}, ...) custom-call(bf16[1024,1536]{1,0:T(8,128)(2,1)} %get-tuple-element.48, ...), custom_call_target="tpu_custom_call" | custom-call | flops 9663676416 | bytes 6291456 | tf_op jit(solution)/shard_map/turn_back/pallas_call | solution.py:429
  (490 shorter events, 218.5 us)
Async XLA Ops:
  1.5 146.1 %collective-permute-start = (bf16[16,1536]{1,0:T(8,128)(2,1)S(1)}, bf16[16,1536]{1,0:T(8,128)(2,1)S(1)}, u32[]{:S(2)}, u32[]{:S(2)}) collective-permute-start(bf16[16,1536]{1,0:T(8,128)(2,1)S(1)} %slice.435), channel_id=1, source_target_pairs={{0,1},{2,3},{4,5},{6,7},{8,9},{10,11},{12,13},{14,15},{16,17},{18,... | collective-permute-start | bytes 147464 | tf_op jit(solution)/shard_map/ppermute | solution.py:957
  10.0 139.2 %collective-permute-start.1 = (f32[8,1536]{1,0:T(8,128)S(1)}, f32[8,1536]{1,0:T(8,128)S(1)}, u32[]{:S(2)}, u32[]{:S(2)}) collective-permute-start(f32[8,1536]{1,0:T(8,128)S(1)} %select_maximum_fusion.refs_3_.refs_7_.refs_5_), channel_id=1, source_target_pairs={{0,1},{1,0},{2,3},{3,2},{4,5},{5,4},{6,7},{7,6},{8,9},{9,8},{10,11... | collective-permute-start | bytes 147464 | tf_op jit(solution)/shard_map/ppermute | solution.py:920
  149.2 50.5 %copy-start.104 = (f32[8,1536]{1,0:T(8,128)}, f32[8,1536]{1,0:T(8,128)S(1)}, u32[]{:S(2)}) copy-start(f32[8,1536]{1,0:T(8,128)S(1)} %collective-permute-done.1.refs_3_.refs_7_.refs_5_) | copy-start | bytes 147460
  246.7 40.1 %copy-start.102 = (f32[16,1536]{1,0:T(8,128)S(1)}, f32[16,1536]{1,0:T(8,128)}, u32[]{:S(2)}) copy-start(f32[16,1536]{1,0:T(8,128)} %get-tuple-element.332) | copy-start | bytes 294916
  287.7 46.9 %collective-permute-start.2 = (f32[2,16,1536]{2,1,0:T(8,128)S(1)}, f32[2,16,1536]{2,1,0:T(8,128)S(1)}, u32[]{:S(2)}, u32[]{:S(2)}) collective-permute-start(f32[2,16,1536]{2,1,0:T(8,128)S(1)} %pad_maximum_fusion.3), channel_id=1, source_target_pairs={{0,1},{2,3},{4,5},{6,7},{8,9},{10,11},{12,13},{14,15},{16,17},{18,... | collective-permute-start | bytes 589832 | tf_op jit(solution)/shard_map/ppermute | solution.py:1000
  514.2 21.4 %copy-start.36 = (bf16[1536,2048]{1,0:T(8,128)(2,1)S(1)}, bf16[1536,2048]{1,0:T(8,128)(2,1)}, u32[]{:S(2)}) copy-start(bf16[1536,2048]{1,0:T(8,128)(2,1)} %get-tuple-element.368) | copy-start | bytes 18874372
  543.4 28.0 %copy-start.10 = (bf16[2,8,48,1024]{3,2,1,0:T(8,128)(2,1)S(1)}, bf16[2,8,48,1024]{3,2,1,0:T(8,128)(2,1)}, u32[]{:S(2)}) copy-start(bf16[2,8,48,1024]{3,2,1,0:T(8,128)(2,1)} %get-tuple-element.550.refs_4_) | copy-start | bytes 4718596
  573.6 34.7 %copy-start.5 = (bf16[8,48,1024]{2,1,0:T(8,128)(2,1)S(1)}, bf16[8,48,1024]{2,1,0:T(8,128)(2,1)}, u32[]{:S(2)}) copy-start(bf16[8,48,1024]{2,1,0:T(8,128)(2,1)} %fusion.14.refs_7_) | copy-start | bytes 2359300
  573.6 38.0 %copy-start.71 = (bf16[4,48,1024]{2,1,0:T(8,128)(2,1)S(1)}, bf16[4,48,1024]{2,1,0:T(8,128)(2,1)}, u32[]{:S(2)}) copy-start(bf16[4,48,1024]{2,1,0:T(8,128)(2,1)} %get-tuple-element.389) | copy-start | bytes 1179652
  622.6 60.8 %slice-start.2 = ((s8[6291456]{0:T(1024)(128)(4,1)}), s8[4194304]{0:T(1024)(128)(4,1)S(1)}, s32[]{:S(2)}) async-start(s8[6291456]{0:T(1024)(128)(4,1)} %bitcast.362), calls=%async_computation.2 | async-start | bytes 8388608
  622.6 60.8 %slice-start.3 = ((s8[6291456]{0:T(1024)(128)(4,1)}), s8[2097152]{0:T(1024)(128)(4,1)S(1)}, s32[]{:S(2)}) async-start(s8[6291456]{0:T(1024)(128)(4,1)} %bitcast.362), calls=%async_computation.3 | async-start | bytes 4194304
  688.8 20.1 %copy-start.4 = (bf16[8,48,1024]{2,1,0:T(8,128)(2,1)S(1)}, bf16[8,48,1024]{2,1,0:T(8,128)(2,1)}, u32[]{:S(2)}) copy-start(bf16[8,48,1024]{2,1,0:T(8,128)(2,1)} %fusion.12.refs_5_) | copy-start | bytes 2359300
  725.1 27.5 %copy-start.9 = (bf16[2,8,48,1024]{3,2,1,0:T(8,128)(2,1)S(1)}, bf16[2,8,48,1024]{3,2,1,0:T(8,128)(2,1)}, u32[]{:S(2)}) copy-start(bf16[2,8,48,1024]{3,2,1,0:T(8,128)(2,1)} %get-tuple-element.543.refs_4_) | copy-start | bytes 4718596
  774.0 25.8 %copy-start.49 = (bf16[4,48,1024]{2,1,0:T(8,128)(2,1)}, bf16[4,48,1024]{2,1,0:T(8,128)(2,1)S(1)}, u32[]{:S(2)}) copy-start(bf16[4,48,1024]{2,1,0:T(8,128)(2,1)S(1)} %slice_add_fusion.21.refs_26_) | copy-start | bytes 1179652
  814.0 20.3 %collective-permute-start.3 = (f32[2,16,1536]{2,1,0:T(8,128)S(1)}, f32[2,16,1536]{2,1,0:T(8,128)S(1)}, u32[]{:S(2)}, u32[]{:S(2)}) collective-permute-start(f32[2,16,1536]{2,1,0:T(8,128)S(1)} %pad_maximum_fusion.4), channel_id=1, source_target_pairs={{1,0},{3,2},{5,4},{7,6},{9,8},{11,10},{13,12},{15,14},{17,16},{19,... | collective-permute-start | bytes 589832 | tf_op jit(solution)/shard_map/ppermute | solution.py:1038
  833.3 64.3 %slice-start.6 = ((s8[4718592]{0:T(1024)(128)(4,1)}), s8[4194304]{0:T(1024)(128)(4,1)S(1)}, s32[]{:S(2)}) async-start(s8[4718592]{0:T(1024)(128)(4,1)} %bitcast.392), calls=%async_computation.6 | async-start | bytes 8388608
  835.0 62.6 %slice-start.7 = ((s8[4718592]{0:T(1024)(128)(4,1)}), s8[524288]{0:T(1024)(128)(4,1)S(1)}, s32[]{:S(2)}) async-start(s8[4718592]{0:T(1024)(128)(4,1)} %bitcast.392), calls=%async_computation.7 | async-start | bytes 1048576
  903.8 19.3 %copy-start.108 = (f32[1,1536]{1,0:T(1,128)}, f32[1,1536]{1,0:T(1,128)S(1)}, u32[]{:S(2)}) copy-start(f32[1,1536]{1,0:T(1,128)S(1)} %get-tuple-element.558) | copy-start | bytes 18436
  924.3 22.5 %copy-start.40 = (bf16[4,48,1536]{2,1,0:T(8,128)(2,1)}, bf16[4,48,1536]{2,1,0:T(8,128)(2,1)S(1)}, u32[]{:S(2)}) copy-start(bf16[4,48,1536]{2,1,0:T(8,128)(2,1)S(1)} %slice_add_fusion.19.refs_21_) | copy-start | bytes 1769476
  949.0 57.6 %copy-start.107 = (f32[4,1536]{1,0:T(4,128)S(1)}, f32[4,1536]{1,0:T(4,128)}, u32[]{:S(2)}) copy-start(f32[4,1536]{1,0:T(4,128)} %param.27) | copy-start | bytes 73732
  949.0 59.3 %copy-start.109 = (f32[1,1536]{1,0:T(1,128)S(1)}, f32[1,1536]{1,0:T(1,128)}, u32[]{:S(2)}) copy-start(f32[1,1536]{1,0:T(1,128)} %copy-done.108) | copy-start | bytes 18436
  949.0 59.3 %copy-start.122 = (f32[16]{0:T(128)S(1)}, f32[16]{0:T(128)}, u32[]{:S(2)}) copy-start(f32[16]{0:T(128)} %pad.69.clone) | copy-start | bytes 196
  1019.0 25.6 %collective-permute-start.4 = (f32[2,16,1536]{2,1,0:T(8,128)S(1)}, f32[2,16,1536]{2,1,0:T(8,128)S(1)}, u32[]{:S(2)}, u32[]{:S(2)}) collective-permute-start(f32[2,16,1536]{2,1,0:T(8,128)S(1)} %pad_maximum_fusion.5), channel_id=1, source_target_pairs={{1,0},{3,2},{5,4},{7,6},{9,8},{11,10},{13,12},{15,14},{17,16},{19,... | collective-permute-start | bytes 589832 | tf_op jit(solution)/shard_map/ppermute | solution.py:1067
  1046.1 40.1 %copy-start.100 = (bf16[1536,128]{1,0:T(8,128)(2,1)S(1)}, bf16[1536,128]{1,0:T(8,128)(2,1)}, u32[]{:S(2)}) copy-start(bf16[1536,128]{1,0:T(8,128)(2,1)} %get-tuple-element.456) | copy-start | bytes 1179652
  1046.1 41.7 %copy-start.99 = (bf16[1536,128]{1,0:T(8,128)(2,1)S(1)}, bf16[1536,128]{1,0:T(8,128)(2,1)}, u32[]{:S(2)}) copy-start(bf16[1536,128]{1,0:T(8,128)(2,1)} %get-tuple-element.457) | copy-start | bytes 1179652
  1091.0 19.0 %copy-start.19 = (bf16[2,8,48,1536]{3,2,1,0:T(8,128)(2,1)S(1)}, bf16[2,8,48,1536]{3,2,1,0:T(8,128)(2,1)}, u32[]{:S(2)}) copy-start(bf16[2,8,48,1536]{3,2,1,0:T(8,128)(2,1)} %get-tuple-element.465) | copy-start | bytes 7077892
  1123.7 35.4 %copy-start.79 = (bf16[8,48,128]{2,1,0:T(8,128)(2,1)S(1)}, bf16[8,48,128]{2,1,0:T(8,128)(2,1)}, u32[]{:S(2)}) copy-start(bf16[8,48,128]{2,1,0:T(8,128)(2,1)} %fusion.44.refs_5_) | copy-start | bytes 294916
  1123.7 36.3 %copy-start.15 = (bf16[8,48,1536]{2,1,0:T(8,128)(2,1)S(1)}, bf16[8,48,1536]{2,1,0:T(8,128)(2,1)}, u32[]{:S(2)}) copy-start(bf16[8,48,1536]{2,1,0:T(8,128)(2,1)} %fusion.3.refs_3_) | copy-start | bytes 3538948
  1164.8 37.8 %slice-start.22 = ((bf16[4,48,128]{2,1,0:T(8,128)(2,1)}), bf16[1,48,128]{2,1,0:T(8,128)(2,1)S(1)}, s32[]{:S(2)}) async-start(bf16[4,48,128]{2,1,0:T(8,128)(2,1)} %copy-done.105), calls=%async_computation.22 | async-start | bytes 24576 | tf_op jit(solution)/shard_map/slice | solution.py:744
  1164.8 40.2 %copy-start.113 = (f32[16,128]{1,0:T(8,128)S(1)}, f32[16,128]{1,0:T(8,128)}, u32[]{:S(2)}) copy-start(f32[16,128]{1,0:T(8,128)} %add_add_fusion.3.refs_8_) | copy-start | bytes 24580
  1164.8 43.7 %slice-start.9 = ((bf16[4,48,1536]{2,1,0:T(8,128)(2,1)}), bf16[1,48,1536]{2,1,0:T(8,128)(2,1)S(1)}, s32[]{:S(2)}) async-start(bf16[4,48,1536]{2,1,0:T(8,128)(2,1)} %copy-done.41), calls=%async_computation.9 | async-start | bytes 294912 | tf_op jit(solution)/shard_map/slice | solution.py:744
  1164.8 43.7 %slice-start.11 = ((bf16[4,48,1536]{2,1,0:T(8,128)(2,1)}), bf16[1,48,1536]{2,1,0:T(8,128)(2,1)S(1)}, s32[]{:S(2)}) async-start(bf16[4,48,1536]{2,1,0:T(8,128)(2,1)} %copy-done.45), calls=%async_computation.11 | async-start | bytes 294912 | tf_op jit(solution)/shard_map/slice | solution.py:744
  (121 other events, 810.4 us)
